TPU v7x, 32 devices: a whole 2x2x4 slice. The times are simulated.
32 devices in a mesh: scen: 8 (over y, x, core), col: 4 (over z).
Axes of the slice: x: 2, y: 2, z: 4, core: 2. Of those that a mesh axis runs over, the one named last changes fastest.
Arguments:
- inverses: float32 [8, 1024, 1024], P('scen'), as said below
- coupling: float32 [8, 1024, 4096], P('scen', None, 'col'), may hold values from -0.1875 to 0.1875
- tile_mask: int32 [8, 8], P('scen'), may hold values 0 or 1
- hess_diag: float32 [512], replicated, may hold values from 1 to 16
Outputs:
- factor: float32 [4096, 512], P(('col', 'scen'))
Inputs may be any that keep to these rules, and one draw needn't show every extreme that they name: `inverses`: each scenario's matrix is symmetric and positive definite.
All inputs are finite; a program needn't handle non-finite values. No bound on the sum of `tile_mask` on one device may be relied on, other than what follows from the above.
Results may differ from a plain program's by a relative error of at most 0.0001.
Values sent between devices are 32-bit elements; how exact they have to be, the bound alone decides.
No kernel may reach another device: no remote copies, remote signals or barrier semaphores. Data moves between devices by JAX's collectives and lax.ppermute only.
A program may use at most 64 MiB of HBM per device.

v0:
```python
import jax
import jax.numpy as jnp
from jax import lax
from jax.sharding import PartitionSpec as P


def broadcast(value, axis, source):
    kept = jnp.where(lax.axis_index(axis) == source, value, 0).astype(value.dtype)
    return lax.psum(kept, axis)


def outer_rows(left, piece):
    return lax.dot_general(
        left,
        piece,
        (((0,), (0,)), ((), ())),
        precision=lax.Precision.HIGHEST,
        preferred_element_type=jnp.float32,
    )


def matmul(left, right):
    return jnp.dot(left, right, precision=lax.Precision.HIGHEST, preferred_element_type=jnp.float32)


def body(inverses, coupling, tile_mask, hess_diag):
    inverse = inverses[0]
    local = coupling[0]
    width = hess_diag.shape[0]
    half = width // 2
    scen_size = lax.axis_size("scen")
    rows = local.shape[1] // scen_size
    row_keep = jnp.repeat(tile_mask[0].astype(jnp.float32), local.shape[0] // tile_mask.shape[1])
    panel = broadcast(local[:, :width], "col", 0)
    panel = panel * row_keep[:, None]
    product = matmul(inverse, panel) * row_keep[:, None]
    block = local
    summed = lax.psum_scatter(outer_rows(block, product), "scen", scatter_dimension=0, tiled=True)
    first = lax.axis_index("col") * local.shape[1] + lax.axis_index("scen") * rows
    global_rows = first + jnp.arange(rows, dtype=jnp.int32)
    columns = jnp.arange(width, dtype=jnp.int32)
    schur = summed + jnp.where(columns[None, :] == global_rows[:, None], hess_diag[None, :], 0.0)

    def fetch(stacked, low):
        whole = lax.all_gather(stacked, "scen", axis=1, tiled=True)
        block = whole[:, low : low + half]
        return broadcast(block, "col", 0)

    identity = jnp.eye(half, dtype=jnp.float32)
    block_one = fetch(schur[None, :, :half], 0)[0]
    chol1 = jnp.linalg.cholesky(block_one)
    inv1 = jax.scipy.linalg.solve_triangular(chol1, identity, lower=True)
    lcol1 = matmul(schur[:, :half], inv1.T)
    own_one = lax.dynamic_slice_in_dim(chol1, jnp.clip(first, 0, half - rows), rows, 0)
    lcol1 = jnp.where(first < half, own_one, lcol1)
    paired = fetch(jnp.stack([schur[:, half:], lcol1]), half)
    lower_b = paired[1]
    update = paired[0] - matmul(lower_b, lower_b.T)
    chol2 = jnp.linalg.cholesky(update)
    inv2 = jax.scipy.linalg.solve_triangular(chol2, identity, lower=True)
    remain = schur[:, half:] - matmul(lcol1, lower_b.T)
    lcol2 = matmul(remain, inv2.T)
    own_two = lax.dynamic_slice_in_dim(chol2, jnp.clip(first - half, 0, half - rows), rows, 0)
    lcol2 = jnp.where(first < width, own_two, lcol2)
    lcol2 = jnp.where(first < half, jnp.zeros_like(lcol2), lcol2)
    return jnp.concatenate([lcol1, lcol2], axis=1)


def solution(mesh):
    in_specs = (P("scen", None, None), P("scen", None, "col"), P("scen", None), P())
    out_specs = P(("col", "scen"), None)
    return jax.shard_map(body, mesh=mesh, in_specs=in_specs, out_specs=out_specs, check_vma=False)
```

profile of v0, /device:TPU:0, one launch (start us, length us, event | category | flops | bytes accessed | tf_op | source)
XLA Modules:
  0.0 433.5 jit_solution(17175849450630514920)
XLA Ops:
  6.5 3.1 slice_select_fusion
  10.4 88.3 %all-reduce.5.cloned.1.call-done = f32[1024,512]{1,0:T(8,128)} async-done(((f32[1024,512]{1,0:T(8,128)}), f32[1024,512]{1,0:T(8,128)}) %all-reduce.5.cloned.1.call-update) | async-done | bytes 2097168 | tf_op jit(solution)/shard_map/psum | solution.py:9
  98.7 16.6 %fusion = f32[512,1024]{1,0:T(8,128)S(1)} fusion(f32[1,1024,1024]{2,1,0:T(8,128)} %param.7, f32[1024,512]{1,0:T(8,128)} %all-reduce.5.cloned.1.call-done, f32[1024]{0:T(1024)S(1)} %broadcast_bitcast_fusion), kind=kOutput, calls=%fused_computation.4 | convolution fusion | flops 6442975232 | bytes 8392704 | tf_op jit(solution)/shard_map/dot_general | solution.py:23
  115.2 8.2 %fusion.5 = f32[1024,512]{0,1:T(8,128)} fusion(f32[512,1024]{1,0:T(8,128)S(1)} %fusion, f32[1024]{0:T(1024)S(1)} %broadcast_bitcast_fusion, f32[1,1024,1024]{2,1,0:T(8,128)S(1)} %copy-done), kind=kOutput, calls=%fused_computation.10 | convolution fusion | flops 6442975232 | bytes 8392704 | tf_op jit(solution)/shard_map/dot_general | solution.py:13
  123.6 40.2 %reduce-scatter.2.cloned.1.call-done = f32[128,512]{0,1:T(8,128)} async-done(((f32[1024,512]{0,1:T(8,128)}), f32[128,512]{0,1:T(8,128)}) %reduce-scatter.2.cloned.1.call-update) | async-done | bytes 262160 | tf_op jit(solution)/shard_map/reduce_scatter | solution.py:38
  163.8 1.1 select_add_fusion
  165.7 23.6 %all-gather.6.cloned.1.call-done = f32[1024,256]{0,1:T(8,128)} async-done(((f32[128,256]{0,1:T(8,128)}), f32[1024,256]{0,1:T(8,128)}) %all-gather.6.cloned.1.call-update) | async-done | bytes 1048592 | tf_op jit(solution)/shard_map/all_gather | solution.py:45
  189.3 1.7 fusion.11
  191.5 35.6 %all-reduce.7.cloned.1.call-done = f32[256,256]{0,1:T(8,128)} async-done(((f32[256,256]{0,1:T(8,128)}), f32[256,256]{0,1:T(8,128)}) %all-reduce.7.cloned.1.call-update) | async-done | bytes 262160 | tf_op jit(solution)/shard_map/psum | solution.py:9
  227.1 1.1 copy.5
  228.2 1.0 fusion.19
  229.2 11.7 %cholesky.130 = f32[128,128]{1,0:T(8,128)S(1)} custom-call(f32[128,128]{1,0:T(8,128)S(1)} %cholesky.194), custom_call_target="Cholesky" | custom-call | tf_op jit(solution)/shard_map/jit(cholesky)/cholesky | solution.py:51
  241.0 9.8 %custom-call.13 = f32[1,128,128]{1,2,0:T(8,128)S(1)} custom-call(f32[1,128,128]{2,1,0:T(8,128)S(1)} %get-tuple-element.60), custom_call_target="InvertDiagBlocksLowerTriangular" | custom-call | tf_op jit(solution)/shard_map/jit(cholesky)/cholesky | solution.py:51
  251.4 11.7 %cholesky.147 = f32[128,128]{1,0:T(8,128)S(1)} custom-call(f32[128,128]{1,0:T(8,128)S(1)} %convolution_subtract_fusion.5), custom_call_target="Cholesky" | custom-call | tf_op jit(solution)/shard_map/jit(cholesky)/cholesky | solution.py:51
  263.3 0.7 compare_reduce_fusion.2
  265.5 4.3 %while.4 = (s32[]{:T(128)}, f32[256,256]{0,1:T(8,128)S(1)}, s32[2,2]{1,0:T(2,128)S(1)}, f32[2,128,128]{2,1,0:T(8,128)S(1)}, s32[]{:T(128)}) while((s32[]{:T(128)}, f32[256,256]{0,1:T(8,128)S(1)}, s32[2,2]{1,0:T(2,128)S(1)}, f32[2,128,128]{2,1,0:T(8,128)S(1)}, s32[]{:T(128)}) %tuple.46), condition=%wide.while_cond, body=%wide.while_body.sunk | while | flops 2 | bytes 393321 | solution.py:52
  266.1 1.4 dynamic-slice.12
  268.3 1.4 dynamic-slice.12
  269.8 19.7 %custom-call.14 = f32[2,128,128]{1,2,0:T(8,128)S(1)} custom-call(f32[2,128,128]{2,1,0:T(8,128)S(1)} %get-tuple-element.21), custom_call_target="InvertDiagBlocksLowerTriangular" | custom-call | tf_op jit(solution)/shard_map/jit(_solve_triangular)/triangular_solve | solution.py:52
  291.8 27.9 %all-gather.4.cloned.1.call-done = f32[2,1024,256]{1,2,0:T(8,128)} async-done(((f32[2,128,256]{1,2,0:T(8,128)}), f32[2,1024,256]{1,2,0:T(8,128)}) %all-gather.4.cloned.1.call-update) | async-done | bytes 2097168 | tf_op jit(solution)/shard_map/all_gather | solution.py:45
  319.7 1.9 slice_select_fusion.1
  321.6 38.9 %all-reduce.9.cloned.1.call-done = f32[2,256,256]{1,2,0:T(8,128)} async-done(((f32[2,256,256]{1,2,0:T(8,128)}), f32[2,256,256]{1,2,0:T(8,128)}) %all-reduce.9.cloned.1.call-update) | async-done | bytes 524304 | tf_op jit(solution)/shard_map/psum | solution.py:9
  360.6 1.7 convolution_subtract_fusion
  362.5 11.7 %cholesky.164 = f32[128,128]{1,0:T(8,128)S(1)} custom-call(f32[128,128]{1,0:T(8,128)S(1)} %cholesky.197), custom_call_target="Cholesky" | custom-call | tf_op jit(solution)/shard_map/jit(cholesky)/cholesky | solution.py:59
  374.3 9.8 %custom-call.15 = f32[1,128,128]{1,2,0:T(8,128)S(1)} custom-call(f32[1,128,128]{2,1,0:T(8,128)S(1)} %get-tuple-element.58), custom_call_target="InvertDiagBlocksLowerTriangular" | custom-call | tf_op jit(solution)/shard_map/jit(cholesky)/cholesky | solution.py:59
  384.8 11.7 %cholesky.181 = f32[128,128]{1,0:T(8,128)S(1)} custom-call(f32[128,128]{1,0:T(8,128)S(1)} %convolution_subtract_fusion.4), custom_call_target="Cholesky" | custom-call | tf_op jit(solution)/shard_map/jit(cholesky)/cholesky | solution.py:59
  396.6 0.7 compare_reduce_fusion
  399.4 4.6 %while.5 = (s32[]{:T(128)}, f32[256,256]{0,1:T(8,128)S(1)}, s32[2,2]{1,0:T(2,128)S(1)}, f32[2,128,128]{2,1,0:T(8,128)S(1)}, s32[]{:T(128)}) while((s32[]{:T(128)}, f32[256,256]{0,1:T(8,128)S(1)}, s32[2,2]{1,0:T(2,128)S(1)}, f32[2,128,128]{2,1,0:T(8,128)S(1)}, s32[]{:T(128)}) %tuple.64), condition=%wide.while_cond.clone, body=%wide.while_body.clone.sunk | while | flops 2 | bytes 393321 | solution.py:60
  400.2 1.4 dynamic-slice.14
  402.4 1.4 dynamic-slice.14
  404.0 19.7 %custom-call.16 = f32[2,128,128]{1,2,0:T(8,128)S(1)} custom-call(f32[2,128,128]{2,1,0:T(8,128)S(1)} %get-tuple-element.22), custom_call_target="InvertDiagBlocksLowerTriangular" | custom-call | tf_op jit(solution)/shard_map/jit(_solve_triangular)/triangular_solve | solution.py:60
  425.6 0.8 copy.16
  (79 shorter events, 11.7 us)
Async XLA Ops:
  6.5 92.1 %all-reduce.5.cloned.1.call-start = ((), (), s32[]{:S(2)}) async-start(), calls=%async_computation.1 | async-start | bytes 4194304 | tf_op jit(solution)/shard_map/psum | solution.py:9
  9.6 0.7 copy-start.3
  9.7 154.1 %reduce-scatter.2.cloned.1.call-start = ((), (), s32[]{:S(2)}) async-start(), calls=%async_computation.2 | async-start | bytes 2359296 | tf_op jit(solution)/shard_map/reduce_scatter | solution.py:38
  98.7 16.6 %copy-start = (f32[1,1024,1024]{2,1,0:T(8,128)S(1)}, f32[1,1024,1024]{2,1,0:T(8,128)}, u32[]{:S(2)}) copy-start(f32[1,1024,1024]{2,1,0:T(8,128)} %param.8) | copy-start | bytes 12582916
  123.5 40.3 %copy-start.2 = (f32[512]{0:T(512)S(1)}, f32[512]{0:T(512)}, u32[]{:S(2)}) copy-start(f32[512]{0:T(512)} %param.10) | copy-start | bytes 6148
  123.5 65.7 %all-gather.6.cloned.1.call-start = ((), (), s32[]{:S(2)}) async-start(), calls=%async_computation.6 | async-start | bytes 1179648 | tf_op jit(solution)/shard_map/all_gather | solution.py:45
  165.6 61.5 %all-reduce.7.cloned.1.call-start = ((), (), s32[]{:S(2)}) async-start(), calls=%async_computation.3 | async-start | bytes 524288 | tf_op jit(solution)/shard_map/psum | solution.py:9
  191.0 128.8 %all-gather.4.cloned.1.call-start = ((), (), s32[]{:S(2)}) async-start(), calls=%async_computation.4 | async-start | bytes 2359296 | tf_op jit(solution)/shard_map/all_gather | solution.py:45
  291.6 69.0 %all-reduce.9.cloned.1.call-start = ((), (), s32[]{:S(2)}) async-start(), calls=%async_computation.5 | async-start | bytes 1048576 | tf_op jit(solution)/shard_map/psum | solution.py:9
  399.3 25.3 %copy-start.1 = (f32[2,256,256]{1,2,0:T(8,128)S(1)}, f32[2,256,256]{1,2,0:T(8,128)}, u32[]{:S(2)}) copy-start(f32[2,256,256]{1,2,0:T(8,128)} %all-reduce.9.cloned.1.call-done) | copy-start | bytes 1572868
Sparse Core Ops, SparseCore 0:
  9.8 88.8 all-reduce.4
  123.6 40.1 reduce-scatter.1
  165.7 23.4 all-gather.5
  191.4 35.5 all-reduce.6
  291.7 27.9 all-gather.3
  321.9 38.6 all-reduce.8
where the time goes:
time: 440 us; the launch traced here: 434 us
  waiting for transfers between devices  255 us (58%)
  other arithmetic  118 us (27%)
  matrix products  30.8 us (7%)
  between operations  16.8 us (4%)
  local copies, waits for them, and re-layouts  12.4 us (3%)
    psum x3, waiting for transfers between devices, broadcast(): return lax.psum(kept, axis)  163 us
    all_gather x2, waiting for transfers between devices, fetch(): whole = lax.all_gather(stacked, 'scen', axis=1, tiled=True)  51.5 us
    reduce_scatter x1, waiting for transfers between devices, body(): lax.psum_scatter(outer_rows(block, product), 'scen', scatter_dimension=0,...  40.2 us
    another operation x7, other arithmetic, body(): chol2 = jnp.linalg.cholesky(update)  34.7 us
    another operation x6, other arithmetic, body(): chol1 = jnp.linalg.cholesky(block_one)  34 us
    another operation x3, other arithmetic, body(): inv1 = jax.scipy.linalg.solve_triangular(chol1, identity, lower=True)  19.7 us
    another operation x2, other arithmetic, body(): inv2 = jax.scipy.linalg.solve_triangular(chol2, identity, lower=True)  19.7 us
    dot_general x5, matrix products, matmul(): jnp.dot(left, right, precision=lax.Precision.HIGHEST, preferred_element_t...  19.6 us
  transfers between devices with their start and end apart: 6, of which 6 were waited for; matrix products, arithmetic and copies ran while one was open for 0% of the time, Pallas kernels for 0%

commit v1 on v0

v1 whole, which is shorter than its diff:
```python
import functools

import jax
import jax.numpy as jnp
from jax import lax
from jax.experimental import pallas as pl
from jax.experimental.pallas import tpu as pltpu
from jax.sharding import PartitionSpec as P

BLOCK = 128
SUB = 8


def high(left, right, dims):
    return lax.dot_general(
        left, right, (dims, ((), ())), precision=lax.Precision.HIGH, preferred_element_type=jnp.float32
    )


def full(left, right, dims):
    return lax.dot_general(
        left, right, (dims, ((), ())), precision=lax.Precision.HIGHEST, preferred_element_type=jnp.float32
    )


def eliminate(tiles):
    count, size = len(tiles), tiles[0].shape[1]
    lane = lax.broadcasted_iota(jnp.int32, (SUB, size), 1)
    sub = lax.broadcasted_iota(jnp.int32, (SUB, size), 0)

    def lanes(x, c):
        return jnp.broadcast_to(x[:, c : c + 1], (SUB, size))

    def subs(x, q):
        return jnp.broadcast_to(x[q : q + 1, :], (SUB, size))

    scaled, scales = [], []
    for at in range(count):
        low = SUB * at
        rows = tiles[at]
        cols = [lanes(rows, low + q) for q in range(SUB)]
        inverse, upper, pivots = [], {}, None
        for q in range(SUB):
            pivot = subs(cols[q], q)
            pivots = pivot if pivots is None else jnp.where(sub == q, pivot, pivots)
            inverse.append(1.0 / pivot)
            times = jnp.where(sub > q, cols[q] * inverse[q], 0.0)
            for p in range(q + 1, SUB):
                upper[q, p] = subs(cols[q], p)
                cols[p] = cols[p] - times * upper[q, p]
            pivot_row = jnp.where(lane == low + q, 1.0, subs(rows, q))
            rows = jnp.where((lane == low + q) & (sub > q), 0.0, rows) - times * pivot_row
        pivot_rows = []
        for q in range(SUB):
            row = jnp.where(lane == low + q, 1.0, subs(rows, q))
            pivot_rows.append(jnp.where((lane > low + q) & (lane < low + SUB), 0.0, row))
        own = (lane >= low) & (lane < low + SUB)
        for other in range(at + 1, count):
            tile = tiles[other]
            theirs = [lanes(tile, low + q) for q in range(SUB)]
            tile = jnp.where(own, 0.0, tile)
            times = []
            for q in range(SUB):
                value = theirs[q]
                for p in range(q):
                    value = value - times[p] * upper[p, q]
                value = value * inverse[q]
                times.append(value)
                tile = tile - value * pivot_rows[q]
            tiles[other] = tile
        scale = lax.rsqrt(pivots)
        scales.append(scale)
        scaled.append(rows * scale)
    return scaled, scales


def factor_kernel(plane_ref, a_ref, l_ref, w_ref, base_ref, scale_ref):
    size = a_ref.shape[0]

    @pl.when(plane_ref[0] == 0)
    def _():
        w_ref[...] = a_ref[...]

        def step(j, carry):
            low = pl.multiple_of(j * BLOCK, BLOCK)
            mine = pl.ds(low, BLOCK)
            tiles = [w_ref[pl.ds(low + SUB * t, SUB), mine] for t in range(BLOCK // SUB)]
            scaled, scales = eliminate(tiles)
            for t in range(BLOCK // SUB):
                base_ref[SUB * t : SUB * t + SUB, :] = scaled[t]
                scale_ref[SUB * t : SUB * t + SUB, :] = scales[t]
            both = base_ref[...]
            row = lax.broadcasted_iota(jnp.int32, (BLOCK, BLOCK), 0)
            col = lax.broadcasted_iota(jnp.int32, (BLOCK, BLOCK), 1)
            inverse = jnp.where(col < row, both, jnp.where(col == row, scale_ref[...], 0.0))
            factor_t = jnp.where(col >= row, both, 0.0)
            below = lax.broadcasted_iota(jnp.int32, (size, BLOCK), 0) >= low + BLOCK
            panel = jnp.where(below, full(w_ref[:, mine], inverse, ((1,), (1,))), 0.0)
            w_ref[mine, :] = full(inverse, w_ref[mine, :], ((1,), (0,)))
            w_ref[mine, mine] = inverse
            pivot_rows = w_ref[mine, :]
            w_ref[:, mine] = jnp.where(below, 0.0, w_ref[:, mine])
            w_ref[...] = w_ref[...] - full(panel, pivot_rows, ((1,), (0,)))
            l_ref[:, mine] = panel
            l_ref[mine, mine] = factor_t.T
            return carry

        lax.fori_loop(0, size // BLOCK, step, 0)
        row = lax.broadcasted_iota(jnp.int32, (size, size), 0)
        col = lax.broadcasted_iota(jnp.int32, (size, size), 1)
        w_ref[...] = jnp.where(col <= row, w_ref[...], 0.0)


def factor(plane, a):
    size = a.shape[0]
    return pl.pallas_call(
        factor_kernel,
        out_shape=(jax.ShapeDtypeStruct((size, size), jnp.float32),) * 2,
        in_specs=[pl.BlockSpec(memory_space=pltpu.SMEM), pl.BlockSpec(memory_space=pltpu.VMEM)],
        out_specs=(pl.BlockSpec(memory_space=pltpu.VMEM),) * 2,
        scratch_shapes=[pltpu.VMEM((BLOCK, BLOCK), jnp.float32)] * 2,
        cost_estimate=pl.CostEstimate(flops=2 * size**3, bytes_accessed=12 * size * size, transcendentals=size),
    )(plane, a)


def pack(a):
    nb = a.shape[0] // BLOCK
    strips = []
    for i in range(nb // 2):
        k = nb - 1 - i
        strips.append(
            jnp.concatenate(
                [a[k * BLOCK : (k + 1) * BLOCK, : (k + 1) * BLOCK], a[i * BLOCK : (i + 1) * BLOCK, : (i + 1) * BLOCK]],
                axis=1,
            )
        )
    return jnp.concatenate(strips, axis=0)


def unpack(p, nb):
    strips = [None] * nb
    for i in range(nb // 2):
        k = nb - 1 - i
        strip = p[i * BLOCK : (i + 1) * BLOCK]
        for b, low in ((k, 0), (i, (k + 1) * BLOCK)):
            part = strip[:, low : low + (b + 1) * BLOCK]
            strips[b] = jnp.pad(part, ((0, 0), (0, (nb - 1 - b) * BLOCK)))
    return jnp.concatenate(strips, axis=0)


def exchange(x, bit, count):
    return lax.ppermute(x, "scen", [(i, i ^ (1 << bit)) for i in range(count)])


def orders(count):
    bits = count.bit_length() - 1
    split = 1 + (bits - 1 + 1) // 2
    near, first, second = [0], list(range(1, split)), list(range(split, bits))
    return bits, near, first, second


def halve(x, names, bit, count):
    axis = names.index(bit)
    mine = (lax.axis_index("scen") >> bit) & 1
    keep = lax.dynamic_index_in_dim(x, mine, axis, keepdims=False)
    send = lax.dynamic_index_in_dim(x, 1 - mine, axis, keepdims=False)
    return keep + exchange(send, bit, count), [n for n in names if n != bit]


def scatter_sum(x):
    count = lax.axis_size("scen")
    bits, near, first, second = orders(count)
    rows = x.shape[0] // count
    x = x.reshape((2,) * bits + (rows,) + x.shape[1:])
    names = list(range(bits - 1, -1, -1))
    for bit in near:
        x, names = halve(x, names, bit, count)
    lead = (slice(None),) * len(names)
    parts = [x[lead + (slice(0, rows // 2),)], x[lead + (slice(rows // 2, rows),)]]
    lists = [list(names), list(names)]
    for a, b in zip(first + second, second + first):
        for i, bit in ((0, a), (1, b)):
            parts[i], lists[i] = halve(parts[i], lists[i], bit, count)
    return jnp.concatenate(parts, axis=0)


def gather_rows(x):
    count = lax.axis_size("scen")
    bits, near, first, second = orders(count)
    rows = x.shape[0]
    me = lax.axis_index("scen")

    def grow(part, names, bit):
        other = exchange(part, bit, count)
        low = ((me >> bit) & 1) == 0
        names2 = sorted(names + [bit], reverse=True)
        pair = [jnp.where(low, part, other), jnp.where(low, other, part)]
        return jnp.stack(pair, axis=names2.index(bit)), names2

    parts, lists = [x[: rows // 2], x[rows // 2 :]], [[], []]
    for a, b in zip((first + second)[::-1], (second + first)[::-1]):
        for i, bit in ((0, a), (1, b)):
            parts[i], lists[i] = grow(parts[i], lists[i], bit)
    whole, names = jnp.concatenate(parts, axis=len(lists[0])), lists[0]
    for bit in near[::-1]:
        whole, names = grow(whole, names, bit)
    return whole.reshape((count * rows,) + x.shape[1:])


def body(inverses, coupling, tile_mask, hess_diag):
    local = coupling[0]
    width = hess_diag.shape[0]
    nb = width // BLOCK
    scen, cols = lax.axis_size("scen"), lax.axis_size("col")
    me, plane = lax.axis_index("scen"), lax.axis_index("col")
    rows = local.shape[1] // scen
    keep = jnp.repeat(tile_mask[0].astype(jnp.float32), local.shape[0] // tile_mask.shape[1])
    masked_inverse = inverses[0] * keep[:, None] * keep[None, :]
    halves, quarters = 2, 4
    half = width // halves
    quarter = local.shape[0] // quarters

    products = [high(masked_inverse, local[:, h * half : (h + 1) * half], ((1,), (0,))) for h in range(halves)]

    chunks = []
    for h in range(halves):
        for q in range(quarters):
            piece = products[h][q * quarter : (q + 1) * quarter]
            mine = jnp.where(plane == 0, piece, 0.0)
            for hop in range(cols - 1):
                piece = lax.ppermute(piece, "col", [(hop, hop + 1)])
                mine = mine + piece
            chunks.append(mine)

    product = jnp.concatenate(products, axis=1)
    corner = high(local[:, :width], product, ((0,), (0,)))
    packed = gather_rows(scatter_sum(pack(corner)))
    square = unpack(packed, nb)
    square = jnp.tril(square)
    square = square + jnp.tril(square, -1).T + jnp.diag(hess_diag)
    lower, winv = factor(plane.astype(jnp.int32).reshape(1), square)

    packed = pack(winv)
    each = packed.shape[0] // scen
    part = lax.dynamic_slice_in_dim(packed, me * each, each, 0)
    sent = jnp.where(plane == 0, part, 0.0)
    for hop in range(1, cols):
        sent = sent + lax.ppermute(part, "col", [(0, hop)])
    winv = unpack(gather_rows(sent), nb)

    sums = []
    for h in range(halves):
        whole = jnp.concatenate(chunks[h * quarters : (h + 1) * quarters], axis=0)
        sums.append(scatter_sum(high(local, whole, ((0,), (0,)))))
    solved = full(jnp.concatenate(sums, axis=1), winv, ((1,), (1,)))
    first = plane * local.shape[1] + me * rows
    own = lax.dynamic_slice_in_dim(lower, jnp.clip(first, 0, width - rows), rows, 0)
    return jnp.where(first < width, own, solved)


def solution(mesh):
    in_specs = (P("scen", None, None), P("scen", None, "col"), P("scen", None), P())
    out_specs = P(("col", "scen"), None)
    return jax.shard_map(body, mesh=mesh, in_specs=in_specs, out_specs=out_specs, check_vma=False)
```

time: 440 us -> 204 us (0.46)
  the two profiles are of different devices: /device:TPU:0 before, /device:TPU:24 now
where the time goes in v1:
time: 204 us; the launch traced here: 203 us
  waiting for transfers between devices  89 us (44%)
  starting transfers between devices  55.6 us (27%)
  matrix products  19.4 us (10%)
  local copies, waits for them, and re-layouts  19.2 us (9%)
  other arithmetic  16 us (8%)
  Pallas kernels  2.55 us (1%)
    ppermute x24, waiting for transfers between devices, body(): piece = lax.ppermute(piece, 'col', [(hop, hop + 1)])  37.4 us
    ppermute x3, waiting for transfers between devices, body(): sent = sent + lax.ppermute(part, 'col', [(0, hop)])  29.1 us
    ppermute x25, starting transfers between devices, exchange(): return lax.ppermute(x, 'scen', [(i, i ^ 1 << bit) for i in range(count)])  26.8 us
    ppermute x24, starting transfers between devices, body(): piece = lax.ppermute(piece, 'col', [(hop, hop + 1)])  26.2 us
    ppermute x25, waiting for transfers between devices, exchange(): return lax.ppermute(x, 'scen', [(i, i ^ 1 << bit) for i in range(count)])  22.6 us
    dot_general x5, matrix products, high(): lax.dot_general(left, right, (dims, ((), ())), precision=lax.Precision.HI...  17 us
    dynamic_slice x7, local copies, waits for them, and re-layouts, halve(): send = lax.dynamic_index_in_dim(x, 1 - mine, axis, keepdims=False)  4.86 us
    add x4, other arithmetic, body(): mine = mine + piece  4.75 us
  transfers between devices with their start and end apart: 52, of which 23 were waited for; matrix products, arithmetic and copies ran while one was open for 20% of the time, Pallas kernels for 1%

profile of v1, /device:TPU:24, one launch (start us, length us, event | category | flops | bytes accessed | tf_op | source)
XLA Modules:
  0.0 202.9 jit_solution(14208198746003226433)
XLA Ops:
  0.9 4.6 %fusion.3 = f32[1024,256]{1,0:T(8,128)S(1)} fusion(f32[1,1024,1024]{2,1,0:T(8,128)} %param.4, f32[1024]{0:T(1024)S(1)} %broadcast_bitcast_fusion, f32[1024,1024]{1,0:T(8,128)} %bitcast.119), kind=kOutput, calls=%fused_computation.3 | convolution fusion | flops 1612709888 | bytes 6299648 | tf_op jit(solution)/shard_map/dot_general | solution.py:15
  5.5 4.1 %fusion.1 = f32[1024,256]{1,0:T(8,128)S(1)} fusion(f32[1,1024,1024]{2,1,0:T(8,128)} %param.4, f32[1024]{0:T(1024)S(1)} %broadcast_bitcast_fusion, f32[1024,1024]{1,0:T(8,128)S(1)} %bitcast.120), kind=kOutput, calls=%fused_computation.2 | convolution fusion | flops 1612709888 | bytes 6299648 | tf_op jit(solution)/shard_map/dot_general | solution.py:15
  9.7 1.9 fusion.14
  16.4 1.6 collective-permute-start.5
  19.5 1.8 collective-permute-done.5
  22.9 1.6 collective-permute-start.2
  27.0 1.6 collective-permute-start.3
  29.5 1.6 collective-permute-start.8
  34.0 1.6 collective-permute-done.4
  45.8 2.5 %bitcast_add_fusion = f32[512,512]{0,1:T(8,128)} fusion(f32[512,512]{1,0:T(8,128)} %copy.23, s32[512]{0:T(512)S(1)} %iota_add_fusion, f32[128,512]{0,1:T(8,128)} %copy.35, f32[128,512]{0,1:T(8,128)S(1)} %broadcast_select_fusion.1, f32[128,256]{0,1:T(8,128)S(1)} %copy.33, f32[128,128]{0,1:T(8,128)} %copy.32), kind=kLoop, calls=%fused_computation.48 | loop fusion | flops 3670016 | bytes 2820096 | tf_op jit(solution)/shard_map/add | solution.py:240
  51.0 2.5 %shard_map.46 = (f32[512,512]{1,0:T(8,128)}, f32[512,512]{1,0:T(8,128)}) custom-call(s32[1]{0:T(128)} %bitcast.plane_ref, f32[512,512]{1,0:T(8,128)} %select_add_fusion.a_ref), custom_call_target="tpu_custom_call" | custom-call | flops 268435456 | bytes 3145728 | tf_op jit(solution)/shard_map/pallas_call | solution.py:116
  63.2 29.1 %collective-permute-done.46 = f32[32,640]{1,0:T(8,128)S(1)} collective-permute-done((f32[32,640]{1,0:T(8,128)S(1)}, f32[32,640]{1,0:T(8,128)S(1)}, u32[]{:S(2)}, u32[]{:S(2)}) %collective-permute-start.46) | collective-permute-done | bytes 81952 | tf_op jit(solution)/shard_map/ppermute | solution.py:248
  92.3 1.6 collective-permute-start.47
  103.6 3.7 %collective-permute-done.50 = f32[2,16,640]{2,1,0:T(8,128)S(1)} collective-permute-done((f32[2,16,640]{2,1,0:T(8,128)S(1)}, f32[2,16,640]{2,1,0:T(8,128)S(1)}, u32[]{:S(2)}, u32[]{:S(2)}) %collective-permute-start.50) | collective-permute-done | bytes 81952 | tf_op jit(solution)/shard_map/ppermute | solution.py:152
  108.3 3.5 %collective-permute-done.48 = f32[2,16,640]{2,1,0:T(8,128)S(1)} collective-permute-done((f32[2,16,640]{2,1,0:T(8,128)S(1)}, f32[2,16,640]{2,1,0:T(8,128)S(1)}, u32[]{:S(2)}, u32[]{:S(2)}) %collective-permute-start.48) | collective-permute-done | bytes 81952 | tf_op jit(solution)/shard_map/ppermute | solution.py:152
  120.6 4.4 %collective-permute-done.21 = f32[256,256]{1,0:T(8,128)S(1)} collective-permute-done((f32[256,256]{1,0:T(8,128)S(1)}, f32[256,256]{1,0:T(8,128)S(1)}, u32[]{:S(2)}, u32[]{:S(2)}) %collective-permute-start.21) | collective-permute-done | bytes 262176 | tf_op jit(solution)/shard_map/ppermute | solution.py:231
  126.2 4.3 %collective-permute-done.18 = f32[256,256]{1,0:T(8,128)S(1)} collective-permute-done((f32[256,256]{1,0:T(8,128)S(1)}, f32[256,256]{1,0:T(8,128)S(1)}, u32[]{:S(2)}, u32[]{:S(2)}) %collective-permute-start.18) | collective-permute-done | bytes 262176 | tf_op jit(solution)/shard_map/ppermute | solution.py:231
  132.1 4.2 %collective-permute-done.15 = f32[256,256]{1,0:T(8,128)S(1)} collective-permute-done((f32[256,256]{1,0:T(8,128)S(1)}, f32[256,256]{1,0:T(8,128)S(1)}, u32[]{:S(2)}, u32[]{:S(2)}) %collective-permute-start.15) | collective-permute-done | bytes 262176 | tf_op jit(solution)/shard_map/ppermute | solution.py:231
  136.6 2.2 %convolution_bitcast_fusion.1 = f32[1024,256]{0,1:T(8,128)S(1)} fusion(f32[256,256]{1,0:T(8,128)S(1)} %get-tuple-element.17, f32[256,256]{1,0:T(8,128)S(1)} %get-tuple-element.16, f32[256,256]{1,0:T(8,128)S(1)} %get-tuple-element.15, f32[256,256]{1,0:T(8,128)S(1)} %get-tuple-element.11, f32[1,1024,1024]{2,1,0:T(8,128)S(1)} %copy-done.1), kind=kOutput, calls=%fused_computation.17 | convolution fusion | flops 1611399168 | bytes 6291456 | tf_op jit(solution)/shard_map/dot_general | solution.py:15
  139.6 16.2 %collective-permute-done.38 = f32[256,256]{1,0:T(8,128)} collective-permute-done((f32[256,256]{1,0:T(8,128)}, f32[256,256]{1,0:T(8,128)}, u32[]{:S(2)}, u32[]{:S(2)}) %collective-permute-start.38) | collective-permute-done | bytes 262176 | tf_op jit(solution)/shard_map/ppermute | solution.py:231
  155.8 5.4 %collective-permute-done.35 = f32[256,256]{1,0:T(8,128)} collective-permute-done((f32[256,256]{1,0:T(8,128)}, f32[256,256]{1,0:T(8,128)}, u32[]{:S(2)}, u32[]{:S(2)}) %collective-permute-start.35) | collective-permute-done | bytes 262176 | tf_op jit(solution)/shard_map/ppermute | solution.py:231
  161.3 2.8 %collective-permute-done.32 = f32[256,256]{1,0:T(8,128)} collective-permute-done((f32[256,256]{1,0:T(8,128)}, f32[256,256]{1,0:T(8,128)}, u32[]{:S(2)}, u32[]{:S(2)}) %collective-permute-start.32) | collective-permute-done | bytes 262176 | tf_op jit(solution)/shard_map/ppermute | solution.py:231
  164.1 1.8 add_add_fusion.2
  165.9 4.2 %convolution_bitcast_fusion = f32[1024,256]{0,1:T(8,128)S(1)} fusion(f32[256,256]{1,0:T(8,128)S(1)} %get-tuple-element.26, f32[256,256]{1,0:T(8,128)S(1)} %get-tuple-element.25, f32[256,256]{1,0:T(8,128)S(1)} %get-tuple-element.24, f32[256,256]{1,0:T(8,128)S(1)} %get-tuple-element.20, f32[1,1024,1024]{2,1,0:T(8,128)} %param.5), kind=kOutput, calls=%fused_computation.16 | convolution fusion | flops 1611399168 | bytes 6291456 | tf_op jit(solution)/shard_map/dot_general | solution.py:15
  170.9 2.8 %constant_dynamic-slice_fusion.6 = (f32[2,2,1,128,256]{3,2,1,0,4:T(1,128)}, f32[2,2,1,128,256]{3,2,1,0,4:T(1,128)S(1)}, f32[2,2,1,128,256]{3,2,1,0,4:T(1,128)S(1)}, f32[2,2,1,128,256]{3,2,1,0,4:T(1,128)}) fusion(f32[2,2,2,128,256]{3,2,1,0,4:T(2,128)S(1)} %reshape.25, s32[]{:T(128)S(6)} %select_n.220, s32[]{:T(128)S(6)} %select_n.219, ...), kind=kLoop, calls=%fused_computation.138 | loop fusion | bytes 4194312 | tf_op jit(solution)/shard_map/jit(dynamic_index_in_dim)/dynamic_slice | solution.py:166
  178.1 1.6 collective-permute-start.42
  185.7 1.6 collective-permute-done.42
  187.7 1.6 collective-permute-start.43
  190.7 2.3 %collective-permute-done.25 = f32[2,64,256]{1,0,2:T(2,128)S(1)} collective-permute-done((f32[2,64,256]{1,0,2:T(2,128)S(1)}, f32[2,64,256]{1,0,2:T(2,128)S(1)}, u32[]{:S(2)}, u32[]{:S(2)}) %collective-permute-start.25) | collective-permute-done | bytes 131104 | tf_op jit(solution)/shard_map/ppermute | solution.py:152
  193.3 1.6 collective-permute-start.26
  197.8 1.6 collective-permute-done.26
  200.4 2.4 %convolution_select_fusion = f32[128,512]{1,0:T(8,128)} fusion(f32[128,256]{0,1:T(8,128)S(1)} %copy.37, f32[128,128]{0,1:T(8,128)S(1)} %copy.36, f32[128,512]{0,1:T(8,128)S(1)} %copy.39, f32[128,512]{0,1:T(8,128)S(1)} %broadcast_select_fusion, f32[64,256]{0,1:T(8,128)S(1)} %add.258, f32[64,256]{0,1:T(8,128)S(1)} %add.256, f32[64,256]{0,1:T(8,128)S(1)} %add.241, ...), kind=kOutput, calls=%fused_computation.18 | convolution fusion | flops 405274624 | bytes 1507333 | tf_op jit(solution)/shard_map/dot_general | solution.py:21
  (204 shorter events, 77.6 us)
Async XLA Ops:
  12.8 23.0 %collective-permute-start.10 = (f32[256,256]{1,0:T(8,128)}, f32[256,256]{1,0:T(8,128)}, u32[]{:S(2)}, u32[]{:S(2)}) collective-permute-start(f32[256,256]{1,0:T(8,128)} %slice.189), channel_id=1, source_target_pairs={{0,1},{4,5},{8,9},{12,13},{16,17},{20,21},{24,25},{28,29}} | collective-permute-start | bytes 786440 | tf_op jit(solution)/shard_map/ppermute | solution.py:231
  14.9 22.3 %collective-permute-start.27 = (f32[256,256]{1,0:T(8,128)}, f32[256,256]{1,0:T(8,128)}, u32[]{:S(2)}, u32[]{:S(2)}) collective-permute-start(f32[256,256]{1,0:T(8,128)} %slice.195), channel_id=1, source_target_pairs={{0,1},{4,5},{8,9},{12,13},{16,17},{20,21},{24,25},{28,29}} | collective-permute-start | bytes 786440 | tf_op jit(solution)/shard_map/ppermute | solution.py:231
  18.0 4.9 %collective-permute-start.1 = (f32[2,16,640]{2,1,0:T(8,128)S(1)}, f32[2,16,640]{2,1,0:T(8,128)S(1)}, u32[]{:S(2)}, u32[]{:S(2)}) collective-permute-start(f32[2,16,640]{2,1,0:T(8,128)S(1)} %dynamic-slice_bitcast_fusion.4), channel_id=1, source_target_pairs={{0,8},{4,12},{8,0},{12,4},{16,24},{20,28},{24,16},{28,20},{1,9},{5... | collective-permute-start | bytes 245768 | tf_op jit(solution)/shard_map/ppermute | solution.py:152
  35.7 5.5 %collective-permute-start.9 = (f32[2,2,32,640]{3,2,1,0:T(8,128)S(1)}, f32[2,2,32,640]{3,2,1,0:T(8,128)S(1)}, u32[]{:S(2)}, u32[]{:S(2)}) collective-permute-start(f32[2,2,32,640]{3,2,1,0:T(8,128)S(1)} %maximum_maximum_fusion.1), channel_id=1, source_target_pairs={{0,4},{4,0},{8,12},{12,8},{16,20},{20,16},{24,28},{28,24},{1,5},{5... | collective-permute-start | bytes 983048 | tf_op jit(solution)/shard_map/ppermute | solution.py:152
  38.6 21.3 %collective-permute-start.12 = (f32[256,256]{1,0:T(8,128)}, f32[256,256]{1,0:T(8,128)}, u32[]{:S(2)}, u32[]{:S(2)}) collective-permute-start(f32[256,256]{1,0:T(8,128)} %collective-permute-done.11), channel_id=1, source_target_pairs={{2,3},{6,7},{10,11},{14,15},{18,19},{22,23},{26,27},{30,31}} | collective-permute-start | bytes 786440 | tf_op jit(solution)/shard_map/ppermute | solution.py:231
  39.9 54.0 %collective-permute-start.29 = (f32[256,256]{1,0:T(8,128)}, f32[256,256]{1,0:T(8,128)}, u32[]{:S(2)}, u32[]{:S(2)}) collective-permute-start(f32[256,256]{1,0:T(8,128)} %collective-permute-done.28), channel_id=1, source_target_pairs={{2,3},{6,7},{10,11},{14,15},{18,19},{22,23},{26,27},{30,31}} | collective-permute-start | bytes 786440 | tf_op jit(solution)/shard_map/ppermute | solution.py:231
  58.6 33.7 %collective-permute-start.46 = (f32[32,640]{1,0:T(8,128)S(1)}, f32[32,640]{1,0:T(8,128)S(1)}, u32[]{:S(2)}, u32[]{:S(2)}) collective-permute-start(f32[32,640]{1,0:T(8,128)S(1)} %fusion.61), channel_id=1, source_target_pairs={{0,3},{4,7},{8,11},{12,15},{16,19},{20,23},{24,27},{28,31}} | collective-permute-start | bytes 245768 | tf_op jit(solution)/shard_map/ppermute | solution.py:248
  61.2 37.4 %collective-permute-start.19 = (f32[256,256]{1,0:T(8,128)S(1)}, f32[256,256]{1,0:T(8,128)S(1)}, u32[]{:S(2)}, u32[]{:S(2)}) collective-permute-start(f32[256,256]{1,0:T(8,128)S(1)} %get-tuple-element.12), channel_id=1, source_target_pairs={{0,1},{4,5},{8,9},{12,13},{16,17},{20,21},{24,25},{28,29}} | collective-permute-start | bytes 786440 | tf_op jit(solution)/shard_map/ppermute | solution.py:231
  61.9 37.5 %collective-permute-start.16 = (f32[256,256]{1,0:T(8,128)S(1)}, f32[256,256]{1,0:T(8,128)S(1)}, u32[]{:S(2)}, u32[]{:S(2)}) collective-permute-start(f32[256,256]{1,0:T(8,128)S(1)} %get-tuple-element.13), channel_id=1, source_target_pairs={{0,1},{4,5},{8,9},{12,13},{16,17},{20,21},{24,25},{28,29}} | collective-permute-start | bytes 786440 | tf_op jit(solution)/shard_map/ppermute | solution.py:231
  62.6 37.5 %collective-permute-start.13 = (f32[256,256]{1,0:T(8,128)S(1)}, f32[256,256]{1,0:T(8,128)S(1)}, u32[]{:S(2)}, u32[]{:S(2)}) collective-permute-start(f32[256,256]{1,0:T(8,128)S(1)} %get-tuple-element.14), channel_id=1, source_target_pairs={{0,1},{4,5},{8,9},{12,13},{16,17},{20,21},{24,25},{28,29}} | collective-permute-start | bytes 786440 | tf_op jit(solution)/shard_map/ppermute | solution.py:231
  99.3 13.8 %collective-permute-start.20 = (f32[256,256]{1,0:T(8,128)S(1)}, f32[256,256]{1,0:T(8,128)S(1)}, u32[]{:S(2)}, u32[]{:S(2)}) collective-permute-start(f32[256,256]{1,0:T(8,128)S(1)} %collective-permute-done.19), channel_id=1, source_target_pairs={{1,2},{5,6},{9,10},{13,14},{17,18},{21,22},{25,26},{29,30}} | collective-permute-start | bytes 786440 | tf_op jit(solution)/shard_map/ppermute | solution.py:231
  100.0 14.5 %collective-permute-start.17 = (f32[256,256]{1,0:T(8,128)S(1)}, f32[256,256]{1,0:T(8,128)S(1)}, u32[]{:S(2)}, u32[]{:S(2)}) collective-permute-start(f32[256,256]{1,0:T(8,128)S(1)} %collective-permute-done.16), channel_id=1, source_target_pairs={{1,2},{5,6},{9,10},{13,14},{17,18},{21,22},{25,26},{29,30}} | collective-permute-start | bytes 786440 | tf_op jit(solution)/shard_map/ppermute | solution.py:231
  100.7 15.1 %collective-permute-start.14 = (f32[256,256]{1,0:T(8,128)S(1)}, f32[256,256]{1,0:T(8,128)S(1)}, u32[]{:S(2)}, u32[]{:S(2)}) collective-permute-start(f32[256,256]{1,0:T(8,128)S(1)} %collective-permute-done.13), channel_id=1, source_target_pairs={{1,2},{5,6},{9,10},{13,14},{17,18},{21,22},{25,26},{29,30}} | collective-permute-start | bytes 786440 | tf_op jit(solution)/shard_map/ppermute | solution.py:231
  101.4 15.7 %collective-permute-start.37 = (f32[256,256]{1,0:T(8,128)S(1)}, f32[256,256]{1,0:T(8,128)}, u32[]{:S(2)}, u32[]{:S(2)}) collective-permute-start(f32[256,256]{1,0:T(8,128)S(1)} %collective-permute-done.36), channel_id=1, source_target_pairs={{1,2},{5,6},{9,10},{13,14},{17,18},{21,22},{25,26},{29,30}} | collective-permute-start | bytes 786440 | tf_op jit(solution)/shard_map/ppermute | solution.py:231
  111.8 7.5 %collective-permute-start.34 = (f32[256,256]{1,0:T(8,128)S(1)}, f32[256,256]{1,0:T(8,128)}, u32[]{:S(2)}, u32[]{:S(2)}) collective-permute-start(f32[256,256]{1,0:T(8,128)S(1)} %collective-permute-done.33), channel_id=1, source_target_pairs={{1,2},{5,6},{9,10},{13,14},{17,18},{21,22},{25,26},{29,30}} | collective-permute-start | bytes 786440 | tf_op jit(solution)/shard_map/ppermute | solution.py:231
  113.1 6.1 %collective-permute-start.31 = (f32[256,256]{1,0:T(8,128)S(1)}, f32[256,256]{1,0:T(8,128)}, u32[]{:S(2)}, u32[]{:S(2)}) collective-permute-start(f32[256,256]{1,0:T(8,128)S(1)} %collective-permute-done.30), channel_id=1, source_target_pairs={{1,2},{5,6},{9,10},{13,14},{17,18},{21,22},{25,26},{29,30}} | collective-permute-start | bytes 786440 | tf_op jit(solution)/shard_map/ppermute | solution.py:231
  114.5 10.5 %collective-permute-start.21 = (f32[256,256]{1,0:T(8,128)S(1)}, f32[256,256]{1,0:T(8,128)S(1)}, u32[]{:S(2)}, u32[]{:S(2)}) collective-permute-start(f32[256,256]{1,0:T(8,128)S(1)} %collective-permute-done.20), channel_id=1, source_target_pairs={{2,3},{6,7},{10,11},{14,15},{18,19},{22,23},{26,27},{30,31}} | collective-permute-start | bytes 786440 | tf_op jit(solution)/shard_map/ppermute | solution.py:231
  115.8 14.8 %collective-permute-start.18 = (f32[256,256]{1,0:T(8,128)S(1)}, f32[256,256]{1,0:T(8,128)S(1)}, u32[]{:S(2)}, u32[]{:S(2)}) collective-permute-start(f32[256,256]{1,0:T(8,128)S(1)} %collective-permute-done.17), channel_id=1, source_target_pairs={{2,3},{6,7},{10,11},{14,15},{18,19},{22,23},{26,27},{30,31}} | collective-permute-start | bytes 786440 | tf_op jit(solution)/shard_map/ppermute | solution.py:231
  117.1 19.2 %collective-permute-start.15 = (f32[256,256]{1,0:T(8,128)S(1)}, f32[256,256]{1,0:T(8,128)S(1)}, u32[]{:S(2)}, u32[]{:S(2)}) collective-permute-start(f32[256,256]{1,0:T(8,128)S(1)} %collective-permute-done.14), channel_id=1, source_target_pairs={{2,3},{6,7},{10,11},{14,15},{18,19},{22,23},{26,27},{30,31}} | collective-permute-start | bytes 786440 | tf_op jit(solution)/shard_map/ppermute | solution.py:231
  119.3 54.5 %collective-permute-start.51 = (f32[2,2,32,640]{3,2,1,0:T(8,128)}, f32[2,2,32,640]{3,2,1,0:T(8,128)}, u32[]{:S(2)}, u32[]{:S(2)}) collective-permute-start(f32[2,2,32,640]{3,2,1,0:T(8,128)} %maximum_maximum_fusion.2), channel_id=1, source_target_pairs={{0,4},{4,0},{8,12},{12,8},{16,20},{20,16},{24,28},{28,24},{1,5},{5... | collective-permute-start | bytes 983048 | tf_op jit(solution)/shard_map/ppermute | solution.py:152
  119.3 36.5 %collective-permute-start.38 = (f32[256,256]{1,0:T(8,128)}, f32[256,256]{1,0:T(8,128)}, u32[]{:S(2)}, u32[]{:S(2)}) collective-permute-start(f32[256,256]{1,0:T(8,128)} %collective-permute-done.37), channel_id=1, source_target_pairs={{2,3},{6,7},{10,11},{14,15},{18,19},{22,23},{26,27},{30,31}} | collective-permute-start | bytes 786440 | tf_op jit(solution)/shard_map/ppermute | solution.py:231
  125.0 36.3 %collective-permute-start.35 = (f32[256,256]{1,0:T(8,128)}, f32[256,256]{1,0:T(8,128)}, u32[]{:S(2)}, u32[]{:S(2)}) collective-permute-start(f32[256,256]{1,0:T(8,128)} %collective-permute-done.34), channel_id=1, source_target_pairs={{2,3},{6,7},{10,11},{14,15},{18,19},{22,23},{26,27},{30,31}} | collective-permute-start | bytes 786440 | tf_op jit(solution)/shard_map/ppermute | solution.py:231
  130.6 33.5 %collective-permute-start.32 = (f32[256,256]{1,0:T(8,128)}, f32[256,256]{1,0:T(8,128)}, u32[]{:S(2)}, u32[]{:S(2)}) collective-permute-start(f32[256,256]{1,0:T(8,128)} %collective-permute-done.31), channel_id=1, source_target_pairs={{2,3},{6,7},{10,11},{14,15},{18,19},{22,23},{26,27},{30,31}} | collective-permute-start | bytes 786440 | tf_op jit(solution)/shard_map/ppermute | solution.py:231
  174.8 6.4 %collective-permute-start.22 = (f32[2,2,128,256]{2,1,0,3:T(2,128)}, f32[2,2,128,256]{2,1,0,3:T(2,128)}, u32[]{:S(2)}, u32[]{:S(2)}) collective-permute-start(f32[2,2,128,256]{2,1,0,3:T(2,128)} %bitcast.136), channel_id=1, source_target_pairs={{0,4},{4,0},{8,12},{12,8},{16,20},{20,16},{24,28},{28,24},{1,5},{5... | collective-permute-start | bytes 1572872 | tf_op jit(solution)/shard_map/ppermute | solution.py:152
  178.1 9.2 %collective-permute-start.42 = (f32[2,64,256]{1,0,2:T(2,128)S(1)}, f32[2,64,256]{1,0,2:T(2,128)S(1)}, u32[]{:S(2)}, u32[]{:S(2)}) collective-permute-start(f32[2,64,256]{1,0,2:T(2,128)S(1)} %dynamic-slice_bitcast_fusion.1), channel_id=1, source_target_pairs={{0,16},{4,20},{8,24},{12,28},{16,0},{20,4},{24,8},{28,12},{1,17},{... | collective-permute-start | bytes 393224 | tf_op jit(solution)/shard_map/ppermute | solution.py:152
  180.1 9.2 %collective-permute-start.40 = (f32[2,64,256]{1,0,2:T(2,128)S(1)}, f32[2,64,256]{1,0,2:T(2,128)S(1)}, u32[]{:S(2)}, u32[]{:S(2)}) collective-permute-start(f32[2,64,256]{1,0,2:T(2,128)S(1)} %bitcast.142), channel_id=1, source_target_pairs={{0,8},{4,12},{8,0},{12,4},{16,24},{20,28},{24,16},{28,20},{1,9},{5... | collective-permute-start | bytes 393224 | tf_op jit(solution)/shard_map/ppermute | solution.py:152
  183.3 9.7 %collective-permute-start.25 = (f32[2,64,256]{1,0,2:T(2,128)S(1)}, f32[2,64,256]{1,0,2:T(2,128)S(1)}, u32[]{:S(2)}, u32[]{:S(2)}) collective-permute-start(f32[2,64,256]{1,0,2:T(2,128)S(1)} %dynamic-slice_bitcast_fusion.2), channel_id=1, source_target_pairs={{0,16},{4,20},{8,24},{12,28},{16,0},{20,4},{24,8},{28,12},{1,17},{... | collective-permute-start | bytes 393224 | tf_op jit(solution)/shard_map/ppermute | solution.py:152
  185.1 9.9 %collective-permute-start.23 = (f32[2,64,256]{1,0,2:T(2,128)S(1)}, f32[2,64,256]{1,0,2:T(2,128)S(1)}, u32[]{:S(2)}, u32[]{:S(2)}) collective-permute-start(f32[2,64,256]{1,0,2:T(2,128)S(1)} %bitcast.141), channel_id=1, source_target_pairs={{0,8},{4,12},{8,0},{12,4},{16,24},{20,28},{24,16},{28,20},{1,9},{5... | collective-permute-start | bytes 393224 | tf_op jit(solution)/shard_map/ppermute | solution.py:152
  187.7 10.1 %collective-permute-start.43 = (f32[64,256]{0,1:T(8,128)S(1)}, f32[64,256]{0,1:T(8,128)S(1)}, u32[]{:S(2)}, u32[]{:S(2)}) collective-permute-start(f32[64,256]{0,1:T(8,128)S(1)} %bitcast.143), channel_id=1, source_target_pairs={{0,8},{4,12},{8,0},{12,4},{16,24},{20,28},{24,16},{28,20},{1,9},{5... | collective-permute-start | bytes 196616 | tf_op jit(solution)/shard_map/ppermute | solution.py:152
  189.7 8.1 %collective-permute-start.41 = (f32[64,256]{0,1:T(8,128)S(1)}, f32[64,256]{0,1:T(8,128)S(1)}, u32[]{:S(2)}, u32[]{:S(2)}) collective-permute-start(f32[64,256]{0,1:T(8,128)S(1)} %bitcast.144), channel_id=1, source_target_pairs={{0,16},{4,20},{8,24},{12,28},{16,0},{20,4},{24,8},{28,12},{1,17},{... | collective-permute-start | bytes 196616 | tf_op jit(solution)/shard_map/ppermute | solution.py:152
  193.3 6.1 %collective-permute-start.26 = (f32[64,256]{0,1:T(8,128)S(1)}, f32[64,256]{0,1:T(8,128)S(1)}, u32[]{:S(2)}, u32[]{:S(2)}) collective-permute-start(f32[64,256]{0,1:T(8,128)S(1)} %bitcast.145), channel_id=1, source_target_pairs={{0,8},{4,12},{8,0},{12,4},{16,24},{20,28},{24,16},{28,20},{1,9},{5... | collective-permute-start | bytes 196616 | tf_op jit(solution)/shard_map/ppermute | solution.py:152
  195.4 5.0 %collective-permute-start.24 = (f32[64,256]{0,1:T(8,128)S(1)}, f32[64,256]{0,1:T(8,128)S(1)}, u32[]{:S(2)}, u32[]{:S(2)}) collective-permute-start(f32[64,256]{0,1:T(8,128)S(1)} %bitcast.146), channel_id=1, source_target_pairs={{0,16},{4,20},{8,24},{12,28},{16,0},{20,4},{24,8},{28,12},{1,17},{... | collective-permute-start | bytes 196616 | tf_op jit(solution)/shard_map/ppermute | solution.py:152
  (33 other events, 308.2 us)

commit v2 on v1

v2 whole, which is shorter than its diff:
```python
import functools

import jax
import jax.numpy as jnp
from jax import lax
from jax.experimental import pallas as pl
from jax.experimental.pallas import tpu as pltpu
from jax.sharding import PartitionSpec as P


BLOCK = 128
SUB = 8


def high(left, right, dims):
    return lax.dot_general(
        left, right, (dims, ((), ())), precision=lax.Precision.HIGH, preferred_element_type=jnp.float32
    )


def full(left, right, dims):
    return lax.dot_general(
        left, right, (dims, ((), ())), precision=lax.Precision.HIGHEST, preferred_element_type=jnp.float32
    )


def eliminate(tiles):
    count, size = len(tiles), tiles[0].shape[1]
    lane = lax.broadcasted_iota(jnp.int32, (SUB, size), 1)
    sub = lax.broadcasted_iota(jnp.int32, (SUB, size), 0)

    def lanes(x, c):
        return jnp.broadcast_to(x[:, c : c + 1], (SUB, size))

    def subs(x, q):
        return jnp.broadcast_to(x[q : q + 1, :], (SUB, size))

    scaled, scales = [], []
    for at in range(count):
        low = SUB * at
        rows = tiles[at]
        cols = [lanes(rows, low + q) for q in range(SUB)]
        inverse, upper, pivots = [], {}, None
        for q in range(SUB):
            pivot = subs(cols[q], q)
            pivots = pivot if pivots is None else jnp.where(sub == q, pivot, pivots)
            inverse.append(1.0 / pivot)
            times = jnp.where(sub > q, cols[q] * inverse[q], 0.0)
            for p in range(q + 1, SUB):
                upper[q, p] = subs(cols[q], p)
                cols[p] = cols[p] - times * upper[q, p]
            pivot_row = jnp.where(lane == low + q, 1.0, subs(rows, q))
            rows = jnp.where((lane == low + q) & (sub > q), 0.0, rows) - times * pivot_row
        pivot_rows = []
        for q in range(SUB):
            row = jnp.where(lane == low + q, 1.0, subs(rows, q))
            pivot_rows.append(jnp.where((lane > low + q) & (lane < low + SUB), 0.0, row))
        own = (lane >= low) & (lane < low + SUB)
        for other in range(at + 1, count):
            tile = tiles[other]
            theirs = [lanes(tile, low + q) for q in range(SUB)]
            tile = jnp.where(own, 0.0, tile)
            times = []
            for q in range(SUB):
                value = theirs[q]
                for p in range(q):
                    value = value - times[p] * upper[p, q]
                value = value * inverse[q]
                times.append(value)
                tile = tile - value * pivot_rows[q]
            tiles[other] = tile
        scale = lax.rsqrt(pivots)
        scales.append(scale)
        scaled.append(rows * scale)
    return scaled, scales


def vmem(count):
    return [pl.BlockSpec(memory_space=pltpu.VMEM)] * count


SMEM = pl.BlockSpec(memory_space=pltpu.SMEM)


def shape(*sizes):
    return jax.ShapeDtypeStruct(sizes, jnp.float32)


def strips(nb):
    for i in range(nb // 2):
        yield i, nb - 1 - i, 0
        yield i, i, (nb - i) * BLOCK


def pack_kernel(core_ref, corner_ref, keep_a_ref, keep_b_ref, send_ref, rect_ref):
    nb = corner_ref.shape[0] // BLOCK
    for i, block, low in strips(nb):
        wide = (block + 1) * BLOCK
        rect_ref[i * BLOCK : (i + 1) * BLOCK, low : low + wide] = corner_ref[
            block * BLOCK : (block + 1) * BLOCK, :wide
        ]
    half = rect_ref.shape[0] // 2
    core = core_ref[0]
    mine = pl.multiple_of(core * half, half)
    theirs = pl.multiple_of((1 - core) * half, half)
    keep_a_ref[...] = rect_ref[pl.ds(mine, half // 2), :]
    keep_b_ref[...] = rect_ref[pl.ds(mine + half // 2, half // 2), :]
    send_ref[...] = rect_ref[pl.ds(theirs, half), :]


def pack(core, corner):
    nb = corner.shape[0] // BLOCK
    tall, wide = nb // 2 * BLOCK, (nb + 1) * BLOCK
    return pl.pallas_call(
        pack_kernel,
        out_shape=(shape(tall // 4, wide), shape(tall // 4, wide), shape(tall // 2, wide)),
        in_specs=[SMEM] + vmem(1),
        out_specs=tuple(vmem(3)),
        scratch_shapes=[pltpu.VMEM((tall, wide), jnp.float32)],
        cost_estimate=pl.CostEstimate(flops=0, bytes_accessed=8 * tall * wide, transcendentals=0),
    )(core, corner)


def factor_kernel(place_ref, own_a, own_b, other_a, other_b, diag_ref, l_ref, piece_ref, w_ref, rect_ref, base_ref, scale_ref):
    size = w_ref.shape[0]
    nb = size // BLOCK
    plane, me = place_ref[0], place_ref[1]

    @pl.when(plane == 0)
    def _():
        half = rect_ref.shape[0] // 2
        quarter = half // 2
        core = me & 1
        mine = pl.multiple_of(core * half, half)
        theirs = pl.multiple_of((1 - core) * half, half)
        rect_ref[pl.ds(mine, quarter), :] = own_a[...]
        rect_ref[pl.ds(mine + quarter, quarter), :] = own_b[...]
        rect_ref[pl.ds(theirs, quarter), :] = other_a[...]
        rect_ref[pl.ds(theirs + quarter, quarter), :] = other_b[...]
        row = lax.broadcasted_iota(jnp.int32, (BLOCK, BLOCK), 0)
        col = lax.broadcasted_iota(jnp.int32, (BLOCK, BLOCK), 1)
        for i, block, low in strips(nb):
            here = slice(block * BLOCK, (block + 1) * BLOCK)
            for k in range(block + 1):
                there = slice(k * BLOCK, (k + 1) * BLOCK)
                part = rect_ref[i * BLOCK : (i + 1) * BLOCK, low + k * BLOCK : low + (k + 1) * BLOCK]
                if k == block:
                    part = jnp.where(col <= row, part, part.T)
                    part = part + jnp.where(col == row, diag_ref[:, here], 0.0)
                else:
                    w_ref[there, here] = part.T
                w_ref[here, there] = part

        def step(j, carry):
            low = pl.multiple_of(j * BLOCK, BLOCK)
            mine = pl.ds(low, BLOCK)
            tiles = [w_ref[pl.ds(low + SUB * t, SUB), mine] for t in range(BLOCK // SUB)]
            scaled, scales = eliminate(tiles)
            for t in range(BLOCK // SUB):
                base_ref[SUB * t : SUB * t + SUB, :] = scaled[t]
                scale_ref[SUB * t : SUB * t + SUB, :] = scales[t]
            both = base_ref[...]
            inverse = jnp.where(col < row, both, jnp.where(col == row, scale_ref[...], 0.0))
            factor_t = jnp.where(col >= row, both, 0.0)
            below = lax.broadcasted_iota(jnp.int32, (size, BLOCK), 0) >= low + BLOCK
            panel = jnp.where(below, full(w_ref[:, mine], inverse, ((1,), (1,))), 0.0)
            w_ref[mine, :] = full(inverse, w_ref[mine, :], ((1,), (0,)))
            w_ref[mine, mine] = inverse
            pivot_rows = w_ref[mine, :]
            w_ref[:, mine] = jnp.where(below, 0.0, w_ref[:, mine])
            w_ref[...] = w_ref[...] - full(panel, pivot_rows, ((1,), (0,)))
            l_ref[:, mine] = panel
            l_ref[mine, mine] = factor_t.T
            return carry

        lax.fori_loop(0, nb, step, 0)
        for i, block, low in strips(nb):
            for k in range(block + 1):
                rect_ref[i * BLOCK : (i + 1) * BLOCK, low + k * BLOCK : low + (k + 1) * BLOCK] = w_ref[
                    block * BLOCK : (block + 1) * BLOCK, k * BLOCK : (k + 1) * BLOCK
                ]
        each = piece_ref.shape[0]
        piece_ref[...] = rect_ref[pl.ds(pl.multiple_of(me * each, each), each), :]


def factor(place, parts, diag, each):
    size = diag.shape[1]
    nb = size // BLOCK
    tall, wide = nb // 2 * BLOCK, (nb + 1) * BLOCK
    return pl.pallas_call(
        factor_kernel,
        out_shape=(shape(size, size), shape(each, wide)),
        in_specs=[SMEM] + vmem(5),
        out_specs=tuple(vmem(2)),
        scratch_shapes=[
            pltpu.VMEM((size, size), jnp.float32),
            pltpu.VMEM((tall, wide), jnp.float32),
            pltpu.VMEM((BLOCK, BLOCK), jnp.float32),
            pltpu.VMEM((BLOCK, BLOCK), jnp.float32),
        ],
        cost_estimate=pl.CostEstimate(flops=20 * size**3, bytes_accessed=12 * size * size, transcendentals=size),
    )(place, *parts, diag)


def last_kernel(count, place_ref, *refs):
    pieces, (keep_a, got_a, keep_b, got_b, l_ref, out_ref, rect_ref, rows_ref) = refs[:count], refs[count:]
    me, first = place_ref[1], place_ref[2]
    rows, width = out_ref.shape
    nb = width // BLOCK
    each = pieces[0].shape[0]
    half = rows // 2
    rows_ref[:half, :] = keep_a[...] + got_a[...]
    rows_ref[half:, :] = keep_b[...] + got_b[...]
    for m in range(count):
        rect_ref[pl.ds(pl.multiple_of((me ^ m) * each, each), each), :] = pieces[m][...]
    for i, block, low in strips(nb):
        wide = (block + 1) * BLOCK
        part = rect_ref[i * BLOCK : (i + 1) * BLOCK, low : low + wide]
        part = jnp.concatenate(
            [part[:, : wide - BLOCK], jnp.where(
                lax.broadcasted_iota(jnp.int32, (BLOCK, BLOCK), 1) <= lax.broadcasted_iota(jnp.int32, (BLOCK, BLOCK), 0),
                part[:, wide - BLOCK :], 0.0)], axis=1) if wide > BLOCK else part
        out_ref[:, block * BLOCK : (block + 1) * BLOCK] = full(rows_ref[:, :wide], part, ((1,), (1,)))

    @pl.when(first < width)
    def _():
        out_ref[...] = l_ref[pl.ds(pl.multiple_of(first, rows), rows), :]


def last(place, pieces, sums, lower, rows):
    width = lower.shape[0]
    nb = width // BLOCK
    tall, wide = nb // 2 * BLOCK, (nb + 1) * BLOCK
    return pl.pallas_call(
        functools.partial(last_kernel, len(pieces)),
        out_shape=shape(rows, width),
        in_specs=[SMEM] + vmem(len(pieces) + 5),
        out_specs=vmem(1)[0],
        scratch_shapes=[pltpu.VMEM((tall, wide), jnp.float32), pltpu.VMEM((rows, width), jnp.float32)],
        cost_estimate=pl.CostEstimate(flops=6 * rows * width * width, bytes_accessed=8 * width * width, transcendentals=0),
    )(place, *pieces, *sums, lower)


def hop(x, source, target):
    return lax.ppermute(x, "col", [(source, target)])


def exchange(x, mask, count):
    return lax.ppermute(x, "scen", [(i, i ^ mask) for i in range(count)])


def orders(count):
    bits = count.bit_length() - 1
    split = 1 + bits // 2
    return bits, list(range(1, split)), list(range(split, bits))


def halve(x, names, bit, count):
    axis = names.index(bit)
    mine = (lax.axis_index("scen") >> bit) & 1
    keep = lax.dynamic_index_in_dim(x, mine, axis, keepdims=False)
    send = lax.dynamic_index_in_dim(x, 1 - mine, axis, keepdims=False)
    return keep, exchange(send, 1 << bit, count), [n for n in names if n != bit]


def scatter_sum(x):
    count = lax.axis_size("scen")
    bits, first, second = orders(count)
    rows = x.shape[0] // count
    x = x.reshape((2,) * bits + (rows,) + x.shape[1:])
    keep, got, names = halve(x, list(range(bits - 1, -1, -1)), 0, count)
    x = keep + got
    lead = (slice(None),) * len(names)
    parts = [x[lead + (slice(0, rows // 2),)], x[lead + (slice(rows // 2, rows),)]]
    lists, pairs = [names, names], [None, None]
    for a, b in zip(first + second, second + first):
        for i, bit in ((0, a), (1, b)):
            if pairs[i] is not None:
                parts[i] = pairs[i][0] + pairs[i][1]
            keep, got, lists[i] = halve(parts[i], lists[i], bit, count)
            pairs[i] = (keep, got)
    return pairs[0] + pairs[1]


PIECES = 8
HEAD = 2
LATE = 2


def bounds(depth):
    units = depth // SUB
    return [units * k // PIECES * SUB for k in range(PIECES + 1)]


def program(inverses, coupling, tile_mask, hess_diag):
    local = coupling[0]
    width = hess_diag.shape[0]
    scen, planes = lax.axis_size("scen"), lax.axis_size("col")
    me, plane = lax.axis_index("scen").astype(jnp.int32), lax.axis_index("col").astype(jnp.int32)
    rows = local.shape[1] // scen
    first = plane * local.shape[1] + me * rows
    place = jnp.stack([plane, me, first])
    depth = local.shape[0]
    keep = jnp.repeat(tile_mask[0].astype(jnp.float32), depth // tile_mask.shape[1])
    masked_inverse = inverses[0] * keep[:, None] * keep[None, :]
    panel = local[:, :width]
    edge = bounds(depth)

    cut = edge[HEAD]
    head = high(masked_inverse[:cut], panel, ((1,), (0,)))
    tail = high(masked_inverse[cut:], panel, ((1,), (0,)))

    heads = lax.optimization_barrier(tuple(head[edge[k] : edge[k + 1]] for k in range(HEAD)))
    tails = lax.optimization_barrier(tuple(tail[edge[k] - cut : edge[k + 1] - cut] for k in range(HEAD, PIECES)))
    arrived = []
    for k in range(PIECES):
        piece = (heads + tails)[k]
        mine = jnp.where(plane == 0, piece, 0.0)
        for h in range(planes - 1):
            piece = hop(piece, h, h + 1)
            mine = mine + piece
        arrived.append(mine)

    corner = high(panel[:cut], head, ((0,), (0,))) + high(panel[cut:], tail, ((0,), (0,)))
    keep_a, keep_b, send = pack((me & 1).reshape(1), corner)
    got = exchange(send, 1, scen)
    a, b = keep_a + got[: got.shape[0] // 2], keep_b + got[got.shape[0] // 2 :]
    _, near, far = orders(scen)
    for p, q in zip(near + far, far + near):
        got_a = exchange(a, 1 << p, scen)
        got_b = exchange(b, 1 << q, scen)
        a, b = a + got_a, b + got_b
    parts = (a, b, exchange(a, 1, scen), exchange(b, 1, scen))
    each = width // BLOCK // 2 * BLOCK // scen
    lower, piece = factor(place, parts, hess_diag[None, :], each)

    mine = jnp.where(plane == 0, piece, 0.0)
    for h in range(1, planes):
        mine = mine + hop(piece, 0, h)
    pieces = [mine if m == 0 else exchange(mine, m, scen) for m in range(0, scen, 2)]
    pieces = [p for m in range(0, scen, 2) for p in (pieces[m // 2], exchange(pieces[m // 2], 1, scen))]

    early = edge[PIECES - LATE]
    top = jnp.concatenate(arrived[: PIECES - LATE], axis=0)
    bottom = jnp.concatenate(arrived[PIECES - LATE :], axis=0)
    total = high(local[:early], top, ((0,), (0,)))
    total = total + high(local[early:], bottom, ((0,), (0,)))
    return last(place, pieces, scatter_sum(total), lower, rows)


def solution(mesh):
    in_specs = (P("scen", None, None), P("scen", None, "col"), P("scen", None), P())
    out_specs = P(("col", "scen"), None)
    return jax.shard_map(program, mesh=mesh, in_specs=in_specs, out_specs=out_specs, check_vma=False)
```

time: 204 us -> 165 us (0.81)
  the two profiles are of different devices: /device:TPU:24 before, /device:TPU:0 now
where the time goes in v2:
time: 165 us; the launch traced here: 164 us
  starting transfers between devices  61.1 us (37%)
  Pallas kernels  31.7 us (19%)
  waiting for transfers between devices  29.4 us (18%)
  local copies, waits for them, and re-layouts  16.2 us (10%)
  matrix products  14.5 us (9%)
  other arithmetic  10.6 us (6%)
    ppermute x27, starting transfers between devices, hop(): return lax.ppermute(x, 'col', [(source, target)])  45.5 us
    pallas_call x1, Pallas kernels, factor(): pl.pallas_call(factor_kernel, out_shape=(shape(size, size), shape(each, w...  26.3 us
    ppermute x19, waiting for transfers between devices, exchange(): return lax.ppermute(x, 'scen', [(i, i ^ mask) for i in range(count)])  18.2 us
    ppermute x19, starting transfers between devices, exchange(): return lax.ppermute(x, 'scen', [(i, i ^ mask) for i in range(count)])  15.5 us
    dot_general x6, matrix products, high(): lax.dot_general(left, right, (dims, ((), ())), precision=lax.Precision.HI...  14.5 us
    ppermute x27, waiting for transfers between devices, hop(): return lax.ppermute(x, 'col', [(source, target)])  11.2 us
    unnamed x38, local copies, waits for them, and re-layouts  5.75 us
    dynamic_slice x1, local copies, waits for them, and re-layouts, halve(): keep = lax.dynamic_index_in_dim(x, mine, axis, keepdims=False)  4.38 us
  transfers between devices with their start and end apart: 46, of which 17 were waited for; matrix products, arithmetic and copies ran while one was open for 20% of the time, Pallas kernels for 17%

profile of v2, /device:TPU:0, one launch (start us, length us, event | category | flops | bytes accessed | tf_op | source)
XLA Modules:
  0.0 164.3 jit_solution(17298800695709532897)
XLA Ops:
  0.7 2.7 %fusion = f32[1024,1024]{1,0:T(8,128)S(1)} fusion(f32[1,1024,1024]{2,1,0:T(8,128)} %param.4, f32[1024]{0:T(1024)S(1)} %broadcast_bitcast_fusion), kind=kLoop, calls=%fused_computation.1 | loop fusion | flops 2097152 | bytes 8392704 | tf_op jit(solution)/shard_map/mul | solution.py:305
  4.2 2.6 %fusion.1 = f32[768,512]{1,0:T(8,128)S(1)} fusion(f32[1024,1024]{1,0:T(8,128)S(1)} %fusion, f32[1024,1024]{1,0:T(8,128)S(1)} %bitcast.52), kind=kOutput, calls=%fused_computation.2 | convolution fusion | flops 2415919104 | bytes 6815744 | tf_op jit(solution)/shard_map/dot_general | solution.py:16
  7.7 5.6 %collective-permute-start.35 = (f32[128,512]{1,0:T(8,128)}, f32[128,512]{1,0:T(8,128)}, u32[]{:S(2)}, u32[]{:S(2)}) collective-permute-start(f32[128,512]{1,0:T(8,128)} %get-tuple-element.28), channel_id=1, source_target_pairs={{0,1},{4,5},{8,9},{12,13},{16,17},{20,21},{24,25},{28,29}} | collective-permute-start | bytes 786440 | tf_op jit(solution)/shard_map/ppermute | solution.py:245
  13.4 2.0 %collective-permute-start.38 = (f32[128,512]{1,0:T(8,128)S(1)}, f32[128,512]{1,0:T(8,128)}, u32[]{:S(2)}, u32[]{:S(2)}) collective-permute-start(f32[128,512]{1,0:T(8,128)S(1)} %get-tuple-element.29), channel_id=1, source_target_pairs={{0,1},{4,5},{8,9},{12,13},{16,17},{20,21},{24,25},{28,29}} | collective-permute-start | bytes 786440 | tf_op jit(solution)/shard_map/ppermute | solution.py:245
  17.3 2.0 %collective-permute-start.17 = (f32[128,512]{1,0:T(8,128)}, f32[128,512]{1,0:T(8,128)}, u32[]{:S(2)}, u32[]{:S(2)}) collective-permute-start(f32[128,512]{1,0:T(8,128)} %get-tuple-element.22), channel_id=1, source_target_pairs={{0,1},{4,5},{8,9},{12,13},{16,17},{20,21},{24,25},{28,29}} | collective-permute-start | bytes 786440 | tf_op jit(solution)/shard_map/ppermute | solution.py:245
  19.3 2.0 %collective-permute-start.20 = (f32[128,512]{1,0:T(8,128)}, f32[128,512]{1,0:T(8,128)}, u32[]{:S(2)}, u32[]{:S(2)}) collective-permute-start(f32[128,512]{1,0:T(8,128)} %get-tuple-element.23), channel_id=1, source_target_pairs={{0,1},{4,5},{8,9},{12,13},{16,17},{20,21},{24,25},{28,29}} | collective-permute-start | bytes 786440 | tf_op jit(solution)/shard_map/ppermute | solution.py:245
  21.3 2.0 %collective-permute-start.23 = (f32[128,512]{1,0:T(8,128)S(1)}, f32[128,512]{1,0:T(8,128)}, u32[]{:S(2)}, u32[]{:S(2)}) collective-permute-start(f32[128,512]{1,0:T(8,128)S(1)} %get-tuple-element.24), channel_id=1, source_target_pairs={{0,1},{4,5},{8,9},{12,13},{16,17},{20,21},{24,25},{28,29}} | collective-permute-start | bytes 786440 | tf_op jit(solution)/shard_map/ppermute | solution.py:245
  26.5 1.7 %fusion.23 = f32[512,512]{0,1:T(8,128)S(1)} fusion(f32[256,512]{1,0:T(8,128)S(1)} %fusion.7, f32[1024,1024]{1,0:T(8,128)} %bitcast.50), kind=kOutput, calls=%fused_computation.20 | convolution fusion | flops 402653184 | bytes 2097152 | tf_op jit(solution)/shard_map/dot_general | solution.py:16
  28.2 2.7 %collective-permute-done.17 = f32[128,512]{1,0:T(8,128)} collective-permute-done((f32[128,512]{1,0:T(8,128)}, f32[128,512]{1,0:T(8,128)}, u32[]{:S(2)}, u32[]{:S(2)}) %collective-permute-start.17) | collective-permute-done | bytes 262176 | tf_op jit(solution)/shard_map/ppermute | solution.py:245
  30.9 4.4 %collective-permute-start.26 = (f32[128,512]{1,0:T(8,128)S(1)}, f32[128,512]{1,0:T(8,128)S(1)}, u32[]{:S(2)}, u32[]{:S(2)}) collective-permute-start(f32[128,512]{1,0:T(8,128)S(1)} %get-tuple-element.25), channel_id=1, source_target_pairs={{0,1},{4,5},{8,9},{12,13},{16,17},{20,21},{24,25},{28,29}} | collective-permute-start | bytes 786440 | tf_op jit(solution)/shard_map/ppermute | solution.py:245
  37.4 3.9 %fusion.16.corner_ref = f32[512,512]{1,0:T(8,128)} fusion(f32[512,512]{0,1:T(8,128)S(1)} %fusion.23, f32[768,512]{1,0:T(8,128)S(1)} %fusion.1, f32[1024,1024]{1,0:T(8,128)} %bitcast.51), kind=kOutput, calls=%fused_computation.14 | convolution fusion | flops 1208221696 | bytes 5242880 | tf_op jit(solution)/shard_map/dot_general | solution.py:16
  41.3 2.2 %shard_map.46 = (f32[64,640]{1,0:T(8,128)}, f32[64,640]{1,0:T(8,128)}, f32[128,640]{1,0:T(8,128)}) custom-call(s32[1]{0:T(128)} %bitcast.3.core_ref, f32[512,512]{1,0:T(8,128)} %fusion.16.corner_ref), custom_call_target="tpu_custom_call" | custom-call | bytes 1310720 | tf_op jit(solution)/shard_map/pallas_call | solution.py:114
  44.8 1.8 %collective-permute-start.32 = (f32[128,512]{1,0:T(8,128)S(1)}, f32[128,512]{1,0:T(8,128)S(1)}, u32[]{:S(2)}, u32[]{:S(2)}) collective-permute-start(f32[128,512]{1,0:T(8,128)S(1)} %get-tuple-element.27), channel_id=1, source_target_pairs={{0,1},{4,5},{8,9},{12,13},{16,17},{20,21},{24,25},{28,29}} | collective-permute-start | bytes 786440 | tf_op jit(solution)/shard_map/ppermute | solution.py:245
  53.9 3.8 %collective-permute-done.32 = f32[128,512]{1,0:T(8,128)S(1)} collective-permute-done((f32[128,512]{1,0:T(8,128)S(1)}, f32[128,512]{1,0:T(8,128)S(1)}, u32[]{:S(2)}, u32[]{:S(2)}) %collective-permute-start.32) | collective-permute-done | bytes 262176 | tf_op jit(solution)/shard_map/ppermute | solution.py:245
  60.5 2.3 %fusion.20 = f32[512,1024]{1,0:T(8,128)S(1)} fusion(f32[1,1024,1024]{2,1,0:T(8,128)} %param.5, f32[128,512]{1,0:T(8,128)S(1)} %add_add_fusion, f32[128,512]{1,0:T(8,128)S(1)} %add_add_fusion.1), kind=kOutput, calls=%fused_computation.17 | convolution fusion | flops 805437440 | bytes 3670016 | tf_op jit(solution)/shard_map/dot_general | solution.py:16
  70.4 3.0 %add_bitcast_fusion = f32[1024,512]{0,1:T(8,128)S(1)} fusion(f32[512,1024]{1,0:T(8,128)S(1)} %fusion.20, f32[768,512]{1,0:T(8,128)S(1)} %add_dynamic-update-slice_fusion, f32[1,1024,1024]{2,1,0:T(8,128)S(1)} %copy-done.1), kind=kOutput, calls=%fused_computation.7 | convolution fusion | flops 2416443392 | bytes 8912896 | tf_op jit(solution)/shard_map/dot_general | solution.py:16
  73.4 2.8 %reshape.12 = f32[2,2,2,128,512]{3,2,1,0,4:T(2,128)} reshape(f32[1024,512]{0,1:T(8,128)S(1)} %add_bitcast_fusion) | data formatting | bytes 4194304 | tf_op jit(solution)/shard_map/reshape | solution.py:270
  76.1 4.4 %constant_dynamic-slice_fusion.1 = (f32[2,2,1,128,512]{3,2,1,0,4:T(1,128)S(1)}, f32[2,2,1,128,512]{3,2,1,0,4:T(1,128)S(1)}) fusion(f32[2,2,2,128,512]{3,2,1,0,4:T(2,128)} %reshape.12, s32[]{:T(128)S(6)} %select_n.81, s32[]{:T(128)S(6)} %select_n.82), kind=kLoop, calls=%fused_computation.45 | loop fusion | bytes 4194312 | tf_op jit(solution)/shard_map/jit(dynamic_index_in_dim)/dynamic_slice | solution.py:261
  80.5 2.4 %copy.14 = f32[2,2,1,128,512]{4,3,1,0,2:T(8,128)} copy(f32[2,2,1,128,512]{3,2,1,0,4:T(1,128)S(1)} %get-tuple-element.32) | data formatting | bytes 2097152
  83.5 1.6 collective-permute-start.3
  86.6 3.1 %collective-permute-done.3 = f32[64,640]{1,0:T(8,128)S(1)} collective-permute-done((f32[64,640]{1,0:T(8,128)S(1)}, f32[64,640]{1,0:T(8,128)S(1)}, u32[]{:S(2)}, u32[]{:S(2)}) %collective-permute-start.3) | collective-permute-done | bytes 163872 | tf_op jit(solution)/shard_map/ppermute | solution.py:249
  89.7 1.6 collective-permute-start.4
  91.3 1.6 collective-permute-start.2
  92.9 2.2 %collective-permute-done.4 = f32[64,640]{1,0:T(8,128)S(1)} collective-permute-done((f32[64,640]{1,0:T(8,128)S(1)}, f32[64,640]{1,0:T(8,128)S(1)}, u32[]{:S(2)}, u32[]{:S(2)}) %collective-permute-start.4) | collective-permute-done | bytes 163872 | tf_op jit(solution)/shard_map/ppermute | solution.py:249
  98.8 26.3 %shard_map.47 = (f32[512,512]{1,0:T(8,128)}, f32[32,640]{1,0:T(8,128)}) custom-call(s32[3]{0:T(128)} %pad_add_fusion.place_ref, f32[64,640]{1,0:T(8,128)} %copy-done.4, f32[64,640]{1,0:T(8,128)} %copy-done.3, f32[64,640]{1,0:T(8,128)} %collective-permute-done.5.other_a, f32[64,640]{1,0:T(8,128)} %collective-permute-done.6.other_b, f32[1,512]{1,0:T(1,128)} %bitcast.54), custom_call_target="tpu_custom_call" | custom-call | flops 2684354560 | bytes 3145728 | tf_op jit(solution)/shard_map/pallas_call | solution.py:190
  125.0 8.8 %collective-permute-start.9 = (f32[32,640]{1,0:T(8,128)}, f32[32,640]{1,0:T(8,128)S(1)}, u32[]{:S(2)}, u32[]{:S(2)}) collective-permute-start(f32[32,640]{1,0:T(8,128)} %get-tuple-element.21), channel_id=1, source_target_pairs={{0,3},{4,7},{8,11},{12,15},{16,19},{20,23},{24,27},{28,31}} | collective-permute-start | bytes 245768 | tf_op jit(solution)/shard_map/ppermute | solution.py:245
  140.0 1.6 collective-permute-start.15
  143.6 2.5 %collective-permute-done.42 = f32[2,64,512]{2,1,0:T(8,128)S(1)} collective-permute-done((f32[2,64,512]{2,1,0:T(8,128)S(1)}, f32[2,64,512]{2,1,0:T(8,128)S(1)}, u32[]{:S(2)}, u32[]{:S(2)}) %collective-permute-start.42) | collective-permute-done | bytes 262176 | tf_op jit(solution)/shard_map/ppermute | solution.py:249
  146.0 1.5 collective-permute-start.44
  148.3 5.3 %collective-permute-done.44 = f32[2,64,512]{2,1,0:T(8,128)S(1)} collective-permute-done((f32[2,64,512]{2,1,0:T(8,128)S(1)}, f32[2,64,512]{2,1,0:T(8,128)S(1)}, u32[]{:S(2)}, u32[]{:S(2)}) %collective-permute-start.44) | collective-permute-done | bytes 262176 | tf_op jit(solution)/shard_map/ppermute | solution.py:249
  158.6 1.7 %collective-permute-done.45.refs_11_ = f32[64,512]{1,0:T(8,128)S(1)} collective-permute-done((f32[64,512]{1,0:T(8,128)S(1)}, f32[64,512]{1,0:T(8,128)S(1)}, u32[]{:S(2)}, u32[]{:S(2)}) %collective-permute-start.45) | collective-permute-done | bytes 131104 | tf_op jit(solution)/shard_map/ppermute | solution.py:249
  161.0 3.3 %shard_map.48 = f32[128,512]{1,0:T(8,128)} custom-call(s32[3]{0:T(128)} %pad_add_fusion.place_ref, f32[32,640]{1,0:T(8,128)} %copy-done.2, f32[32,640]{1,0:T(8,128)} %copy-done.12, f32[32,640]{1,0:T(8,128)} %copy-done.11, f32[32,640]{1,0:T(8,128)} %copy-done.15, f32[32,640]{1,0:T(8,128)} %copy-done.10, f32[32,640]{1,0:T(8,128)} %copy-done.14, ...), custom_call_target="tpu_custom_call" | custom-call | flops 201326592 | bytes 2097152 | tf_op jit(solution)/shard_map/pallas_call | solution.py:234
  (137 shorter events, 48.4 us)
Async XLA Ops:
  7.7 15.6 %collective-permute-start.35 = (f32[128,512]{1,0:T(8,128)}, f32[128,512]{1,0:T(8,128)}, u32[]{:S(2)}, u32[]{:S(2)}) collective-permute-start(f32[128,512]{1,0:T(8,128)} %get-tuple-element.28), channel_id=1, source_target_pairs={{0,1},{4,5},{8,9},{12,13},{16,17},{20,21},{24,25},{28,29}} | collective-permute-start | bytes 786440 | tf_op jit(solution)/shard_map/ppermute | solution.py:245
  13.4 11.8 %collective-permute-start.38 = (f32[128,512]{1,0:T(8,128)S(1)}, f32[128,512]{1,0:T(8,128)}, u32[]{:S(2)}, u32[]{:S(2)}) collective-permute-start(f32[128,512]{1,0:T(8,128)S(1)} %get-tuple-element.29), channel_id=1, source_target_pairs={{0,1},{4,5},{8,9},{12,13},{16,17},{20,21},{24,25},{28,29}} | collective-permute-start | bytes 786440 | tf_op jit(solution)/shard_map/ppermute | solution.py:245
  17.3 13.6 %collective-permute-start.17 = (f32[128,512]{1,0:T(8,128)}, f32[128,512]{1,0:T(8,128)}, u32[]{:S(2)}, u32[]{:S(2)}) collective-permute-start(f32[128,512]{1,0:T(8,128)} %get-tuple-element.22), channel_id=1, source_target_pairs={{0,1},{4,5},{8,9},{12,13},{16,17},{20,21},{24,25},{28,29}} | collective-permute-start | bytes 786440 | tf_op jit(solution)/shard_map/ppermute | solution.py:245
  19.3 24.2 %collective-permute-start.20 = (f32[128,512]{1,0:T(8,128)}, f32[128,512]{1,0:T(8,128)}, u32[]{:S(2)}, u32[]{:S(2)}) collective-permute-start(f32[128,512]{1,0:T(8,128)} %get-tuple-element.23), channel_id=1, source_target_pairs={{0,1},{4,5},{8,9},{12,13},{16,17},{20,21},{24,25},{28,29}} | collective-permute-start | bytes 786440 | tf_op jit(solution)/shard_map/ppermute | solution.py:245
  21.3 23.5 %collective-permute-start.23 = (f32[128,512]{1,0:T(8,128)S(1)}, f32[128,512]{1,0:T(8,128)}, u32[]{:S(2)}, u32[]{:S(2)}) collective-permute-start(f32[128,512]{1,0:T(8,128)S(1)} %get-tuple-element.24), channel_id=1, source_target_pairs={{0,1},{4,5},{8,9},{12,13},{16,17},{20,21},{24,25},{28,29}} | collective-permute-start | bytes 786440 | tf_op jit(solution)/shard_map/ppermute | solution.py:245
  23.3 12.0 %collective-permute-start.36 = (f32[128,512]{1,0:T(8,128)}, f32[128,512]{1,0:T(8,128)}, u32[]{:S(2)}, u32[]{:S(2)}) collective-permute-start(f32[128,512]{1,0:T(8,128)} %collective-permute-done.35), channel_id=1, source_target_pairs={{1,2},{5,6},{9,10},{13,14},{17,18},{21,22},{25,26},{29,30}} | collective-permute-start | bytes 786440 | tf_op jit(solution)/shard_map/ppermute | solution.py:245
  25.2 10.8 %collective-permute-start.39 = (f32[128,512]{1,0:T(8,128)}, f32[128,512]{1,0:T(8,128)}, u32[]{:S(2)}, u32[]{:S(2)}) collective-permute-start(f32[128,512]{1,0:T(8,128)} %collective-permute-done.38), channel_id=1, source_target_pairs={{1,2},{5,6},{9,10},{13,14},{17,18},{21,22},{25,26},{29,30}} | collective-permute-start | bytes 786440 | tf_op jit(solution)/shard_map/ppermute | solution.py:245
  30.9 16.7 %collective-permute-start.26 = (f32[128,512]{1,0:T(8,128)S(1)}, f32[128,512]{1,0:T(8,128)S(1)}, u32[]{:S(2)}, u32[]{:S(2)}) collective-permute-start(f32[128,512]{1,0:T(8,128)S(1)} %get-tuple-element.25), channel_id=1, source_target_pairs={{0,1},{4,5},{8,9},{12,13},{16,17},{20,21},{24,25},{28,29}} | collective-permute-start | bytes 786440 | tf_op jit(solution)/shard_map/ppermute | solution.py:245
  35.3 13.0 %collective-permute-start.37 = (f32[128,512]{1,0:T(8,128)}, f32[128,512]{1,0:T(8,128)S(1)}, u32[]{:S(2)}, u32[]{:S(2)}) collective-permute-start(f32[128,512]{1,0:T(8,128)} %collective-permute-done.36), channel_id=1, source_target_pairs={{2,3},{6,7},{10,11},{14,15},{18,19},{22,23},{26,27},{30,31}} | collective-permute-start | bytes 786440 | tf_op jit(solution)/shard_map/ppermute | solution.py:245
  36.0 13.0 %collective-permute-start.40 = (f32[128,512]{1,0:T(8,128)}, f32[128,512]{1,0:T(8,128)}, u32[]{:S(2)}, u32[]{:S(2)}) collective-permute-start(f32[128,512]{1,0:T(8,128)} %collective-permute-done.39), channel_id=1, source_target_pairs={{2,3},{6,7},{10,11},{14,15},{18,19},{22,23},{26,27},{30,31}} | collective-permute-start | bytes 786440 | tf_op jit(solution)/shard_map/ppermute | solution.py:245
  43.4 9.8 %collective-permute-start.29 = (f32[128,512]{1,0:T(8,128)S(1)}, f32[128,512]{1,0:T(8,128)S(1)}, u32[]{:S(2)}, u32[]{:S(2)}) collective-permute-start(f32[128,512]{1,0:T(8,128)S(1)} %get-tuple-element.26), channel_id=1, source_target_pairs={{0,1},{4,5},{8,9},{12,13},{16,17},{20,21},{24,25},{28,29}} | collective-permute-start | bytes 786440 | tf_op jit(solution)/shard_map/ppermute | solution.py:245
  44.8 13.0 %collective-permute-start.32 = (f32[128,512]{1,0:T(8,128)S(1)}, f32[128,512]{1,0:T(8,128)S(1)}, u32[]{:S(2)}, u32[]{:S(2)}) collective-permute-start(f32[128,512]{1,0:T(8,128)S(1)} %get-tuple-element.27), channel_id=1, source_target_pairs={{0,1},{4,5},{8,9},{12,13},{16,17},{20,21},{24,25},{28,29}} | collective-permute-start | bytes 786440 | tf_op jit(solution)/shard_map/ppermute | solution.py:245
  47.6 10.8 %collective-permute-start.18 = (f32[128,512]{1,0:T(8,128)}, f32[128,512]{1,0:T(8,128)S(1)}, u32[]{:S(2)}, u32[]{:S(2)}) collective-permute-start(f32[128,512]{1,0:T(8,128)} %collective-permute-done.17), channel_id=1, source_target_pairs={{1,2},{5,6},{9,10},{13,14},{17,18},{21,22},{25,26},{29,30}} | collective-permute-start | bytes 786440 | tf_op jit(solution)/shard_map/ppermute | solution.py:245
  48.3 10.8 %collective-permute-start.21 = (f32[128,512]{1,0:T(8,128)}, f32[128,512]{1,0:T(8,128)S(1)}, u32[]{:S(2)}, u32[]{:S(2)}) collective-permute-start(f32[128,512]{1,0:T(8,128)} %collective-permute-done.20), channel_id=1, source_target_pairs={{1,2},{5,6},{9,10},{13,14},{17,18},{21,22},{25,26},{29,30}} | collective-permute-start | bytes 786440 | tf_op jit(solution)/shard_map/ppermute | solution.py:245
  49.0 10.8 %collective-permute-start.24 = (f32[128,512]{1,0:T(8,128)}, f32[128,512]{1,0:T(8,128)S(1)}, u32[]{:S(2)}, u32[]{:S(2)}) collective-permute-start(f32[128,512]{1,0:T(8,128)} %collective-permute-done.23), channel_id=1, source_target_pairs={{1,2},{5,6},{9,10},{13,14},{17,18},{21,22},{25,26},{29,30}} | collective-permute-start | bytes 786440 | tf_op jit(solution)/shard_map/ppermute | solution.py:245
  53.3 11.4 %collective-permute-start.27 = (f32[128,512]{1,0:T(8,128)S(1)}, f32[128,512]{1,0:T(8,128)S(1)}, u32[]{:S(2)}, u32[]{:S(2)}) collective-permute-start(f32[128,512]{1,0:T(8,128)S(1)} %collective-permute-done.26), channel_id=1, source_target_pairs={{1,2},{5,6},{9,10},{13,14},{17,18},{21,22},{25,26},{29,30}} | collective-permute-start | bytes 786440 | tf_op jit(solution)/shard_map/ppermute | solution.py:245
  57.7 7.0 %collective-permute-start.30 = (f32[128,512]{1,0:T(8,128)S(1)}, f32[128,512]{1,0:T(8,128)S(1)}, u32[]{:S(2)}, u32[]{:S(2)}) collective-permute-start(f32[128,512]{1,0:T(8,128)S(1)} %collective-permute-done.29), channel_id=1, source_target_pairs={{1,2},{5,6},{9,10},{13,14},{17,18},{21,22},{25,26},{29,30}} | collective-permute-start | bytes 786440 | tf_op jit(solution)/shard_map/ppermute | solution.py:245
  58.4 7.0 %collective-permute-start.33 = (f32[128,512]{1,0:T(8,128)S(1)}, f32[128,512]{1,0:T(8,128)S(1)}, u32[]{:S(2)}, u32[]{:S(2)}) collective-permute-start(f32[128,512]{1,0:T(8,128)S(1)} %collective-permute-done.32), channel_id=1, source_target_pairs={{1,2},{5,6},{9,10},{13,14},{17,18},{21,22},{25,26},{29,30}} | collective-permute-start | bytes 786440 | tf_op jit(solution)/shard_map/ppermute | solution.py:245
  59.8 6.3 %collective-permute-start.22 = (f32[128,512]{1,0:T(8,128)S(1)}, f32[128,512]{1,0:T(8,128)S(1)}, u32[]{:S(2)}, u32[]{:S(2)}) collective-permute-start(f32[128,512]{1,0:T(8,128)S(1)} %collective-permute-done.21), channel_id=1, source_target_pairs={{2,3},{6,7},{10,11},{14,15},{18,19},{22,23},{26,27},{30,31}} | collective-permute-start | bytes 786440 | tf_op jit(solution)/shard_map/ppermute | solution.py:245
  64.6 18.8 %collective-permute-start = (f32[128,640]{1,0:T(8,128)S(1)}, f32[128,640]{1,0:T(8,128)S(1)}, u32[]{:S(2)}, u32[]{:S(2)}) collective-permute-start(f32[128,640]{1,0:T(8,128)S(1)} %copy-done.17), channel_id=1, source_target_pairs={{0,4},{4,0},{8,12},{12,8},{16,20},{20,16},{24,28},{28,24},{1,5},{5... | collective-permute-start | bytes 983048 | tf_op jit(solution)/shard_map/ppermute | solution.py:249
  82.9 53.5 %collective-permute-start.41 = (f32[2,2,128,512]{3,2,1,0:T(8,128)}, f32[2,2,128,512]{3,2,1,0:T(8,128)S(1)}, u32[]{:S(2)}, u32[]{:S(2)}) collective-permute-start(f32[2,2,128,512]{3,2,1,0:T(8,128)} %bitcast.14), channel_id=1, source_target_pairs={{0,4},{4,0},{8,12},{12,8},{16,20},{20,16},{24,28},{28,24},{1,5},{5... | collective-permute-start | bytes 3145736 | tf_op jit(solution)/shard_map/ppermute | solution.py:249
  83.5 6.2 %collective-permute-start.3 = (f32[64,640]{1,0:T(8,128)S(1)}, f32[64,640]{1,0:T(8,128)S(1)}, u32[]{:S(2)}, u32[]{:S(2)}) collective-permute-start(f32[64,640]{1,0:T(8,128)S(1)} %get-tuple-element.43), channel_id=1, source_target_pairs={{0,16},{4,20},{8,24},{12,28},{16,0},{20,4},{24,8},{28,12},{1,17},{... | collective-permute-start | bytes 491528 | tf_op jit(solution)/shard_map/ppermute | solution.py:249
  85.1 6.2 %collective-permute-start.1 = (f32[64,640]{1,0:T(8,128)S(1)}, f32[64,640]{1,0:T(8,128)S(1)}, u32[]{:S(2)}, u32[]{:S(2)}) collective-permute-start(f32[64,640]{1,0:T(8,128)S(1)} %get-tuple-element.44), channel_id=1, source_target_pairs={{0,8},{4,12},{8,0},{12,4},{16,24},{20,28},{24,16},{28,20},{1,9},{5... | collective-permute-start | bytes 491528 | tf_op jit(solution)/shard_map/ppermute | solution.py:249
  89.7 5.4 %collective-permute-start.4 = (f32[64,640]{1,0:T(8,128)S(1)}, f32[64,640]{1,0:T(8,128)S(1)}, u32[]{:S(2)}, u32[]{:S(2)}) collective-permute-start(f32[64,640]{1,0:T(8,128)S(1)} %add.158), channel_id=1, source_target_pairs={{0,8},{4,12},{8,0},{12,4},{16,24},{20,28},{24,16},{28,20},{1,9},{5... | collective-permute-start | bytes 491528 | tf_op jit(solution)/shard_map/ppermute | solution.py:249
  91.3 5.4 %collective-permute-start.2 = (f32[64,640]{1,0:T(8,128)S(1)}, f32[64,640]{1,0:T(8,128)S(1)}, u32[]{:S(2)}, u32[]{:S(2)}) collective-permute-start(f32[64,640]{1,0:T(8,128)S(1)} %add.155), channel_id=1, source_target_pairs={{0,16},{4,20},{8,24},{12,28},{16,0},{20,4},{24,8},{28,12},{1,17},{... | collective-permute-start | bytes 491528 | tf_op jit(solution)/shard_map/ppermute | solution.py:249
  125.0 13.0 %collective-permute-start.9 = (f32[32,640]{1,0:T(8,128)}, f32[32,640]{1,0:T(8,128)S(1)}, u32[]{:S(2)}, u32[]{:S(2)}) collective-permute-start(f32[32,640]{1,0:T(8,128)} %get-tuple-element.21), channel_id=1, source_target_pairs={{0,3},{4,7},{8,11},{12,15},{16,19},{20,23},{24,27},{28,31}} | collective-permute-start | bytes 245768 | tf_op jit(solution)/shard_map/ppermute | solution.py:245
  136.8 9.2 %collective-permute-start.42 = (f32[2,64,512]{2,1,0:T(8,128)S(1)}, f32[2,64,512]{2,1,0:T(8,128)S(1)}, u32[]{:S(2)}, u32[]{:S(2)}) collective-permute-start(f32[2,64,512]{2,1,0:T(8,128)S(1)} %dynamic-slice_bitcast_fusion.1), channel_id=1, source_target_pairs={{0,8},{4,12},{8,0},{12,4},{16,24},{20,28},{24,16},{28,20},{1,9},{5... | collective-permute-start | bytes 786440 | tf_op jit(solution)/shard_map/ppermute | solution.py:249
  140.0 15.4 %collective-permute-start.15 = (f32[32,640]{1,0:T(8,128)S(1)}, f32[32,640]{1,0:T(8,128)S(1)}, u32[]{:S(2)}, u32[]{:S(2)}) collective-permute-start(f32[32,640]{1,0:T(8,128)S(1)} %add_add_fusion.2.refs_0_), channel_id=1, source_target_pairs={{0,24},{4,28},{8,16},{12,20},{16,8},{20,12},{24,0},{28,4},{1,25},{... | collective-permute-start | bytes 245768 | tf_op jit(solution)/shard_map/ppermute | solution.py:249
  141.5 14.6 %collective-permute-start.13 = (f32[32,640]{1,0:T(8,128)S(1)}, f32[32,640]{1,0:T(8,128)S(1)}, u32[]{:S(2)}, u32[]{:S(2)}) collective-permute-start(f32[32,640]{1,0:T(8,128)S(1)} %add_add_fusion.2.refs_0_), channel_id=1, source_target_pairs={{0,16},{4,20},{8,24},{12,28},{16,0},{20,4},{24,8},{28,12},{1,17},{... | collective-permute-start | bytes 245768 | tf_op jit(solution)/shard_map/ppermute | solution.py:249
  142.7 13.4 %collective-permute-start.11 = (f32[32,640]{1,0:T(8,128)S(1)}, f32[32,640]{1,0:T(8,128)S(1)}, u32[]{:S(2)}, u32[]{:S(2)}) collective-permute-start(f32[32,640]{1,0:T(8,128)S(1)} %add_add_fusion.2.refs_0_), channel_id=1, source_target_pairs={{0,8},{4,12},{8,0},{12,4},{16,24},{20,28},{24,16},{28,20},{1,9},{5... | collective-permute-start | bytes 245768 | tf_op jit(solution)/shard_map/ppermute | solution.py:249
  143.5 13.1 %collective-permute-start.10 = (f32[32,640]{1,0:T(8,128)S(1)}, f32[32,640]{1,0:T(8,128)S(1)}, u32[]{:S(2)}, u32[]{:S(2)}) collective-permute-start(f32[32,640]{1,0:T(8,128)S(1)} %add_add_fusion.2.refs_0_), channel_id=1, source_target_pairs={{0,4},{4,0},{8,12},{12,8},{16,20},{20,16},{24,28},{28,24},{1,5},{5... | collective-permute-start | bytes 245768 | tf_op jit(solution)/shard_map/ppermute | solution.py:249
  146.0 7.6 %collective-permute-start.44 = (f32[2,64,512]{2,1,0:T(8,128)S(1)}, f32[2,64,512]{2,1,0:T(8,128)S(1)}, u32[]{:S(2)}, u32[]{:S(2)}) collective-permute-start(f32[2,64,512]{2,1,0:T(8,128)S(1)} %dynamic-slice_bitcast_fusion), channel_id=1, source_target_pairs={{0,16},{4,20},{8,24},{12,28},{16,0},{20,4},{24,8},{28,12},{1,17},{... | collective-permute-start | bytes 786440 | tf_op jit(solution)/shard_map/ppermute | solution.py:249
  (32 other events, 131.5 us)

commit v3 on v2

--- a/solution.py
+++ b/solution.py
@@ -92,36 +92,160 @@
         yield i, i, (nb - i) * BLOCK
 
 
-def pack_kernel(core_ref, corner_ref, keep_a_ref, keep_b_ref, send_ref, rect_ref):
-    nb = corner_ref.shape[0] // BLOCK
+HBM = pl.BlockSpec(memory_space=pltpu.HBM)
+
+
+def split(x):
+    high_part = x.astype(jnp.bfloat16)
+    return high_part, (x - high_part.astype(jnp.float32)).astype(jnp.bfloat16)
+
+
+def three(left, right, dims):
+    def one(a, b):
+        return lax.dot_general(a, b, (dims, ((), ())), preferred_element_type=jnp.float32)
+
+    (ah, al), (bh, bl) = left, right
+    return one(ah, bh) + (one(ah, bl) + one(al, bh))
+
+
+def product_kernel(edges, tall, place_ref, mask_ref, inverse_hbm, coupling_hbm, *refs):
+    count = len(edges) - 1
+    pieces = refs[:count]
+    keep_a, keep_b, send, panel, rows, ph, plo, qh, ql, rect, sems = refs[count:]
+    depth, width = panel.shape
+    nb, steps, tile = width // BLOCK, depth // tall, depth // mask_ref.shape[1]
+    copies = [pltpu.make_async_copy(coupling_hbm.at[:, pl.ds(0, width)], panel, sems.at[0])]
+    for i in range(steps):
+        copies.append(pltpu.make_async_copy(inverse_hbm.at[pl.ds(i * tall, tall)], rows.at[i], sems.at[1 + i]))
+    for copy in copies:
+        copy.start()
+    kept = [mask_ref[0, t].astype(jnp.float32) for t in range(depth // tile)]
+    copies[0].wait()
+    for t in range(depth // tile):
+        here = slice(t * tile, (t + 1) * tile)
+        ph[here, :], plo[here, :] = split(panel[here, :] * kept[t])
+    for i in range(steps):
+        copies[1 + i].wait()
+        value = three(split(rows[i]), (ph[...], plo[...]), ((1,), (0,)))
+        for t in range(i * tall // tile, (i + 1) * tall // tile):
+            part = value[t * tile - i * tall : (t + 1) * tile - i * tall, :] * kept[t]
+            here = slice(t * tile, (t + 1) * tile)
+            qh[here, :], ql[here, :] = split(part)
+            for k in range(count):
+                lo, hi = max(edges[k], t * tile), min(edges[k + 1], (t + 1) * tile)
+                if lo < hi:
+                    pieces[k][lo - edges[k] : hi - edges[k], :] = part[lo - t * tile : hi - t * tile, :]
     for i, block, low in strips(nb):
         wide = (block + 1) * BLOCK
-        rect_ref[i * BLOCK : (i + 1) * BLOCK, low : low + wide] = corner_ref[
-            block * BLOCK : (block + 1) * BLOCK, :wide
-        ]
-    half = rect_ref.shape[0] // 2
-    core = core_ref[0]
+        mine = slice(block * BLOCK, wide)
+        rect[i * BLOCK : (i + 1) * BLOCK, low : low + wide] = three(
+            (ph[:, mine], plo[:, mine]), (qh[:, :wide], ql[:, :wide]), ((0,), (0,))
+        )
+    half = rect.shape[0] // 2
+    core = place_ref[1] & 1
     mine = pl.multiple_of(core * half, half)
     theirs = pl.multiple_of((1 - core) * half, half)
-    keep_a_ref[...] = rect_ref[pl.ds(mine, half // 2), :]
-    keep_b_ref[...] = rect_ref[pl.ds(mine + half // 2, half // 2), :]
-    send_ref[...] = rect_ref[pl.ds(theirs, half), :]
-
-
-def pack(core, corner):
-    nb = corner.shape[0] // BLOCK
-    tall, wide = nb // 2 * BLOCK, (nb + 1) * BLOCK
+    keep_a[...] = rect[pl.ds(mine, half // 2), :]
+    keep_b[...] = rect[pl.ds(mine + half // 2, half // 2), :]
+    send[...] = rect[pl.ds(theirs, half), :]
+
+
+def product(place, mask, inverse, coupling, width, edges):
+    depth, count = inverse.shape[0], len(edges) - 1
+    nb, tall = width // BLOCK, depth // 4
+    high_rows, wide = nb // 2 * BLOCK, (nb + 1) * BLOCK
     return pl.pallas_call(
-        pack_kernel,
-        out_shape=(shape(tall // 4, wide), shape(tall // 4, wide), shape(tall // 2, wide)),
-        in_specs=[SMEM] + vmem(1),
-        out_specs=tuple(vmem(3)),
-        scratch_shapes=[pltpu.VMEM((tall, wide), jnp.float32)],
-        cost_estimate=pl.CostEstimate(flops=0, bytes_accessed=8 * tall * wide, transcendentals=0),
-    )(core, corner)
-
-
-def factor_kernel(place_ref, own_a, own_b, other_a, other_b, diag_ref, l_ref, piece_ref, w_ref, rect_ref, base_ref, scale_ref):
+        functools.partial(product_kernel, edges, tall),
+        out_shape=tuple(shape(b - a, width) for a, b in zip(edges, edges[1:]))
+        + (shape(high_rows // 4, wide), shape(high_rows // 4, wide), shape(high_rows // 2, wide)),
+        in_specs=[SMEM, SMEM, HBM, HBM],
+        out_specs=tuple(vmem(count + 3)),
+        scratch_shapes=[pltpu.VMEM((depth, width), jnp.float32), pltpu.VMEM((depth // tall, tall, depth), jnp.float32)]
+        + [pltpu.VMEM((depth, width), jnp.bfloat16)] * 4
+        + [pltpu.VMEM((high_rows, wide), jnp.float32), pltpu.SemaphoreType.DMA((1 + depth // tall,))],
+        compiler_params=pltpu.CompilerParams(vmem_limit_bytes=61 << 20),
+        cost_estimate=pl.CostEstimate(
+            flops=6 * depth * width * (depth + width), bytes_accessed=4 * depth * (depth + 2 * width), transcendentals=0
+        ),
+    )(place, mask, inverse, coupling)
+
+
+def collect_kernel(planes, count, place_ref, *refs):
+    groups, (out_ref, sems) = refs[: planes * count], refs[planes * count :]
+    for h in range(planes):
+
+        @pl.when(place_ref[0] == h)
+        def _(h=h):
+            low, copies = 0, []
+            for k in range(count):
+                ref = groups[h * count + k]
+                copies.append(pltpu.make_async_copy(ref, out_ref.at[pl.ds(low, ref.shape[0])], sems.at[k]))
+                low += ref.shape[0]
+            for copy in copies:
+                copy.start()
+            for copy in copies:
+                copy.wait()
+
+
+def collect(place, groups):
+    count = len(groups[0])
+    rows, width = sum(x.shape[0] for x in groups[0]), groups[0][0].shape[1]
+    return pl.pallas_call(
+        functools.partial(collect_kernel, len(groups), count),
+        out_shape=shape(rows, width),
+        in_specs=[SMEM] + [pl.BlockSpec(memory_space=pl.ANY)] * (len(groups) * count),
+        out_specs=vmem(1)[0],
+        scratch_shapes=[pltpu.SemaphoreType.DMA((count,))],
+        compiler_params=pltpu.CompilerParams(vmem_limit_bytes=8 << 20),
+        cost_estimate=pl.CostEstimate(flops=0, bytes_accessed=8 * rows * width, transcendentals=0),
+    )(place, *[x for group in groups for x in group])
+
+
+def part_kernel(place_ref, first_ref, second_ref, keep_ref, send_ref):
+    core, wide = place_ref[1] & 1, keep_ref.shape[2]
+    for ref, bit in ((keep_ref, core), (send_ref, 1 - core)):
+        for j in range(ref.shape[0]):
+            here = pl.ds(pl.multiple_of((2 * j + bit) * wide, wide), wide)
+            ref[j] = first_ref[:, here] + second_ref[:, here]
+
+
+def part(place, first, second, scen):
+    width, cols = first.shape
+    half = shape(scen // 2, width, cols // scen)
+    return pl.pallas_call(
+        part_kernel,
+        out_shape=(half, half),
+        in_specs=[SMEM] + vmem(2),
+        out_specs=tuple(vmem(2)),
+        compiler_params=pltpu.CompilerParams(vmem_limit_bytes=24 << 20),
+        cost_estimate=pl.CostEstimate(flops=width * cols, bytes_accessed=12 * width * cols, transcendentals=0),
+    )(place, first, second)
+
+
+def turn_kernel(cuts, place_ref, own_ref, got_ref, *outs):
+    for (low, high_row, position, bit), keep_ref, send_ref in zip(cuts, outs[::2], outs[1::2]):
+        mine = (place_ref[1] >> bit) & 1
+        rows = slice(low, high_row)
+        for ref, value in ((keep_ref, mine), (send_ref, 1 - mine)):
+            for j in range(ref.shape[0]):
+                at = ((j >> position) << (position + 1)) + (j & ((1 << position) - 1)) + (value << position)
+                ref[j] = own_ref[at, rows, :] + got_ref[at, rows, :]
+
+
+def turn(place, own, got, cuts):
+    blocks, _, wide = own.shape
+    outs = tuple(shape(blocks // 2, high_row - low, wide) for low, high_row, _, _ in cuts for _ in range(2))
+    return pl.pallas_call(
+        functools.partial(turn_kernel, cuts),
+        out_shape=outs,
+        in_specs=[SMEM] + vmem(2),
+        out_specs=tuple(vmem(len(outs))),
+        compiler_params=pltpu.CompilerParams(vmem_limit_bytes=12 << 20),
+        cost_estimate=pl.CostEstimate(flops=own.size, bytes_accessed=12 * own.size, transcendentals=0),
+    )(place, own, got)
+
+
+def factor_kernel(place_ref, own_a, own_b, other_a, other_b, diag_ref, own_ref, piece_ref, l_ref, w_ref, rect_ref, base_ref, scale_ref):
     size = w_ref.shape[0]
     nb = size // BLOCK
     plane, me = place_ref[0], place_ref[1]
@@ -179,38 +303,48 @@
                 rect_ref[i * BLOCK : (i + 1) * BLOCK, low + k * BLOCK : low + (k + 1) * BLOCK] = w_ref[
                     block * BLOCK : (block + 1) * BLOCK, k * BLOCK : (k + 1) * BLOCK
                 ]
+        rows = own_ref.shape[0]
+        first = jnp.minimum(place_ref[2], size - rows)
+        own_ref[...] = l_ref[pl.ds(pl.multiple_of(first, rows), rows), :]
         each = piece_ref.shape[0]
         piece_ref[...] = rect_ref[pl.ds(pl.multiple_of(me * each, each), each), :]
 
 
-def factor(place, parts, diag, each):
+def factor(place, parts, diag, each, rows):
     size = diag.shape[1]
     nb = size // BLOCK
     tall, wide = nb // 2 * BLOCK, (nb + 1) * BLOCK
     return pl.pallas_call(
         factor_kernel,
-        out_shape=(shape(size, size), shape(each, wide)),
+        out_shape=(shape(rows, size), shape(each, wide)),
         in_specs=[SMEM] + vmem(5),
         out_specs=tuple(vmem(2)),
         scratch_shapes=[
+            pltpu.VMEM((size, size), jnp.float32),
             pltpu.VMEM((size, size), jnp.float32),
             pltpu.VMEM((tall, wide), jnp.float32),
             pltpu.VMEM((BLOCK, BLOCK), jnp.float32),
             pltpu.VMEM((BLOCK, BLOCK), jnp.float32),
         ],
+        compiler_params=pltpu.CompilerParams(vmem_limit_bytes=16 << 20),
         cost_estimate=pl.CostEstimate(flops=20 * size**3, bytes_accessed=12 * size * size, transcendentals=size),
     )(place, *parts, diag)
 
 
 def last_kernel(count, place_ref, *refs):
-    pieces, (keep_a, got_a, keep_b, got_b, l_ref, out_ref, rect_ref, rows_ref) = refs[:count], refs[count:]
+    pieces, (keep_a, got_a, keep_b, got_b, own_ref, out_ref, rect_ref, rows_ref) = refs[:count], refs[count:]
     me, first = place_ref[1], place_ref[2]
     rows, width = out_ref.shape
     nb = width // BLOCK
     each = pieces[0].shape[0]
-    half = rows // 2
-    rows_ref[:half, :] = keep_a[...] + got_a[...]
-    rows_ref[half:, :] = keep_b[...] + got_b[...]
+    if len(keep_a.shape) == 3:
+        half = keep_a.shape[1]
+        rows_ref[:, :half] = (keep_a[0] + got_a[0]).T
+        rows_ref[:, half:] = (keep_b[0] + got_b[0]).T
+    else:
+        half = rows // 2
+        rows_ref[:half, :] = keep_a[...] + got_a[...]
+        rows_ref[half:, :] = keep_b[...] + got_b[...]
     for m in range(count):
         rect_ref[pl.ds(pl.multiple_of((me ^ m) * each, each), each), :] = pieces[m][...]
     for i, block, low in strips(nb):
@@ -224,11 +358,11 @@
 
     @pl.when(first < width)
     def _():
-        out_ref[...] = l_ref[pl.ds(pl.multiple_of(first, rows), rows), :]
-
-
-def last(place, pieces, sums, lower, rows):
-    width = lower.shape[0]
+        out_ref[...] = own_ref[...]
+
+
+def last(place, pieces, sums, own):
+    rows, width = own.shape
     nb = width // BLOCK
     tall, wide = nb // 2 * BLOCK, (nb + 1) * BLOCK
     return pl.pallas_call(
@@ -237,8 +371,9 @@
         in_specs=[SMEM] + vmem(len(pieces) + 5),
         out_specs=vmem(1)[0],
         scratch_shapes=[pltpu.VMEM((tall, wide), jnp.float32), pltpu.VMEM((rows, width), jnp.float32)],
+        compiler_params=pltpu.CompilerParams(vmem_limit_bytes=12 << 20),
         cost_estimate=pl.CostEstimate(flops=6 * rows * width * width, bytes_accessed=8 * width * width, transcendentals=0),
-    )(place, *pieces, *sums, lower)
+    )(place, *pieces, *sums, own)
 
 
 def hop(x, source, target):
@@ -282,8 +417,30 @@
     return pairs[0] + pairs[1]
 
 
+def scatter_sum_columns(place, first, second):
+    count = lax.axis_size("scen")
+    bits, near, far = orders(count)
+    half = first.shape[0] // 2
+    keep, send = part(place, first, second, count)
+    got = exchange(send, 1, count)
+    left = [list(range(1, bits)), list(range(1, bits))]
+    pairs = None
+    for a, b in zip(near + far, far + near):
+        if pairs is None:
+            cuts = tuple((i * half, (i + 1) * half, left[i].index(bit), bit) for i, bit in ((0, a), (1, b)))
+            outs = turn(place, keep, got, cuts)
+        else:
+            outs = ()
+            for i, bit in ((0, a), (1, b)):
+                outs += turn(place, *pairs[i], ((0, half, left[i].index(bit), bit),))
+        pairs = []
+        for i, bit in ((0, a), (1, b)):
+            left[i].remove(bit)
+            pairs.append((outs[2 * i], exchange(outs[2 * i + 1], 1 << bit, count)))
+    return pairs[0] + pairs[1]
+
+
 PIECES = 8
-HEAD = 2
 LATE = 2
 
 
@@ -298,31 +455,15 @@
     scen, planes = lax.axis_size("scen"), lax.axis_size("col")
     me, plane = lax.axis_index("scen").astype(jnp.int32), lax.axis_index("col").astype(jnp.int32)
     rows = local.shape[1] // scen
-    first = plane * local.shape[1] + me * rows
-    place = jnp.stack([plane, me, first])
-    depth = local.shape[0]
-    keep = jnp.repeat(tile_mask[0].astype(jnp.float32), depth // tile_mask.shape[1])
-    masked_inverse = inverses[0] * keep[:, None] * keep[None, :]
-    panel = local[:, :width]
-    edge = bounds(depth)
-
-    cut = edge[HEAD]
-    head = high(masked_inverse[:cut], panel, ((1,), (0,)))
-    tail = high(masked_inverse[cut:], panel, ((1,), (0,)))
-
-    heads = lax.optimization_barrier(tuple(head[edge[k] : edge[k + 1]] for k in range(HEAD)))
-    tails = lax.optimization_barrier(tuple(tail[edge[k] - cut : edge[k + 1] - cut] for k in range(HEAD, PIECES)))
-    arrived = []
-    for k in range(PIECES):
-        piece = (heads + tails)[k]
-        mine = jnp.where(plane == 0, piece, 0.0)
-        for h in range(planes - 1):
-            piece = hop(piece, h, h + 1)
-            mine = mine + piece
-        arrived.append(mine)
-
-    corner = high(panel[:cut], head, ((0,), (0,))) + high(panel[cut:], tail, ((0,), (0,)))
-    keep_a, keep_b, send = pack((me & 1).reshape(1), corner)
+    place = jnp.stack([plane, me, plane * local.shape[1] + me * rows])
+    edge = bounds(local.shape[0])
+
+    *own, keep_a, keep_b, send = product(place, tile_mask, inverses[0], local, width, edge)
+
+    groups = [own]
+    for h in range(planes - 1):
+        groups.append([hop(groups[h][k], h, h + 1) for k in range(PIECES)])
+
     got = exchange(send, 1, scen)
     a, b = keep_a + got[: got.shape[0] // 2], keep_b + got[got.shape[0] // 2 :]
     _, near, far = orders(scen)
@@ -332,7 +473,7 @@
         a, b = a + got_a, b + got_b
     parts = (a, b, exchange(a, 1, scen), exchange(b, 1, scen))
     each = width // BLOCK // 2 * BLOCK // scen
-    lower, piece = factor(place, parts, hess_diag[None, :], each)
+    lower, piece = factor(place, parts, hess_diag[None, :], each, rows)
 
     mine = jnp.where(plane == 0, piece, 0.0)
     for h in range(1, planes):
@@ -340,12 +481,17 @@
     pieces = [mine if m == 0 else exchange(mine, m, scen) for m in range(0, scen, 2)]
     pieces = [p for m in range(0, scen, 2) for p in (pieces[m // 2], exchange(pieces[m // 2], 1, scen))]
 
-    early = edge[PIECES - LATE]
-    top = jnp.concatenate(arrived[: PIECES - LATE], axis=0)
-    bottom = jnp.concatenate(arrived[PIECES - LATE :], axis=0)
-    total = high(local[:early], top, ((0,), (0,)))
-    total = total + high(local[early:], bottom, ((0,), (0,)))
-    return last(place, pieces, scatter_sum(total), lower, rows)
+    cut = PIECES - LATE
+    early = edge[cut]
+    top = collect(place, [group[:cut] for group in groups])
+    bottom = collect(place, [group[cut:] for group in groups])
+    if rows % BLOCK == 0:
+        first, second = high(top, local[:early], ((0,), (0,))), high(bottom, local[early:], ((0,), (0,)))
+        sums = scatter_sum_columns(place, first, second)
+    else:
+        first, second = high(local[:early], top, ((0,), (0,))), high(local[early:], bottom, ((0,), (0,)))
+        sums = scatter_sum(first + second)
+    return last(place, pieces, sums, lower)
 
 
 def solution(mesh):

time: 165 us -> 161 us (0.976)
  matrix products: 14.5 us -> 4.02 us
  waiting for transfers between devices: 29.4 us -> 39.6 us
  local copies, waits for them, and re-layouts: 16.2 us -> 7.16 us
  other arithmetic: 10.6 us -> 1.72 us
  Pallas kernels: 31.7 us -> 40.2 us
  starting transfers between devices: 61.1 us -> 67 us
    ppermute x27, waiting for transfers between devices: 11.2 us -> 24.4 us  [hop(): return lax.ppermute(x, 'col', [(source, target)])]
    dot_general x6 -> x2, matrix products: 14.5 us -> 4.02 us  [high(): lax.dot_general(left, right, (dims, ((), ())), precision=lax.Precision.HI...]
    pallas_call x2 -> x8, Pallas kernels: 28.4 us -> 38.1 us  [the longest x1 24.4 us: factor(): pl.pallas_call(factor_kernel, out_shape=(shape(rows, size), shape(each, w...]
    ppermute x27, starting transfers between devices: 45.5 us -> 51 us  [hop(): return lax.ppermute(x, 'col', [(source, target)])]
    dynamic_slice x1 -> x0, local copies, waits for them, and re-layouts: 4.38 us -> none  [halve(): keep = lax.dynamic_index_in_dim(x, mine, axis, keepdims=False)]
    unnamed x5 -> x0, other arithmetic: 3.66 us -> none
    ppermute x19, waiting for transfers between devices: 18.2 us -> 15.3 us  [exchange(): return lax.ppermute(x, 'scen', [(i, i ^ mask) for i in range(count)])]
    reshape x1 -> x0, local copies, waits for them, and re-layouts: 2.79 us -> none  [scatter_sum(): x = x.reshape((2,) * bits + (rows,) + x.shape[1:])]
  transfers between devices with their start and end apart: 46 -> 46, of which waited for: 17 -> 18; matrix products, arithmetic and copies ran while one was open for 20% -> 3% of each run, Pallas kernels for 17% -> 18%
where the time goes in v3:
time: 161 us; the launch traced here: 160 us
  starting transfers between devices  67 us (42%)
  Pallas kernels  40.2 us (25%)
  waiting for transfers between devices  39.6 us (25%)
  local copies, waits for them, and re-layouts  7.16 us (4%)
  matrix products  4.02 us (2%)
  other arithmetic  1.72 us (1%)
    ppermute x27, starting transfers between devices, hop(): return lax.ppermute(x, 'col', [(source, target)])  51 us
    ppermute x27, waiting for transfers between devices, hop(): return lax.ppermute(x, 'col', [(source, target)])  24.4 us
    pallas_call x1, Pallas kernels, factor(): pl.pallas_call(factor_kernel, out_shape=(shape(rows, size), shape(each, w...  24.4 us
    ppermute x19, starting transfers between devices, exchange(): return lax.ppermute(x, 'scen', [(i, i ^ mask) for i in range(count)])  16 us
    ppermute x19, waiting for transfers between devices, exchange(): return lax.ppermute(x, 'scen', [(i, i ^ mask) for i in range(count)])  15.3 us
    pallas_call x1, Pallas kernels, product(): pl.pallas_call(functools.partial(product_kernel, edges, tall), out_shape=...  9.3 us
    unnamed x26, local copies, waits for them, and re-layouts  7.16 us
    dot_general x2, matrix products, high(): lax.dot_general(left, right, (dims, ((), ())), precision=lax.Precision.HI...  4.02 us
  transfers between devices with their start and end apart: 46, of which 18 were waited for; matrix products, arithmetic and copies ran while one was open for 3% of the time, Pallas kernels for 18%

profile of v3, /device:TPU:0, one launch (start us, length us, event | category | flops | bytes accessed | tf_op | source)
XLA Modules:
  0.0 160.4 jit_solution(14597300633330342163)
XLA Ops:
  0.6 9.3 %shard_map.46 = (f32[128,512]{1,0:T(8,128)}, f32[128,512]{1,0:T(8,128)}, f32[128,512]{1,0:T(8,128)}, f32[128,512]{1,0:T(8,128)}, f32[128,512]{1,0:T(8,128)}, /*i...) custom-call(s32[3]{0:T(128)} %pad_add_fusion.place_ref, ...), custom_call_target="tpu_custom_call" | custom-call | flops 4831838208 | bytes 8388608 | tf_op jit(solution)/shard_map/pallas_call | solution.py:157
  9.9 5.0 %collective-permute-start.17 = (f32[128,512]{1,0:T(8,128)}, f32[128,512]{1,0:T(8,128)S(1)}, u32[]{:S(2)}, u32[]{:S(2)}) collective-permute-start(f32[128,512]{1,0:T(8,128)} %get-tuple-element.32.refs_0_), channel_id=1, source_target_pairs={{0,1},{4,5},{8,9},{12,13},{16,17},{20,21},{24,25},{28,29}} | collective-permute-start | bytes 786440 | tf_op jit(solution)/shard_map/ppermute | solution.py:380
  20.2 1.7 %collective-permute-done.17.refs_6_ = f32[128,512]{1,0:T(8,128)S(1)} collective-permute-done((f32[128,512]{1,0:T(8,128)}, f32[128,512]{1,0:T(8,128)S(1)}, u32[]{:S(2)}, u32[]{:S(2)}) %collective-permute-start.17) | collective-permute-done | bytes 262176 | tf_op jit(solution)/shard_map/ppermute | solution.py:380
  21.9 4.3 %collective-permute-start.22 = (f32[128,512]{1,0:T(8,128)}, f32[128,512]{1,0:T(8,128)S(1)}, u32[]{:S(2)}, u32[]{:S(2)}) collective-permute-start(f32[128,512]{1,0:T(8,128)} %get-tuple-element.37.refs_5_), channel_id=1, source_target_pairs={{0,1},{4,5},{8,9},{12,13},{16,17},{20,21},{24,25},{28,29}} | collective-permute-start | bytes 786440 | tf_op jit(solution)/shard_map/ppermute | solution.py:380
  27.5 4.3 %collective-permute-start.35 = (f32[128,512]{1,0:T(8,128)}, f32[128,512]{1,0:T(8,128)S(1)}, u32[]{:S(2)}, u32[]{:S(2)}) collective-permute-start(f32[128,512]{1,0:T(8,128)} %get-tuple-element.38.refs_0_), channel_id=1, source_target_pairs={{0,1},{4,5},{8,9},{12,13},{16,17},{20,21},{24,25},{28,29}} | collective-permute-start | bytes 786440 | tf_op jit(solution)/shard_map/ppermute | solution.py:380
  33.1 4.3 %collective-permute-start.36 = (f32[128,512]{1,0:T(8,128)}, f32[128,512]{1,0:T(8,128)S(1)}, u32[]{:S(2)}, u32[]{:S(2)}) collective-permute-start(f32[128,512]{1,0:T(8,128)} %get-tuple-element.39.refs_1_), channel_id=1, source_target_pairs={{0,1},{4,5},{8,9},{12,13},{16,17},{20,21},{24,25},{28,29}} | collective-permute-start | bytes 786440 | tf_op jit(solution)/shard_map/ppermute | solution.py:380
  39.4 4.9 %collective-permute-done.21.refs_10_ = f32[128,512]{1,0:T(8,128)S(1)} collective-permute-done((f32[128,512]{1,0:T(8,128)}, f32[128,512]{1,0:T(8,128)S(1)}, u32[]{:S(2)}, u32[]{:S(2)}) %collective-permute-start.21) | collective-permute-done | bytes 262176 | tf_op jit(solution)/shard_map/ppermute | solution.py:380
  45.0 4.9 %collective-permute-done.22.refs_11_ = f32[128,512]{1,0:T(8,128)S(1)} collective-permute-done((f32[128,512]{1,0:T(8,128)}, f32[128,512]{1,0:T(8,128)S(1)}, u32[]{:S(2)}, u32[]{:S(2)}) %collective-permute-start.22) | collective-permute-done | bytes 262176 | tf_op jit(solution)/shard_map/ppermute | solution.py:380
  50.6 4.9 %collective-permute-done.35.refs_2_ = f32[128,512]{1,0:T(8,128)S(1)} collective-permute-done((f32[128,512]{1,0:T(8,128)}, f32[128,512]{1,0:T(8,128)S(1)}, u32[]{:S(2)}, u32[]{:S(2)}) %collective-permute-start.35) | collective-permute-done | bytes 262176 | tf_op jit(solution)/shard_map/ppermute | solution.py:380
  56.3 3.8 %collective-permute-done.36.refs_3_ = f32[128,512]{1,0:T(8,128)S(1)} collective-permute-done((f32[128,512]{1,0:T(8,128)}, f32[128,512]{1,0:T(8,128)S(1)}, u32[]{:S(2)}, u32[]{:S(2)}) %collective-permute-start.36) | collective-permute-done | bytes 262176 | tf_op jit(solution)/shard_map/ppermute | solution.py:380
  75.0 1.4 copy-done.10
  76.4 2.9 %fusion.first_ref = f32[512,1024]{1,0:T(8,128)S(1)} fusion(f32[768,512]{1,0:T(8,128)S(1)} %shard_map.48, f32[1,1024,1024]{2,1,0:T(8,128)S(1)} %copy-done.10), kind=kOutput, calls=%fused_computation | convolution fusion | flops 2415919104 | bytes 6815744 | tf_op jit(solution)/shard_map/dot_general | solution.py:16
  83.1 1.6 collective-permute-start.3
  84.6 1.5 collective-permute-start.1
  86.1 3.1 %collective-permute-done.3 = f32[64,640]{1,0:T(8,128)S(1)} collective-permute-done((f32[64,640]{1,0:T(8,128)S(1)}, f32[64,640]{1,0:T(8,128)S(1)}, u32[]{:S(2)}, u32[]{:S(2)}) %collective-permute-start.3) | collective-permute-done | bytes 163872 | tf_op jit(solution)/shard_map/ppermute | solution.py:384
  89.3 1.6 collective-permute-start.4
  90.9 1.6 collective-permute-start.2
  92.5 2.2 %collective-permute-done.4 = f32[64,640]{1,0:T(8,128)S(1)} collective-permute-done((f32[64,640]{1,0:T(8,128)S(1)}, f32[64,640]{1,0:T(8,128)S(1)}, u32[]{:S(2)}, u32[]{:S(2)}) %collective-permute-start.4) | collective-permute-done | bytes 163872 | tf_op jit(solution)/shard_map/ppermute | solution.py:384
  94.8 1.5 collective-permute-done.2
  96.4 1.4 collective-permute-done.5.other_a
  97.8 24.4 %shard_map.47 = (f32[128,512]{1,0:T(8,128)S(1)}, f32[32,640]{1,0:T(8,128)S(1)}) custom-call(s32[3]{0:T(128)S(1)} %copy-done.8, f32[64,640]{1,0:T(8,128)S(1)} %add.33.own_a, f32[64,640]{1,0:T(8,128)S(1)} %add.36.own_b, f32[64,640]{1,0:T(8,128)S(1)} %collective-permute-done.5.other_a, f32[64,640]{1,0:T(8,128)S(1)} %collective-permute-done.6.other_b, ...), custom_call_target="tpu_custom_call" | custom-call | flops 2684354560 | bytes 3145728 | tf_op jit(solution)/shard_map/pallas_call | solution.py:317
  122.1 13.3 %collective-permute-start.9 = (f32[32,640]{1,0:T(8,128)S(1)}, f32[32,640]{1,0:T(8,128)}, u32[]{:S(2)}, u32[]{:S(2)}) collective-permute-start(f32[32,640]{1,0:T(8,128)S(1)} %get-tuple-element.31), channel_id=1, source_target_pairs={{0,3},{4,7},{8,11},{12,15},{16,19},{20,23},{24,27},{28,31}} | collective-permute-start | bytes 245768 | tf_op jit(solution)/shard_map/ppermute | solution.py:380
  135.5 1.9 %collective-permute-start.8 = (f32[32,640]{1,0:T(8,128)S(1)}, f32[32,640]{1,0:T(8,128)}, u32[]{:S(2)}, u32[]{:S(2)}) collective-permute-start(f32[32,640]{1,0:T(8,128)S(1)} %get-tuple-element.31), channel_id=1, source_target_pairs={{0,2},{4,6},{8,10},{12,14},{16,18},{20,22},{24,26},{28,30}} | collective-permute-start | bytes 245768 | tf_op jit(solution)/shard_map/ppermute | solution.py:380
  137.4 1.9 %collective-permute-start.7 = (f32[32,640]{1,0:T(8,128)S(1)}, f32[32,640]{1,0:T(8,128)}, u32[]{:S(2)}, u32[]{:S(2)}) collective-permute-start(f32[32,640]{1,0:T(8,128)S(1)} %get-tuple-element.31), channel_id=1, source_target_pairs={{0,1},{4,5},{8,9},{12,13},{16,17},{20,21},{24,25},{28,29}} | collective-permute-start | bytes 245768 | tf_op jit(solution)/shard_map/ppermute | solution.py:380
  143.1 1.5 collective-permute-start.15
  144.6 1.5 collective-permute-start.13
  146.6 2.6 %collective-permute-done.42.got_ref = f32[2,256,128]{2,1,0:T(8,128)S(1)} collective-permute-done((f32[2,256,128]{2,1,0:T(8,128)S(1)}, f32[2,256,128]{2,1,0:T(8,128)S(1)}, u32[]{:S(2)}, u32[]{:S(2)}) %collective-permute-start.42) | collective-permute-done | bytes 262176 | tf_op jit(solution)/shard_map/ppermute | solution.py:384
  149.8 1.5 collective-permute-done.44.got_ref
  151.3 1.3 collective-permute-start.43
  153.2 1.4 collective-permute-start.45
  156.4 1.8 %collective-permute-done.45.refs_11_ = f32[1,256,128]{2,1,0:T(8,128)S(1)} collective-permute-done((f32[1,256,128]{2,1,0:T(8,128)S(1)}, f32[1,256,128]{2,1,0:T(8,128)S(1)}, u32[]{:S(2)}, u32[]{:S(2)}) %collective-permute-start.45) | collective-permute-done | bytes 131104 | tf_op jit(solution)/shard_map/ppermute | solution.py:384
  158.2 2.1 %shard_map.54 = f32[128,512]{1,0:T(8,128)} custom-call(s32[3]{0:T(128)S(1)} %copy-done.8, f32[32,640]{1,0:T(8,128)S(1)} %add_add_fusion.refs_0_, f32[32,640]{1,0:T(8,128)S(1)} %collective-permute-done.10.refs_1_, f32[32,640]{1,0:T(8,128)S(1)} %collective-permute-done.11.refs_2_, f32[32,640]{1,0:T(8,128)S(1)} %collective-permute-done.12.refs_3_, ...), custom_call_target="tpu_custom_call" | custom-call | flops 201326592 | bytes 2097152 | tf_op jit(solution)/shard_map/pallas_call | solution.py:368
  (104 shorter events, 38.3 us)
Async XLA Ops:
  9.9 12.0 %collective-permute-start.17 = (f32[128,512]{1,0:T(8,128)}, f32[128,512]{1,0:T(8,128)S(1)}, u32[]{:S(2)}, u32[]{:S(2)}) collective-permute-start(f32[128,512]{1,0:T(8,128)} %get-tuple-element.32.refs_0_), channel_id=1, source_target_pairs={{0,1},{4,5},{8,9},{12,13},{16,17},{20,21},{24,25},{28,29}} | collective-permute-start | bytes 786440 | tf_op jit(solution)/shard_map/ppermute | solution.py:380
  14.9 12.6 %collective-permute-start.18 = (f32[128,512]{1,0:T(8,128)}, f32[128,512]{1,0:T(8,128)S(1)}, u32[]{:S(2)}, u32[]{:S(2)}) collective-permute-start(f32[128,512]{1,0:T(8,128)} %get-tuple-element.33.refs_1_), channel_id=1, source_target_pairs={{0,1},{4,5},{8,9},{12,13},{16,17},{20,21},{24,25},{28,29}} | collective-permute-start | bytes 786440 | tf_op jit(solution)/shard_map/ppermute | solution.py:380
  16.2 16.9 %collective-permute-start.19 = (f32[128,512]{1,0:T(8,128)}, f32[128,512]{1,0:T(8,128)S(1)}, u32[]{:S(2)}, u32[]{:S(2)}) collective-permute-start(f32[128,512]{1,0:T(8,128)} %get-tuple-element.34.refs_2_), channel_id=1, source_target_pairs={{0,1},{4,5},{8,9},{12,13},{16,17},{20,21},{24,25},{28,29}} | collective-permute-start | bytes 786440 | tf_op jit(solution)/shard_map/ppermute | solution.py:380
  17.5 21.2 %collective-permute-start.20 = (f32[128,512]{1,0:T(8,128)}, f32[128,512]{1,0:T(8,128)S(1)}, u32[]{:S(2)}, u32[]{:S(2)}) collective-permute-start(f32[128,512]{1,0:T(8,128)} %get-tuple-element.35.refs_3_), channel_id=1, source_target_pairs={{0,1},{4,5},{8,9},{12,13},{16,17},{20,21},{24,25},{28,29}} | collective-permute-start | bytes 786440 | tf_op jit(solution)/shard_map/ppermute | solution.py:380
  18.8 25.5 %collective-permute-start.21 = (f32[128,512]{1,0:T(8,128)}, f32[128,512]{1,0:T(8,128)S(1)}, u32[]{:S(2)}, u32[]{:S(2)}) collective-permute-start(f32[128,512]{1,0:T(8,128)} %get-tuple-element.36.refs_4_), channel_id=1, source_target_pairs={{0,1},{4,5},{8,9},{12,13},{16,17},{20,21},{24,25},{28,29}} | collective-permute-start | bytes 786440 | tf_op jit(solution)/shard_map/ppermute | solution.py:380
  21.9 28.1 %collective-permute-start.22 = (f32[128,512]{1,0:T(8,128)}, f32[128,512]{1,0:T(8,128)S(1)}, u32[]{:S(2)}, u32[]{:S(2)}) collective-permute-start(f32[128,512]{1,0:T(8,128)} %get-tuple-element.37.refs_5_), channel_id=1, source_target_pairs={{0,1},{4,5},{8,9},{12,13},{16,17},{20,21},{24,25},{28,29}} | collective-permute-start | bytes 786440 | tf_op jit(solution)/shard_map/ppermute | solution.py:380
  27.5 28.1 %collective-permute-start.35 = (f32[128,512]{1,0:T(8,128)}, f32[128,512]{1,0:T(8,128)S(1)}, u32[]{:S(2)}, u32[]{:S(2)}) collective-permute-start(f32[128,512]{1,0:T(8,128)} %get-tuple-element.38.refs_0_), channel_id=1, source_target_pairs={{0,1},{4,5},{8,9},{12,13},{16,17},{20,21},{24,25},{28,29}} | collective-permute-start | bytes 786440 | tf_op jit(solution)/shard_map/ppermute | solution.py:380
  33.1 27.0 %collective-permute-start.36 = (f32[128,512]{1,0:T(8,128)}, f32[128,512]{1,0:T(8,128)S(1)}, u32[]{:S(2)}, u32[]{:S(2)}) collective-permute-start(f32[128,512]{1,0:T(8,128)} %get-tuple-element.39.refs_1_), channel_id=1, source_target_pairs={{0,1},{4,5},{8,9},{12,13},{16,17},{20,21},{24,25},{28,29}} | collective-permute-start | bytes 786440 | tf_op jit(solution)/shard_map/ppermute | solution.py:380
  38.7 22.0 %collective-permute-start.23 = (f32[128,512]{1,0:T(8,128)S(1)}, f32[128,512]{1,0:T(8,128)S(1)}, u32[]{:S(2)}, u32[]{:S(2)}) collective-permute-start(f32[128,512]{1,0:T(8,128)S(1)} %collective-permute-done.17.refs_6_), channel_id=1, source_target_pairs={{1,2},{5,6},{9,10},{13,14},{17,18},{21,22},{25,26},{29,30}} | collective-permute-start | bytes 786440 | tf_op jit(solution)/shard_map/ppermute | solution.py:380
  44.4 17.1 %collective-permute-start.24 = (f32[128,512]{1,0:T(8,128)S(1)}, f32[128,512]{1,0:T(8,128)S(1)}, u32[]{:S(2)}, u32[]{:S(2)}) collective-permute-start(f32[128,512]{1,0:T(8,128)S(1)} %collective-permute-done.18.refs_7_), channel_id=1, source_target_pairs={{1,2},{5,6},{9,10},{13,14},{17,18},{21,22},{25,26},{29,30}} | collective-permute-start | bytes 786440 | tf_op jit(solution)/shard_map/ppermute | solution.py:380
  50.0 12.2 %collective-permute-start.25 = (f32[128,512]{1,0:T(8,128)S(1)}, f32[128,512]{1,0:T(8,128)S(1)}, u32[]{:S(2)}, u32[]{:S(2)}) collective-permute-start(f32[128,512]{1,0:T(8,128)S(1)} %collective-permute-done.19.refs_8_), channel_id=1, source_target_pairs={{1,2},{5,6},{9,10},{13,14},{17,18},{21,22},{25,26},{29,30}} | collective-permute-start | bytes 786440 | tf_op jit(solution)/shard_map/ppermute | solution.py:380
  55.6 7.2 %collective-permute-start.26 = (f32[128,512]{1,0:T(8,128)S(1)}, f32[128,512]{1,0:T(8,128)S(1)}, u32[]{:S(2)}, u32[]{:S(2)}) collective-permute-start(f32[128,512]{1,0:T(8,128)S(1)} %collective-permute-done.20.refs_9_), channel_id=1, source_target_pairs={{1,2},{5,6},{9,10},{13,14},{17,18},{21,22},{25,26},{29,30}} | collective-permute-start | bytes 786440 | tf_op jit(solution)/shard_map/ppermute | solution.py:380
  60.8 3.5 %collective-permute-start.28 = (f32[128,512]{1,0:T(8,128)S(1)}, f32[128,512]{1,0:T(8,128)S(1)}, u32[]{:S(2)}, u32[]{:S(2)}) collective-permute-start(f32[128,512]{1,0:T(8,128)S(1)} %collective-permute-done.22.refs_11_), channel_id=1, source_target_pairs={{1,2},{5,6},{9,10},{13,14},{17,18},{21,22},{25,26},{29,30}} | collective-permute-start | bytes 786440 | tf_op jit(solution)/shard_map/ppermute | solution.py:380
  67.0 16.0 %collective-permute-start = (f32[128,640]{1,0:T(8,128)}, f32[128,640]{1,0:T(8,128)S(1)}, u32[]{:S(2)}, u32[]{:S(2)}) collective-permute-start(f32[128,640]{1,0:T(8,128)} %get-tuple-element.29), channel_id=1, source_target_pairs={{0,4},{4,0},{8,12},{12,8},{16,20},{20,16},{24,28},{28,24},{1,5},{5... | collective-permute-start | bytes 983048 | tf_op jit(solution)/shard_map/ppermute | solution.py:384
  67.1 12.2 %collective-permute-start.39 = (f32[128,512]{1,0:T(8,128)S(1)}, f32[128,512]{1,0:T(8,128)S(1)}, u32[]{:S(2)}, u32[]{:S(2)}) collective-permute-start(f32[128,512]{1,0:T(8,128)S(1)} %collective-permute-done.37.refs_4_), channel_id=1, source_target_pairs={{2,3},{6,7},{10,11},{14,15},{18,19},{22,23},{26,27},{30,31}} | collective-permute-start | bytes 786440 | tf_op jit(solution)/shard_map/ppermute | solution.py:380
  67.8 11.6 %collective-permute-start.40 = (f32[128,512]{1,0:T(8,128)S(1)}, f32[128,512]{1,0:T(8,128)S(1)}, u32[]{:S(2)}, u32[]{:S(2)}) collective-permute-start(f32[128,512]{1,0:T(8,128)S(1)} %collective-permute-done.38.refs_5_), channel_id=1, source_target_pairs={{2,3},{6,7},{10,11},{14,15},{18,19},{22,23},{26,27},{30,31}} | collective-permute-start | bytes 786440 | tf_op jit(solution)/shard_map/ppermute | solution.py:380
  82.5 56.8 %collective-permute-start.41 = (f32[4,512,128]{2,1,0:T(8,128)S(1)}, f32[4,512,128]{2,1,0:T(8,128)S(1)}, u32[]{:S(2)}, u32[]{:S(2)}) collective-permute-start(f32[4,512,128]{2,1,0:T(8,128)S(1)} %get-tuple-element.41), channel_id=1, source_target_pairs={{0,4},{4,0},{8,12},{12,8},{16,20},{20,16},{24,28},{28,24},{1,5},{5... | collective-permute-start | bytes 3145736 | tf_op jit(solution)/shard_map/ppermute | solution.py:384
  83.1 6.2 %collective-permute-start.3 = (f32[64,640]{1,0:T(8,128)S(1)}, f32[64,640]{1,0:T(8,128)S(1)}, u32[]{:S(2)}, u32[]{:S(2)}) collective-permute-start(f32[64,640]{1,0:T(8,128)S(1)} %get-tuple-element.51), channel_id=1, source_target_pairs={{0,16},{4,20},{8,24},{12,28},{16,0},{20,4},{24,8},{28,12},{1,17},{... | collective-permute-start | bytes 491528 | tf_op jit(solution)/shard_map/ppermute | solution.py:384
  84.6 6.2 %collective-permute-start.1 = (f32[64,640]{1,0:T(8,128)S(1)}, f32[64,640]{1,0:T(8,128)S(1)}, u32[]{:S(2)}, u32[]{:S(2)}) collective-permute-start(f32[64,640]{1,0:T(8,128)S(1)} %get-tuple-element.52), channel_id=1, source_target_pairs={{0,8},{4,12},{8,0},{12,4},{16,24},{20,28},{24,16},{28,20},{1,9},{5... | collective-permute-start | bytes 491528 | tf_op jit(solution)/shard_map/ppermute | solution.py:384
  89.3 5.4 %collective-permute-start.4 = (f32[64,640]{1,0:T(8,128)S(1)}, f32[64,640]{1,0:T(8,128)S(1)}, u32[]{:S(2)}, u32[]{:S(2)}) collective-permute-start(f32[64,640]{1,0:T(8,128)S(1)} %add.35), channel_id=1, source_target_pairs={{0,8},{4,12},{8,0},{12,4},{16,24},{20,28},{24,16},{28,20},{1,9},{5... | collective-permute-start | bytes 491528 | tf_op jit(solution)/shard_map/ppermute | solution.py:384
  90.9 5.4 %collective-permute-start.2 = (f32[64,640]{1,0:T(8,128)S(1)}, f32[64,640]{1,0:T(8,128)S(1)}, u32[]{:S(2)}, u32[]{:S(2)}) collective-permute-start(f32[64,640]{1,0:T(8,128)S(1)} %add.32), channel_id=1, source_target_pairs={{0,16},{4,20},{8,24},{12,28},{16,0},{20,4},{24,8},{28,12},{1,17},{... | collective-permute-start | bytes 491528 | tf_op jit(solution)/shard_map/ppermute | solution.py:384
  122.1 20.0 %collective-permute-start.9 = (f32[32,640]{1,0:T(8,128)S(1)}, f32[32,640]{1,0:T(8,128)}, u32[]{:S(2)}, u32[]{:S(2)}) collective-permute-start(f32[32,640]{1,0:T(8,128)S(1)} %get-tuple-element.31), channel_id=1, source_target_pairs={{0,3},{4,7},{8,11},{12,15},{16,19},{20,23},{24,27},{28,31}} | collective-permute-start | bytes 245768 | tf_op jit(solution)/shard_map/ppermute | solution.py:380
  135.5 6.6 %collective-permute-start.8 = (f32[32,640]{1,0:T(8,128)S(1)}, f32[32,640]{1,0:T(8,128)}, u32[]{:S(2)}, u32[]{:S(2)}) collective-permute-start(f32[32,640]{1,0:T(8,128)S(1)} %get-tuple-element.31), channel_id=1, source_target_pairs={{0,2},{4,6},{8,10},{12,14},{16,18},{20,22},{24,26},{28,30}} | collective-permute-start | bytes 245768 | tf_op jit(solution)/shard_map/ppermute | solution.py:380
  137.4 4.7 %collective-permute-start.7 = (f32[32,640]{1,0:T(8,128)S(1)}, f32[32,640]{1,0:T(8,128)}, u32[]{:S(2)}, u32[]{:S(2)}) collective-permute-start(f32[32,640]{1,0:T(8,128)S(1)} %get-tuple-element.31), channel_id=1, source_target_pairs={{0,1},{4,5},{8,9},{12,13},{16,17},{20,21},{24,25},{28,29}} | collective-permute-start | bytes 245768 | tf_op jit(solution)/shard_map/ppermute | solution.py:380
  139.9 9.2 %collective-permute-start.42 = (f32[2,256,128]{2,1,0:T(8,128)S(1)}, f32[2,256,128]{2,1,0:T(8,128)S(1)}, u32[]{:S(2)}, u32[]{:S(2)}) collective-permute-start(f32[2,256,128]{2,1,0:T(8,128)S(1)} %get-tuple-element.43), channel_id=1, source_target_pairs={{0,8},{4,12},{8,0},{12,4},{16,24},{20,28},{24,16},{28,20},{1,9},{5... | collective-permute-start | bytes 786440 | tf_op jit(solution)/shard_map/ppermute | solution.py:384
  141.2 10.1 %collective-permute-start.44 = (f32[2,256,128]{2,1,0:T(8,128)S(1)}, f32[2,256,128]{2,1,0:T(8,128)S(1)}, u32[]{:S(2)}, u32[]{:S(2)}) collective-permute-start(f32[2,256,128]{2,1,0:T(8,128)S(1)} %get-tuple-element.47), channel_id=1, source_target_pairs={{0,16},{4,20},{8,24},{12,28},{16,0},{20,4},{24,8},{28,12},{1,17},{... | collective-permute-start | bytes 786440 | tf_op jit(solution)/shard_map/ppermute | solution.py:384
  143.1 10.1 %collective-permute-start.15 = (f32[32,640]{1,0:T(8,128)S(1)}, f32[32,640]{1,0:T(8,128)S(1)}, u32[]{:S(2)}, u32[]{:S(2)}) collective-permute-start(f32[32,640]{1,0:T(8,128)S(1)} %add_add_fusion.refs_0_), channel_id=1, source_target_pairs={{0,24},{4,28},{8,16},{12,20},{16,8},{20,12},{24,0},{28,4},{1,25},{... | collective-permute-start | bytes 245768 | tf_op jit(solution)/shard_map/ppermute | solution.py:384
  144.6 10.1 %collective-permute-start.13 = (f32[32,640]{1,0:T(8,128)S(1)}, f32[32,640]{1,0:T(8,128)S(1)}, u32[]{:S(2)}, u32[]{:S(2)}) collective-permute-start(f32[32,640]{1,0:T(8,128)S(1)} %add_add_fusion.refs_0_), channel_id=1, source_target_pairs={{0,16},{4,20},{8,24},{12,28},{16,0},{20,4},{24,8},{28,12},{1,17},{... | collective-permute-start | bytes 245768 | tf_op jit(solution)/shard_map/ppermute | solution.py:384
  146.1 8.6 %collective-permute-start.11 = (f32[32,640]{1,0:T(8,128)S(1)}, f32[32,640]{1,0:T(8,128)S(1)}, u32[]{:S(2)}, u32[]{:S(2)}) collective-permute-start(f32[32,640]{1,0:T(8,128)S(1)} %add_add_fusion.refs_0_), channel_id=1, source_target_pairs={{0,8},{4,12},{8,0},{12,4},{16,24},{20,28},{24,16},{28,20},{1,9},{5... | collective-permute-start | bytes 245768 | tf_op jit(solution)/shard_map/ppermute | solution.py:384
  149.2 6.0 %collective-permute-start.10 = (f32[32,640]{1,0:T(8,128)S(1)}, f32[32,640]{1,0:T(8,128)S(1)}, u32[]{:S(2)}, u32[]{:S(2)}) collective-permute-start(f32[32,640]{1,0:T(8,128)S(1)} %add_add_fusion.refs_0_), channel_id=1, source_target_pairs={{0,4},{4,0},{8,12},{12,8},{16,20},{20,16},{24,28},{28,24},{1,5},{5... | collective-permute-start | bytes 245768 | tf_op jit(solution)/shard_map/ppermute | solution.py:384
  151.3 5.2 %collective-permute-start.43 = (f32[1,256,128]{2,1,0:T(8,128)S(1)}, f32[1,256,128]{2,1,0:T(8,128)S(1)}, u32[]{:S(2)}, u32[]{:S(2)}) collective-permute-start(f32[1,256,128]{2,1,0:T(8,128)S(1)} %get-tuple-element.45), channel_id=1, source_target_pairs={{0,16},{4,20},{8,24},{12,28},{16,0},{20,4},{24,8},{28,12},{1,17},{... | collective-permute-start | bytes 393224 | tf_op jit(solution)/shard_map/ppermute | solution.py:384
  153.2 5.0 %collective-permute-start.45 = (f32[1,256,128]{2,1,0:T(8,128)S(1)}, f32[1,256,128]{2,1,0:T(8,128)S(1)}, u32[]{:S(2)}, u32[]{:S(2)}) collective-permute-start(f32[1,256,128]{2,1,0:T(8,128)S(1)} %get-tuple-element.49), channel_id=1, source_target_pairs={{0,8},{4,12},{8,0},{12,4},{16,24},{20,28},{24,16},{28,20},{1,9},{5... | collective-permute-start | bytes 393224 | tf_op jit(solution)/shard_map/ppermute | solution.py:384
  (27 other events, 139.0 us)

commit v4 on v3

--- a/solution.py
+++ b/solution.py
@@ -112,42 +112,45 @@
     count = len(edges) - 1
     pieces = refs[:count]
     keep_a, keep_b, send, panel, rows, ph, plo, qh, ql, rect, sems = refs[count:]
-    depth, width = panel.shape
-    nb, steps, tile = width // BLOCK, depth // tall, depth // mask_ref.shape[1]
-    copies = [pltpu.make_async_copy(coupling_hbm.at[:, pl.ds(0, width)], panel, sems.at[0])]
-    for i in range(steps):
-        copies.append(pltpu.make_async_copy(inverse_hbm.at[pl.ds(i * tall, tall)], rows.at[i], sems.at[1 + i]))
-    for copy in copies:
-        copy.start()
-    kept = [mask_ref[0, t].astype(jnp.float32) for t in range(depth // tile)]
-    copies[0].wait()
-    for t in range(depth // tile):
-        here = slice(t * tile, (t + 1) * tile)
-        ph[here, :], plo[here, :] = split(panel[here, :] * kept[t])
-    for i in range(steps):
-        copies[1 + i].wait()
-        value = three(split(rows[i]), (ph[...], plo[...]), ((1,), (0,)))
-        for t in range(i * tall // tile, (i + 1) * tall // tile):
-            part = value[t * tile - i * tall : (t + 1) * tile - i * tall, :] * kept[t]
+
+    @pl.when(place_ref[0] == 0)
+    def _():
+        depth, width = panel.shape
+        nb, steps, tile = width // BLOCK, depth // tall, depth // mask_ref.shape[1]
+        copies = [pltpu.make_async_copy(coupling_hbm.at[:, pl.ds(0, width)], panel, sems.at[0])]
+        for i in range(steps):
+            copies.append(pltpu.make_async_copy(inverse_hbm.at[pl.ds(i * tall, tall)], rows.at[i], sems.at[1 + i]))
+        for copy in copies:
+            copy.start()
+        kept = [mask_ref[0, t].astype(jnp.float32) for t in range(depth // tile)]
+        copies[0].wait()
+        for t in range(depth // tile):
             here = slice(t * tile, (t + 1) * tile)
-            qh[here, :], ql[here, :] = split(part)
-            for k in range(count):
-                lo, hi = max(edges[k], t * tile), min(edges[k + 1], (t + 1) * tile)
-                if lo < hi:
-                    pieces[k][lo - edges[k] : hi - edges[k], :] = part[lo - t * tile : hi - t * tile, :]
-    for i, block, low in strips(nb):
-        wide = (block + 1) * BLOCK
-        mine = slice(block * BLOCK, wide)
-        rect[i * BLOCK : (i + 1) * BLOCK, low : low + wide] = three(
-            (ph[:, mine], plo[:, mine]), (qh[:, :wide], ql[:, :wide]), ((0,), (0,))
-        )
-    half = rect.shape[0] // 2
-    core = place_ref[1] & 1
-    mine = pl.multiple_of(core * half, half)
-    theirs = pl.multiple_of((1 - core) * half, half)
-    keep_a[...] = rect[pl.ds(mine, half // 2), :]
-    keep_b[...] = rect[pl.ds(mine + half // 2, half // 2), :]
-    send[...] = rect[pl.ds(theirs, half), :]
+            ph[here, :], plo[here, :] = split(panel[here, :] * kept[t])
+        for i in range(steps):
+            copies[1 + i].wait()
+            value = three(split(rows[i]), (ph[...], plo[...]), ((1,), (0,)))
+            for t in range(i * tall // tile, (i + 1) * tall // tile):
+                part = value[t * tile - i * tall : (t + 1) * tile - i * tall, :] * kept[t]
+                here = slice(t * tile, (t + 1) * tile)
+                qh[here, :], ql[here, :] = split(part)
+                for k in range(count):
+                    lo, hi = max(edges[k], t * tile), min(edges[k + 1], (t + 1) * tile)
+                    if lo < hi:
+                        pieces[k][lo - edges[k] : hi - edges[k], :] = part[lo - t * tile : hi - t * tile, :]
+        for i, block, low in strips(nb):
+            wide = (block + 1) * BLOCK
+            mine = slice(block * BLOCK, wide)
+            rect[i * BLOCK : (i + 1) * BLOCK, low : low + wide] = three(
+                (ph[:, mine], plo[:, mine]), (qh[:, :wide], ql[:, :wide]), ((0,), (0,))
+            )
+        half = rect.shape[0] // 2
+        core = place_ref[1] & 1
+        mine = pl.multiple_of(core * half, half)
+        theirs = pl.multiple_of((1 - core) * half, half)
+        keep_a[...] = rect[pl.ds(mine, half // 2), :]
+        keep_b[...] = rect[pl.ds(mine + half // 2, half // 2), :]
+        send[...] = rect[pl.ds(theirs, half), :]
 
 
 def product(place, mask, inverse, coupling, width, edges):
@@ -271,33 +274,38 @@
                 if k == block:
                     part = jnp.where(col <= row, part, part.T)
                     part = part + jnp.where(col == row, diag_ref[:, here], 0.0)
-                else:
-                    w_ref[there, here] = part.T
                 w_ref[here, there] = part
 
-        def step(j, carry):
-            low = pl.multiple_of(j * BLOCK, BLOCK)
-            mine = pl.ds(low, BLOCK)
-            tiles = [w_ref[pl.ds(low + SUB * t, SUB), mine] for t in range(BLOCK // SUB)]
-            scaled, scales = eliminate(tiles)
+        def nt(left, right):
+            return full(left, right, ((1,), (1,)))
+
+        def nn(left, right):
+            return full(left, right, ((1,), (0,)))
+
+        for j in range(nb):
+            low, top = j * BLOCK, (j + 1) * BLOCK
+            mine = slice(low, top)
+            scaled, scales = eliminate([w_ref[low + SUB * t : low + SUB * (t + 1), mine] for t in range(BLOCK // SUB)])
             for t in range(BLOCK // SUB):
                 base_ref[SUB * t : SUB * t + SUB, :] = scaled[t]
                 scale_ref[SUB * t : SUB * t + SUB, :] = scales[t]
             both = base_ref[...]
             inverse = jnp.where(col < row, both, jnp.where(col == row, scale_ref[...], 0.0))
-            factor_t = jnp.where(col >= row, both, 0.0)
-            below = lax.broadcasted_iota(jnp.int32, (size, BLOCK), 0) >= low + BLOCK
-            panel = jnp.where(below, full(w_ref[:, mine], inverse, ((1,), (1,))), 0.0)
-            w_ref[mine, :] = full(inverse, w_ref[mine, :], ((1,), (0,)))
+            l_ref[mine, mine] = jnp.where(col >= row, both, 0.0).T
+            if top < size:
+                l_ref[mine, top:] = jnp.zeros((BLOCK, size - top), jnp.float32)
+            if j:
+                w_ref[mine, :low] = nn(inverse, w_ref[mine, :low])
             w_ref[mine, mine] = inverse
-            pivot_rows = w_ref[mine, :]
-            w_ref[:, mine] = jnp.where(below, 0.0, w_ref[:, mine])
-            w_ref[...] = w_ref[...] - full(panel, pivot_rows, ((1,), (0,)))
-            l_ref[:, mine] = panel
-            l_ref[mine, mine] = factor_t.T
-            return carry
-
-        lax.fori_loop(0, nb, step, 0)
+            if top < size:
+                panel = nt(w_ref[top:, mine], inverse)
+                l_ref[top:, mine] = panel
+                for k in range(j + 1, nb):
+                    here, skip = slice(k * BLOCK, (k + 1) * BLOCK), (k - j - 1) * BLOCK
+                    w_ref[k * BLOCK :, here] = w_ref[k * BLOCK :, here] - nt(panel[skip:], panel[skip : skip + BLOCK])
+                if j:
+                    w_ref[top:, :low] = w_ref[top:, :low] - nn(panel, w_ref[mine, :low])
+                w_ref[top:, mine] = -nn(panel, inverse)
         for i, block, low in strips(nb):
             for k in range(block + 1):
                 rect_ref[i * BLOCK : (i + 1) * BLOCK, low + k * BLOCK : low + (k + 1) * BLOCK] = w_ref[
@@ -307,7 +315,7 @@
         first = jnp.minimum(place_ref[2], size - rows)
         own_ref[...] = l_ref[pl.ds(pl.multiple_of(first, rows), rows), :]
         each = piece_ref.shape[0]
-        piece_ref[...] = rect_ref[pl.ds(pl.multiple_of(me * each, each), each), :]
+        piece_ref[...] = rect_ref[pl.ds(pl.multiple_of((me >> 1) * each, each), each), :]
 
 
 def factor(place, parts, diag, each, rows):
@@ -346,7 +354,7 @@
         rows_ref[:half, :] = keep_a[...] + got_a[...]
         rows_ref[half:, :] = keep_b[...] + got_b[...]
     for m in range(count):
-        rect_ref[pl.ds(pl.multiple_of((me ^ m) * each, each), each), :] = pieces[m][...]
+        rect_ref[pl.ds(pl.multiple_of(((me >> 1) ^ m) * each, each), each), :] = pieces[m][...]
     for i, block, low in strips(nb):
         wide = (block + 1) * BLOCK
         part = rect_ref[i * BLOCK : (i + 1) * BLOCK, low : low + wide]
@@ -354,7 +362,7 @@
             [part[:, : wide - BLOCK], jnp.where(
                 lax.broadcasted_iota(jnp.int32, (BLOCK, BLOCK), 1) <= lax.broadcasted_iota(jnp.int32, (BLOCK, BLOCK), 0),
                 part[:, wide - BLOCK :], 0.0)], axis=1) if wide > BLOCK else part
-        out_ref[:, block * BLOCK : (block + 1) * BLOCK] = full(rows_ref[:, :wide], part, ((1,), (1,)))
+        out_ref[:, block * BLOCK : (block + 1) * BLOCK] = three(split(rows_ref[:, :wide]), split(part), ((1,), (1,)))
 
     @pl.when(first < width)
     def _():
@@ -472,14 +480,13 @@
         got_b = exchange(b, 1 << q, scen)
         a, b = a + got_a, b + got_b
     parts = (a, b, exchange(a, 1, scen), exchange(b, 1, scen))
-    each = width // BLOCK // 2 * BLOCK // scen
+    each = width // BLOCK // 2 * BLOCK // (scen // 2)
     lower, piece = factor(place, parts, hess_diag[None, :], each, rows)
 
     mine = jnp.where(plane == 0, piece, 0.0)
     for h in range(1, planes):
         mine = mine + hop(piece, 0, h)
     pieces = [mine if m == 0 else exchange(mine, m, scen) for m in range(0, scen, 2)]
-    pieces = [p for m in range(0, scen, 2) for p in (pieces[m // 2], exchange(pieces[m // 2], 1, scen))]
 
     cut = PIECES - LATE
     early = edge[cut]

time: 161 us -> 161 us (level)
  waiting for transfers between devices: 39.6 us -> 44.4 us
  Pallas kernels: 40.2 us -> 38.3 us
  starting transfers between devices: 67 us -> 65.1 us
    ppermute x27, waiting for transfers between devices: 24.4 us -> 30.7 us  [hop(): return lax.ppermute(x, 'col', [(source, target)])]
    pallas_call x1, Pallas kernels: 24.4 us -> 21.2 us  [factor(): pl.pallas_call(factor_kernel, out_shape=(shape(rows, size), shape(each, w...]
    ppermute x27, starting transfers between devices: 51 us -> 49.2 us  [hop(): return lax.ppermute(x, 'col', [(source, target)])]
    ppermute x19 -> x15, waiting for transfers between devices: 15.3 us -> 13.7 us  [exchange(): return lax.ppermute(x, 'scen', [(i, i ^ mask) for i in range(count)])]
    ppermute x19 -> x15, starting transfers between devices: 16 us -> 15.9 us  [exchange(): return lax.ppermute(x, 'scen', [(i, i ^ mask) for i in range(count)])]
  transfers between devices with their start and end apart: 46 -> 42, of which waited for: 18 -> 19; matrix products, arithmetic and copies ran while one was open for 3% -> 3% of each run, Pallas kernels for 18% -> 17%
where the time goes in v4:
time: 161 us; the launch traced here: 160 us
  starting transfers between devices  65.1 us (40%)
  waiting for transfers between devices  44.4 us (28%)
  Pallas kernels  38.3 us (24%)
  local copies, waits for them, and re-layouts  7.16 us (4%)
  matrix products  4.02 us (2%)
    ppermute x27, starting transfers between devices, hop(): return lax.ppermute(x, 'col', [(source, target)])  49.2 us
    ppermute x27, waiting for transfers between devices, hop(): return lax.ppermute(x, 'col', [(source, target)])  30.7 us
    pallas_call x1, Pallas kernels, factor(): pl.pallas_call(factor_kernel, out_shape=(shape(rows, size), shape(each, w...  21.2 us
    ppermute x15, starting transfers between devices, exchange(): return lax.ppermute(x, 'scen', [(i, i ^ mask) for i in range(count)])  15.9 us
    ppermute x15, waiting for transfers between devices, exchange(): return lax.ppermute(x, 'scen', [(i, i ^ mask) for i in range(count)])  13.7 us
    pallas_call x1, Pallas kernels, product(): pl.pallas_call(functools.partial(product_kernel, edges, tall), out_shape=...  10.1 us
    unnamed x26, local copies, waits for them, and re-layouts  7.16 us
    dot_general x2, matrix products, high(): lax.dot_general(left, right, (dims, ((), ())), precision=lax.Precision.HI...  4.02 us
  transfers between devices with their start and end apart: 42, of which 19 were waited for; matrix products, arithmetic and copies ran while one was open for 3% of the time, Pallas kernels for 17%

profile of v4, /device:TPU:0, one launch (start us, length us, event | category | flops | bytes accessed | tf_op | source)
XLA Modules:
  0.0 160.3 jit_solution(639472898885874538)
XLA Ops:
  0.6 10.1 %shard_map.46 = (f32[128,512]{1,0:T(8,128)}, f32[128,512]{1,0:T(8,128)}, f32[128,512]{1,0:T(8,128)}, f32[128,512]{1,0:T(8,128)}, f32[128,512]{1,0:T(8,128)}, /*i...) custom-call(s32[3]{0:T(128)} %pad_add_fusion.place_ref, ...), custom_call_target="tpu_custom_call" | custom-call | flops 4831838208 | bytes 8388608 | tf_op jit(solution)/shard_map/pallas_call | solution.py:160
  10.7 1.3 collective-permute-start.13
  17.2 1.7 %collective-permute-done.13.refs_6_ = f32[128,512]{1,0:T(8,128)S(1)} collective-permute-done((f32[128,512]{1,0:T(8,128)}, f32[128,512]{1,0:T(8,128)S(1)}, u32[]{:S(2)}, u32[]{:S(2)}) %collective-permute-start.13) | collective-permute-done | bytes 262176 | tf_op jit(solution)/shard_map/ppermute | solution.py:388
  19.0 4.3 %collective-permute-start.18 = (f32[128,512]{1,0:T(8,128)}, f32[128,512]{1,0:T(8,128)S(1)}, u32[]{:S(2)}, u32[]{:S(2)}) collective-permute-start(f32[128,512]{1,0:T(8,128)} %get-tuple-element.37.refs_5_), channel_id=1, source_target_pairs={{0,1},{4,5},{8,9},{12,13},{16,17},{20,21},{24,25},{28,29}} | collective-permute-start | bytes 786440 | tf_op jit(solution)/shard_map/ppermute | solution.py:388
  23.3 1.3 collective-permute-done.14.refs_7_
  24.6 4.3 %collective-permute-start.31 = (f32[128,512]{1,0:T(8,128)}, f32[128,512]{1,0:T(8,128)S(1)}, u32[]{:S(2)}, u32[]{:S(2)}) collective-permute-start(f32[128,512]{1,0:T(8,128)} %get-tuple-element.38.refs_0_), channel_id=1, source_target_pairs={{0,1},{4,5},{8,9},{12,13},{16,17},{20,21},{24,25},{28,29}} | collective-permute-start | bytes 786440 | tf_op jit(solution)/shard_map/ppermute | solution.py:388
  28.9 1.3 collective-permute-done.15.refs_8_
  30.2 4.3 %collective-permute-start.32 = (f32[128,512]{1,0:T(8,128)}, f32[128,512]{1,0:T(8,128)S(1)}, u32[]{:S(2)}, u32[]{:S(2)}) collective-permute-start(f32[128,512]{1,0:T(8,128)} %get-tuple-element.39.refs_1_), channel_id=1, source_target_pairs={{0,1},{4,5},{8,9},{12,13},{16,17},{20,21},{24,25},{28,29}} | collective-permute-start | bytes 786440 | tf_op jit(solution)/shard_map/ppermute | solution.py:388
  34.5 1.3 collective-permute-done.16.refs_9_
  36.5 4.9 %collective-permute-done.17.refs_10_ = f32[128,512]{1,0:T(8,128)S(1)} collective-permute-done((f32[128,512]{1,0:T(8,128)}, f32[128,512]{1,0:T(8,128)S(1)}, u32[]{:S(2)}, u32[]{:S(2)}) %collective-permute-start.17) | collective-permute-done | bytes 262176 | tf_op jit(solution)/shard_map/ppermute | solution.py:388
  42.1 4.9 %collective-permute-done.18.refs_11_ = f32[128,512]{1,0:T(8,128)S(1)} collective-permute-done((f32[128,512]{1,0:T(8,128)}, f32[128,512]{1,0:T(8,128)S(1)}, u32[]{:S(2)}, u32[]{:S(2)}) %collective-permute-start.18) | collective-permute-done | bytes 262176 | tf_op jit(solution)/shard_map/ppermute | solution.py:388
  47.7 4.9 %collective-permute-done.31.refs_2_ = f32[128,512]{1,0:T(8,128)S(1)} collective-permute-done((f32[128,512]{1,0:T(8,128)}, f32[128,512]{1,0:T(8,128)S(1)}, u32[]{:S(2)}, u32[]{:S(2)}) %collective-permute-start.31) | collective-permute-done | bytes 262176 | tf_op jit(solution)/shard_map/ppermute | solution.py:388
  53.3 4.8 %collective-permute-done.32.refs_3_ = f32[128,512]{1,0:T(8,128)S(1)} collective-permute-done((f32[128,512]{1,0:T(8,128)}, f32[128,512]{1,0:T(8,128)S(1)}, u32[]{:S(2)}, u32[]{:S(2)}) %collective-permute-start.32) | collective-permute-done | bytes 262176 | tf_op jit(solution)/shard_map/ppermute | solution.py:388
  73.0 1.4 copy-done.10
  74.5 2.9 %fusion.first_ref = f32[512,1024]{1,0:T(8,128)S(1)} fusion(f32[768,512]{1,0:T(8,128)S(1)} %shard_map.48, f32[1,1024,1024]{2,1,0:T(8,128)S(1)} %copy-done.10), kind=kOutput, calls=%fused_computation | convolution fusion | flops 2415919104 | bytes 6815744 | tf_op jit(solution)/shard_map/dot_general | solution.py:16
  79.2 2.1 %shard_map.50 = (f32[4,512,128]{2,1,0:T(8,128)S(1)}, f32[4,512,128]{2,1,0:T(8,128)}) custom-call(s32[3]{0:T(128)S(1)} %copy-done.8, f32[512,1024]{1,0:T(8,128)S(1)} %fusion.first_ref, f32[512,1024]{1,0:T(8,128)S(1)} %fusion.3.second_ref), custom_call_target="tpu_custom_call" | custom-call | flops 524288 | bytes 6291456 | tf_op jit(solution)/shard_map/pallas_call | solution.py:218
  81.9 2.4 %collective-permute-start.3 = (f32[64,640]{1,0:T(8,128)S(1)}, f32[64,640]{1,0:T(8,128)S(1)}, u32[]{:S(2)}, u32[]{:S(2)}) collective-permute-start(f32[64,640]{1,0:T(8,128)S(1)} %get-tuple-element.51), channel_id=1, source_target_pairs={{0,16},{4,20},{8,24},{12,28},{16,0},{20,4},{24,8},{28,12},{1,17},{... | collective-permute-start | bytes 491528 | tf_op jit(solution)/shard_map/ppermute | solution.py:392
  84.3 1.5 collective-permute-start.1
  85.8 2.9 %collective-permute-done.3 = f32[64,640]{1,0:T(8,128)S(1)} collective-permute-done((f32[64,640]{1,0:T(8,128)S(1)}, f32[64,640]{1,0:T(8,128)S(1)}, u32[]{:S(2)}, u32[]{:S(2)}) %collective-permute-start.3) | collective-permute-done | bytes 163872 | tf_op jit(solution)/shard_map/ppermute | solution.py:392
  88.7 1.8 %collective-permute-start.4 = (f32[64,640]{1,0:T(8,128)S(1)}, f32[64,640]{1,0:T(8,128)S(1)}, u32[]{:S(2)}, u32[]{:S(2)}) collective-permute-start(f32[64,640]{1,0:T(8,128)S(1)} %add.35), channel_id=1, source_target_pairs={{0,8},{4,12},{8,0},{12,4},{16,24},{20,28},{24,16},{28,20},{1,9},{5... | collective-permute-start | bytes 491528 | tf_op jit(solution)/shard_map/ppermute | solution.py:392
  90.5 1.6 collective-permute-start.2
  92.1 2.2 %collective-permute-done.4 = f32[64,640]{1,0:T(8,128)S(1)} collective-permute-done((f32[64,640]{1,0:T(8,128)S(1)}, f32[64,640]{1,0:T(8,128)S(1)}, u32[]{:S(2)}, u32[]{:S(2)}) %collective-permute-start.4) | collective-permute-done | bytes 163872 | tf_op jit(solution)/shard_map/ppermute | solution.py:392
  94.4 1.4 collective-permute-done.2
  96.0 1.4 collective-permute-done.5.other_a
  97.4 21.2 %shard_map.47 = (f32[128,512]{1,0:T(8,128)S(1)}, f32[64,640]{1,0:T(8,128)S(1)}) custom-call(s32[3]{0:T(128)S(1)} %copy-done.8, f32[64,640]{1,0:T(8,128)S(1)} %add.33.own_a, f32[64,640]{1,0:T(8,128)S(1)} %add.36.own_b, f32[64,640]{1,0:T(8,128)S(1)} %collective-permute-done.5.other_a, f32[64,640]{1,0:T(8,128)S(1)} %collective-permute-done.6.other_b, ...), custom_call_target="tpu_custom_call" | custom-call | flops 2684354560 | bytes 3145728 | tf_op jit(solution)/shard_map/pallas_call | solution.py:325
  118.5 16.4 %collective-permute-start.9 = (f32[64,640]{1,0:T(8,128)S(1)}, f32[64,640]{1,0:T(8,128)S(1)}, u32[]{:S(2)}, u32[]{:S(2)}) collective-permute-start(f32[64,640]{1,0:T(8,128)S(1)} %get-tuple-element.31), channel_id=1, source_target_pairs={{0,3},{4,7},{8,11},{12,15},{16,19},{20,23},{24,27},{28,31}} | collective-permute-start | bytes 491528 | tf_op jit(solution)/shard_map/ppermute | solution.py:388
  140.4 2.7 %collective-permute-done.8 = f32[64,640]{1,0:T(8,128)S(1)} collective-permute-done((f32[64,640]{1,0:T(8,128)S(1)}, f32[64,640]{1,0:T(8,128)S(1)}, u32[]{:S(2)}, u32[]{:S(2)}) %collective-permute-start.8) | collective-permute-done | bytes 163872 | tf_op jit(solution)/shard_map/ppermute | solution.py:388
  143.0 2.7 %collective-permute-done.7 = f32[64,640]{1,0:T(8,128)S(1)} collective-permute-done((f32[64,640]{1,0:T(8,128)S(1)}, f32[64,640]{1,0:T(8,128)S(1)}, u32[]{:S(2)}, u32[]{:S(2)}) %collective-permute-start.7) | collective-permute-done | bytes 163872 | tf_op jit(solution)/shard_map/ppermute | solution.py:388
  145.8 1.7 %collective-permute-start.12 = (f32[64,640]{1,0:T(8,128)S(1)}, f32[64,640]{1,0:T(8,128)S(1)}, u32[]{:S(2)}, u32[]{:S(2)}) collective-permute-start(f32[64,640]{1,0:T(8,128)S(1)} %add_add_fusion.refs_0_), channel_id=1, source_target_pairs={{0,24},{4,28},{8,16},{12,20},{16,8},{20,12},{24,0},{28,4},{1,25},{... | collective-permute-start | bytes 491528 | tf_op jit(solution)/shard_map/ppermute | solution.py:392
  149.9 1.6 collective-permute-start.39
  153.8 2.1 %collective-permute-done.11.refs_2_ = f32[64,640]{1,0:T(8,128)S(1)} collective-permute-done((f32[64,640]{1,0:T(8,128)S(1)}, f32[64,640]{1,0:T(8,128)S(1)}, u32[]{:S(2)}, u32[]{:S(2)}) %collective-permute-start.11) | collective-permute-done | bytes 163872 | tf_op jit(solution)/shard_map/ppermute | solution.py:392
  158.6 1.8 %shard_map.54 = f32[128,512]{1,0:T(8,128)} custom-call(s32[3]{0:T(128)S(1)} %copy-done.8, f32[64,640]{1,0:T(8,128)S(1)} %add_add_fusion.refs_0_, f32[64,640]{1,0:T(8,128)S(1)} %collective-permute-done.10.refs_1_, f32[64,640]{1,0:T(8,128)S(1)} %collective-permute-done.11.refs_2_, f32[64,640]{1,0:T(8,128)S(1)} %collective-permute-done.12.refs_3_, ...), custom_call_target="tpu_custom_call" | custom-call | flops 201326592 | bytes 2097152 | tf_op jit(solution)/shard_map/pallas_call | solution.py:376
  (96 shorter events, 38.5 us)
Async XLA Ops:
  10.7 8.3 %collective-permute-start.13 = (f32[128,512]{1,0:T(8,128)}, f32[128,512]{1,0:T(8,128)S(1)}, u32[]{:S(2)}, u32[]{:S(2)}) collective-permute-start(f32[128,512]{1,0:T(8,128)} %get-tuple-element.32.refs_0_), channel_id=1, source_target_pairs={{0,1},{4,5},{8,9},{12,13},{16,17},{20,21},{24,25},{28,29}} | collective-permute-start | bytes 786440 | tf_op jit(solution)/shard_map/ppermute | solution.py:388
  12.0 12.6 %collective-permute-start.14 = (f32[128,512]{1,0:T(8,128)}, f32[128,512]{1,0:T(8,128)S(1)}, u32[]{:S(2)}, u32[]{:S(2)}) collective-permute-start(f32[128,512]{1,0:T(8,128)} %get-tuple-element.33.refs_1_), channel_id=1, source_target_pairs={{0,1},{4,5},{8,9},{12,13},{16,17},{20,21},{24,25},{28,29}} | collective-permute-start | bytes 786440 | tf_op jit(solution)/shard_map/ppermute | solution.py:388
  13.3 16.9 %collective-permute-start.15 = (f32[128,512]{1,0:T(8,128)}, f32[128,512]{1,0:T(8,128)S(1)}, u32[]{:S(2)}, u32[]{:S(2)}) collective-permute-start(f32[128,512]{1,0:T(8,128)} %get-tuple-element.34.refs_2_), channel_id=1, source_target_pairs={{0,1},{4,5},{8,9},{12,13},{16,17},{20,21},{24,25},{28,29}} | collective-permute-start | bytes 786440 | tf_op jit(solution)/shard_map/ppermute | solution.py:388
  14.6 21.2 %collective-permute-start.16 = (f32[128,512]{1,0:T(8,128)}, f32[128,512]{1,0:T(8,128)S(1)}, u32[]{:S(2)}, u32[]{:S(2)}) collective-permute-start(f32[128,512]{1,0:T(8,128)} %get-tuple-element.35.refs_3_), channel_id=1, source_target_pairs={{0,1},{4,5},{8,9},{12,13},{16,17},{20,21},{24,25},{28,29}} | collective-permute-start | bytes 786440 | tf_op jit(solution)/shard_map/ppermute | solution.py:388
  15.9 25.5 %collective-permute-start.17 = (f32[128,512]{1,0:T(8,128)}, f32[128,512]{1,0:T(8,128)S(1)}, u32[]{:S(2)}, u32[]{:S(2)}) collective-permute-start(f32[128,512]{1,0:T(8,128)} %get-tuple-element.36.refs_4_), channel_id=1, source_target_pairs={{0,1},{4,5},{8,9},{12,13},{16,17},{20,21},{24,25},{28,29}} | collective-permute-start | bytes 786440 | tf_op jit(solution)/shard_map/ppermute | solution.py:388
  19.0 28.1 %collective-permute-start.18 = (f32[128,512]{1,0:T(8,128)}, f32[128,512]{1,0:T(8,128)S(1)}, u32[]{:S(2)}, u32[]{:S(2)}) collective-permute-start(f32[128,512]{1,0:T(8,128)} %get-tuple-element.37.refs_5_), channel_id=1, source_target_pairs={{0,1},{4,5},{8,9},{12,13},{16,17},{20,21},{24,25},{28,29}} | collective-permute-start | bytes 786440 | tf_op jit(solution)/shard_map/ppermute | solution.py:388
  24.6 28.1 %collective-permute-start.31 = (f32[128,512]{1,0:T(8,128)}, f32[128,512]{1,0:T(8,128)S(1)}, u32[]{:S(2)}, u32[]{:S(2)}) collective-permute-start(f32[128,512]{1,0:T(8,128)} %get-tuple-element.38.refs_0_), channel_id=1, source_target_pairs={{0,1},{4,5},{8,9},{12,13},{16,17},{20,21},{24,25},{28,29}} | collective-permute-start | bytes 786440 | tf_op jit(solution)/shard_map/ppermute | solution.py:388
  30.2 27.9 %collective-permute-start.32 = (f32[128,512]{1,0:T(8,128)}, f32[128,512]{1,0:T(8,128)S(1)}, u32[]{:S(2)}, u32[]{:S(2)}) collective-permute-start(f32[128,512]{1,0:T(8,128)} %get-tuple-element.39.refs_1_), channel_id=1, source_target_pairs={{0,1},{4,5},{8,9},{12,13},{16,17},{20,21},{24,25},{28,29}} | collective-permute-start | bytes 786440 | tf_op jit(solution)/shard_map/ppermute | solution.py:388
  35.8 23.0 %collective-permute-start.19 = (f32[128,512]{1,0:T(8,128)S(1)}, f32[128,512]{1,0:T(8,128)S(1)}, u32[]{:S(2)}, u32[]{:S(2)}) collective-permute-start(f32[128,512]{1,0:T(8,128)S(1)} %collective-permute-done.13.refs_6_), channel_id=1, source_target_pairs={{1,2},{5,6},{9,10},{13,14},{17,18},{21,22},{25,26},{29,30}} | collective-permute-start | bytes 786440 | tf_op jit(solution)/shard_map/ppermute | solution.py:388
  41.4 18.0 %collective-permute-start.20 = (f32[128,512]{1,0:T(8,128)S(1)}, f32[128,512]{1,0:T(8,128)S(1)}, u32[]{:S(2)}, u32[]{:S(2)}) collective-permute-start(f32[128,512]{1,0:T(8,128)S(1)} %collective-permute-done.14.refs_7_), channel_id=1, source_target_pairs={{1,2},{5,6},{9,10},{13,14},{17,18},{21,22},{25,26},{29,30}} | collective-permute-start | bytes 786440 | tf_op jit(solution)/shard_map/ppermute | solution.py:388
  47.1 13.1 %collective-permute-start.21 = (f32[128,512]{1,0:T(8,128)S(1)}, f32[128,512]{1,0:T(8,128)S(1)}, u32[]{:S(2)}, u32[]{:S(2)}) collective-permute-start(f32[128,512]{1,0:T(8,128)S(1)} %collective-permute-done.15.refs_8_), channel_id=1, source_target_pairs={{1,2},{5,6},{9,10},{13,14},{17,18},{21,22},{25,26},{29,30}} | collective-permute-start | bytes 786440 | tf_op jit(solution)/shard_map/ppermute | solution.py:388
  52.7 8.2 %collective-permute-start.22 = (f32[128,512]{1,0:T(8,128)S(1)}, f32[128,512]{1,0:T(8,128)S(1)}, u32[]{:S(2)}, u32[]{:S(2)}) collective-permute-start(f32[128,512]{1,0:T(8,128)S(1)} %collective-permute-done.16.refs_9_), channel_id=1, source_target_pairs={{1,2},{5,6},{9,10},{13,14},{17,18},{21,22},{25,26},{29,30}} | collective-permute-start | bytes 786440 | tf_op jit(solution)/shard_map/ppermute | solution.py:388
  59.5 3.5 %collective-permute-start.33 = (f32[128,512]{1,0:T(8,128)S(1)}, f32[128,512]{1,0:T(8,128)S(1)}, u32[]{:S(2)}, u32[]{:S(2)}) collective-permute-start(f32[128,512]{1,0:T(8,128)S(1)} %collective-permute-done.31.refs_2_), channel_id=1, source_target_pairs={{1,2},{5,6},{9,10},{13,14},{17,18},{21,22},{25,26},{29,30}} | collective-permute-start | bytes 786440 | tf_op jit(solution)/shard_map/ppermute | solution.py:388
  60.9 3.5 %collective-permute-start.25 = (f32[128,512]{1,0:T(8,128)S(1)}, f32[128,512]{1,0:T(8,128)S(1)}, u32[]{:S(2)}, u32[]{:S(2)}) collective-permute-start(f32[128,512]{1,0:T(8,128)S(1)} %collective-permute-done.19.refs_12_), channel_id=1, source_target_pairs={{2,3},{6,7},{10,11},{14,15},{18,19},{22,23},{26,27},{30,31}} | collective-permute-start | bytes 786440 | tf_op jit(solution)/shard_map/ppermute | solution.py:388
  65.1 16.8 %collective-permute-start = (f32[128,640]{1,0:T(8,128)}, f32[128,640]{1,0:T(8,128)S(1)}, u32[]{:S(2)}, u32[]{:S(2)}) collective-permute-start(f32[128,640]{1,0:T(8,128)} %get-tuple-element.29), channel_id=1, source_target_pairs={{0,4},{4,0},{8,12},{12,8},{16,20},{20,16},{24,28},{28,24},{1,5},{5... | collective-permute-start | bytes 983048 | tf_op jit(solution)/shard_map/ppermute | solution.py:392
  65.1 12.2 %collective-permute-start.35 = (f32[128,512]{1,0:T(8,128)S(1)}, f32[128,512]{1,0:T(8,128)S(1)}, u32[]{:S(2)}, u32[]{:S(2)}) collective-permute-start(f32[128,512]{1,0:T(8,128)S(1)} %collective-permute-done.33.refs_4_), channel_id=1, source_target_pairs={{2,3},{6,7},{10,11},{14,15},{18,19},{22,23},{26,27},{30,31}} | collective-permute-start | bytes 786440 | tf_op jit(solution)/shard_map/ppermute | solution.py:388
  65.8 11.6 %collective-permute-start.36 = (f32[128,512]{1,0:T(8,128)S(1)}, f32[128,512]{1,0:T(8,128)S(1)}, u32[]{:S(2)}, u32[]{:S(2)}) collective-permute-start(f32[128,512]{1,0:T(8,128)S(1)} %collective-permute-done.34.refs_5_), channel_id=1, source_target_pairs={{2,3},{6,7},{10,11},{14,15},{18,19},{22,23},{26,27},{30,31}} | collective-permute-start | bytes 786440 | tf_op jit(solution)/shard_map/ppermute | solution.py:388
  81.3 56.3 %collective-permute-start.37 = (f32[4,512,128]{2,1,0:T(8,128)}, f32[4,512,128]{2,1,0:T(8,128)S(1)}, u32[]{:S(2)}, u32[]{:S(2)}) collective-permute-start(f32[4,512,128]{2,1,0:T(8,128)} %get-tuple-element.41), channel_id=1, source_target_pairs={{0,4},{4,0},{8,12},{12,8},{16,20},{20,16},{24,28},{28,24},{1,5},{5... | collective-permute-start | bytes 3145736 | tf_op jit(solution)/shard_map/ppermute | solution.py:392
  81.9 6.8 %collective-permute-start.3 = (f32[64,640]{1,0:T(8,128)S(1)}, f32[64,640]{1,0:T(8,128)S(1)}, u32[]{:S(2)}, u32[]{:S(2)}) collective-permute-start(f32[64,640]{1,0:T(8,128)S(1)} %get-tuple-element.51), channel_id=1, source_target_pairs={{0,16},{4,20},{8,24},{12,28},{16,0},{20,4},{24,8},{28,12},{1,17},{... | collective-permute-start | bytes 491528 | tf_op jit(solution)/shard_map/ppermute | solution.py:392
  84.3 6.2 %collective-permute-start.1 = (f32[64,640]{1,0:T(8,128)S(1)}, f32[64,640]{1,0:T(8,128)S(1)}, u32[]{:S(2)}, u32[]{:S(2)}) collective-permute-start(f32[64,640]{1,0:T(8,128)S(1)} %get-tuple-element.52), channel_id=1, source_target_pairs={{0,8},{4,12},{8,0},{12,4},{16,24},{20,28},{24,16},{28,20},{1,9},{5... | collective-permute-start | bytes 491528 | tf_op jit(solution)/shard_map/ppermute | solution.py:392
  88.7 5.6 %collective-permute-start.4 = (f32[64,640]{1,0:T(8,128)S(1)}, f32[64,640]{1,0:T(8,128)S(1)}, u32[]{:S(2)}, u32[]{:S(2)}) collective-permute-start(f32[64,640]{1,0:T(8,128)S(1)} %add.35), channel_id=1, source_target_pairs={{0,8},{4,12},{8,0},{12,4},{16,24},{20,28},{24,16},{28,20},{1,9},{5... | collective-permute-start | bytes 491528 | tf_op jit(solution)/shard_map/ppermute | solution.py:392
  90.5 5.4 %collective-permute-start.2 = (f32[64,640]{1,0:T(8,128)S(1)}, f32[64,640]{1,0:T(8,128)S(1)}, u32[]{:S(2)}, u32[]{:S(2)}) collective-permute-start(f32[64,640]{1,0:T(8,128)S(1)} %add.32), channel_id=1, source_target_pairs={{0,16},{4,20},{8,24},{12,28},{16,0},{20,4},{24,8},{28,12},{1,17},{... | collective-permute-start | bytes 491528 | tf_op jit(solution)/shard_map/ppermute | solution.py:392
  118.5 21.8 %collective-permute-start.9 = (f32[64,640]{1,0:T(8,128)S(1)}, f32[64,640]{1,0:T(8,128)S(1)}, u32[]{:S(2)}, u32[]{:S(2)}) collective-permute-start(f32[64,640]{1,0:T(8,128)S(1)} %get-tuple-element.31), channel_id=1, source_target_pairs={{0,3},{4,7},{8,11},{12,15},{16,19},{20,23},{24,27},{28,31}} | collective-permute-start | bytes 491528 | tf_op jit(solution)/shard_map/ppermute | solution.py:388
  135.0 8.1 %collective-permute-start.8 = (f32[64,640]{1,0:T(8,128)S(1)}, f32[64,640]{1,0:T(8,128)S(1)}, u32[]{:S(2)}, u32[]{:S(2)}) collective-permute-start(f32[64,640]{1,0:T(8,128)S(1)} %get-tuple-element.31), channel_id=1, source_target_pairs={{0,2},{4,6},{8,10},{12,14},{16,18},{20,22},{24,26},{28,30}} | collective-permute-start | bytes 491528 | tf_op jit(solution)/shard_map/ppermute | solution.py:388
  136.3 9.5 %collective-permute-start.7 = (f32[64,640]{1,0:T(8,128)S(1)}, f32[64,640]{1,0:T(8,128)S(1)}, u32[]{:S(2)}, u32[]{:S(2)}) collective-permute-start(f32[64,640]{1,0:T(8,128)S(1)} %get-tuple-element.31), channel_id=1, source_target_pairs={{0,1},{4,5},{8,9},{12,13},{16,17},{20,21},{24,25},{28,29}} | collective-permute-start | bytes 491528 | tf_op jit(solution)/shard_map/ppermute | solution.py:388
  138.3 11.1 %collective-permute-start.38 = (f32[2,256,128]{2,1,0:T(8,128)S(1)}, f32[2,256,128]{2,1,0:T(8,128)S(1)}, u32[]{:S(2)}, u32[]{:S(2)}) collective-permute-start(f32[2,256,128]{2,1,0:T(8,128)S(1)} %get-tuple-element.43), channel_id=1, source_target_pairs={{0,8},{4,12},{8,0},{12,4},{16,24},{20,28},{24,16},{28,20},{1,9},{5... | collective-permute-start | bytes 786440 | tf_op jit(solution)/shard_map/ppermute | solution.py:392
  139.5 12.0 %collective-permute-start.40 = (f32[2,256,128]{2,1,0:T(8,128)S(1)}, f32[2,256,128]{2,1,0:T(8,128)S(1)}, u32[]{:S(2)}, u32[]{:S(2)}) collective-permute-start(f32[2,256,128]{2,1,0:T(8,128)S(1)} %get-tuple-element.47), channel_id=1, source_target_pairs={{0,16},{4,20},{8,24},{12,28},{16,0},{20,4},{24,8},{28,12},{1,17},{... | collective-permute-start | bytes 786440 | tf_op jit(solution)/shard_map/ppermute | solution.py:392
  145.8 8.0 %collective-permute-start.12 = (f32[64,640]{1,0:T(8,128)S(1)}, f32[64,640]{1,0:T(8,128)S(1)}, u32[]{:S(2)}, u32[]{:S(2)}) collective-permute-start(f32[64,640]{1,0:T(8,128)S(1)} %add_add_fusion.refs_0_), channel_id=1, source_target_pairs={{0,24},{4,28},{8,16},{12,20},{16,8},{20,12},{24,0},{28,4},{1,25},{... | collective-permute-start | bytes 491528 | tf_op jit(solution)/shard_map/ppermute | solution.py:392
  147.4 8.5 %collective-permute-start.11 = (f32[64,640]{1,0:T(8,128)S(1)}, f32[64,640]{1,0:T(8,128)S(1)}, u32[]{:S(2)}, u32[]{:S(2)}) collective-permute-start(f32[64,640]{1,0:T(8,128)S(1)} %add_add_fusion.refs_0_), channel_id=1, source_target_pairs={{0,16},{4,20},{8,24},{12,28},{16,0},{20,4},{24,8},{28,12},{1,17},{... | collective-permute-start | bytes 491528 | tf_op jit(solution)/shard_map/ppermute | solution.py:392
  148.5 8.7 %collective-permute-start.10 = (f32[64,640]{1,0:T(8,128)S(1)}, f32[64,640]{1,0:T(8,128)S(1)}, u32[]{:S(2)}, u32[]{:S(2)}) collective-permute-start(f32[64,640]{1,0:T(8,128)S(1)} %add_add_fusion.refs_0_), channel_id=1, source_target_pairs={{0,8},{4,12},{8,0},{12,4},{16,24},{20,28},{24,16},{28,20},{1,9},{5... | collective-permute-start | bytes 491528 | tf_op jit(solution)/shard_map/ppermute | solution.py:392
  149.9 8.5 %collective-permute-start.39 = (f32[1,256,128]{2,1,0:T(8,128)S(1)}, f32[1,256,128]{2,1,0:T(8,128)S(1)}, u32[]{:S(2)}, u32[]{:S(2)}) collective-permute-start(f32[1,256,128]{2,1,0:T(8,128)S(1)} %get-tuple-element.45), channel_id=1, source_target_pairs={{0,16},{4,20},{8,24},{12,28},{16,0},{20,4},{24,8},{28,12},{1,17},{... | collective-permute-start | bytes 393224 | tf_op jit(solution)/shard_map/ppermute | solution.py:392
  152.1 6.5 %collective-permute-start.41 = (f32[1,256,128]{2,1,0:T(8,128)S(1)}, f32[1,256,128]{2,1,0:T(8,128)S(1)}, u32[]{:S(2)}, u32[]{:S(2)}) collective-permute-start(f32[1,256,128]{2,1,0:T(8,128)S(1)} %get-tuple-element.49), channel_id=1, source_target_pairs={{0,8},{4,12},{8,0},{12,4},{16,24},{20,28},{24,16},{28,20},{1,9},{5... | collective-permute-start | bytes 393224 | tf_op jit(solution)/shard_map/ppermute | solution.py:392
  (23 other events, 133.2 us)

commit v5 on v4

--- a/solution.py
+++ b/solution.py
@@ -35,39 +35,54 @@
     def subs(x, q):
         return jnp.broadcast_to(x[q : q + 1, :], (SUB, size))
 
-    scaled, scales = [], []
+    def row_times(columns, upper, inverse):
+        raw, times = [], []
+        for q in range(SUB):
+            value = columns[q]
+            for p in range(q):
+                value = value - times[p] * upper[p, q]
+            raw.append(value)
+            times.append(value * inverse[q])
+        return raw, times
+
+    scaled, scales, ready = [], [], None
     for at in range(count):
         low = SUB * at
         rows = tiles[at]
-        cols = [lanes(rows, low + q) for q in range(SUB)]
-        inverse, upper, pivots = [], {}, None
+        cols = ready or [lanes(rows, low + q) for q in range(SUB)]
+        if at + 1 < count:
+            ready = [lanes(tiles[at + 1], low + SUB + q) for q in range(SUB)]
+            below = [lanes(tiles[at + 1], low + q) for q in range(SUB)]
+        inverse, upper, pivots, factors = [], {}, None, []
         for q in range(SUB):
             pivot = subs(cols[q], q)
             pivots = pivot if pivots is None else jnp.where(sub == q, pivot, pivots)
             inverse.append(1.0 / pivot)
-            times = jnp.where(sub > q, cols[q] * inverse[q], 0.0)
+            factors.append(jnp.where(sub > q, cols[q] * inverse[q], 0.0))
             for p in range(q + 1, SUB):
                 upper[q, p] = subs(cols[q], p)
-                cols[p] = cols[p] - times * upper[q, p]
+                cols[p] = cols[p] - factors[q] * upper[q, p]
+        if at + 1 < count:
+            raw, next_times = row_times(below, upper, inverse)
+            for q in range(SUB):
+                for p in range(SUB):
+                    ready[q] = ready[q] - next_times[p] * subs(raw[p], q)
+        for q in range(SUB):
             pivot_row = jnp.where(lane == low + q, 1.0, subs(rows, q))
-            rows = jnp.where((lane == low + q) & (sub > q), 0.0, rows) - times * pivot_row
+            rows = jnp.where((lane == low + q) & (sub > q), 0.0, rows) - factors[q] * pivot_row
         pivot_rows = []
         for q in range(SUB):
             row = jnp.where(lane == low + q, 1.0, subs(rows, q))
             pivot_rows.append(jnp.where((lane > low + q) & (lane < low + SUB), 0.0, row))
         own = (lane >= low) & (lane < low + SUB)
         for other in range(at + 1, count):
-            tile = tiles[other]
-            theirs = [lanes(tile, low + q) for q in range(SUB)]
-            tile = jnp.where(own, 0.0, tile)
-            times = []
+            if other == at + 1:
+                times = next_times
+            else:
+                _, times = row_times([lanes(tiles[other], low + q) for q in range(SUB)], upper, inverse)
+            tile = jnp.where(own, 0.0, tiles[other])
             for q in range(SUB):
-                value = theirs[q]
-                for p in range(q):
-                    value = value - times[p] * upper[p, q]
-                value = value * inverse[q]
-                times.append(value)
-                tile = tile - value * pivot_rows[q]
+                tile = tile - times[q] * pivot_rows[q]
             tiles[other] = tile
         scale = lax.rsqrt(pivots)
         scales.append(scale)
@@ -220,7 +235,7 @@
         out_shape=(half, half),
         in_specs=[SMEM] + vmem(2),
         out_specs=tuple(vmem(2)),
-        compiler_params=pltpu.CompilerParams(vmem_limit_bytes=24 << 20),
+        compiler_params=pltpu.CompilerParams(vmem_limit_bytes=14 << 20),
         cost_estimate=pl.CostEstimate(flops=width * cols, bytes_accessed=12 * width * cols, transcendentals=0),
     )(place, first, second)
 
@@ -315,7 +330,7 @@
         first = jnp.minimum(place_ref[2], size - rows)
         own_ref[...] = l_ref[pl.ds(pl.multiple_of(first, rows), rows), :]
         each = piece_ref.shape[0]
-        piece_ref[...] = rect_ref[pl.ds(pl.multiple_of((me >> 1) * each, each), each), :]
+        piece_ref[...] = rect_ref[pl.ds(pl.multiple_of(me * each, each), each), :]
 
 
 def factor(place, parts, diag, each, rows):
@@ -354,7 +369,7 @@
         rows_ref[:half, :] = keep_a[...] + got_a[...]
         rows_ref[half:, :] = keep_b[...] + got_b[...]
     for m in range(count):
-        rect_ref[pl.ds(pl.multiple_of(((me >> 1) ^ m) * each, each), each), :] = pieces[m][...]
+        rect_ref[pl.ds(pl.multiple_of((me ^ m) * each, each), each), :] = pieces[m][...]
     for i, block, low in strips(nb):
         wide = (block + 1) * BLOCK
         part = rect_ref[i * BLOCK : (i + 1) * BLOCK, low : low + wide]
@@ -449,7 +464,7 @@
 
 
 PIECES = 8
-LATE = 2
+LATE = 1
 
 
 def bounds(depth):
@@ -480,13 +495,14 @@
         got_b = exchange(b, 1 << q, scen)
         a, b = a + got_a, b + got_b
     parts = (a, b, exchange(a, 1, scen), exchange(b, 1, scen))
-    each = width // BLOCK // 2 * BLOCK // (scen // 2)
+    each = width // BLOCK // 2 * BLOCK // scen
     lower, piece = factor(place, parts, hess_diag[None, :], each, rows)
 
     mine = jnp.where(plane == 0, piece, 0.0)
     for h in range(1, planes):
         mine = mine + hop(piece, 0, h)
     pieces = [mine if m == 0 else exchange(mine, m, scen) for m in range(0, scen, 2)]
+    pieces = [p for m in range(0, scen, 2) for p in (pieces[m // 2], exchange(pieces[m // 2], 1, scen))]
 
     cut = PIECES - LATE
     early = edge[cut]

time: 161 us -> 167 us (1.037)
  starting transfers between devices: 65.1 us -> 79 us
  Pallas kernels: 38.3 us -> 31.8 us
  waiting for transfers between devices: 44.4 us -> 40.4 us
    ppermute x27, starting transfers between devices: 49.2 us -> 62 us  [hop(): return lax.ppermute(x, 'col', [(source, target)])]
    pallas_call x1, Pallas kernels: 21.2 us -> 15.8 us  [factor(): pl.pallas_call(factor_kernel, out_shape=(shape(rows, size), shape(each, w...]
    ppermute x27, waiting for transfers between devices: 30.7 us -> 25.3 us  [hop(): return lax.ppermute(x, 'col', [(source, target)])]
    ppermute x15 -> x19, waiting for transfers between devices: 13.7 us -> 15 us  [exchange(): return lax.ppermute(x, 'scen', [(i, i ^ mask) for i in range(count)])]
    ppermute x15 -> x19, starting transfers between devices: 15.9 us -> 17 us  [exchange(): return lax.ppermute(x, 'scen', [(i, i ^ mask) for i in range(count)])]
  transfers between devices with their start and end apart: 42 -> 46, of which waited for: 19 -> 18; matrix products, arithmetic and copies ran while one was open for 3% -> 4% of each run, Pallas kernels for 17% -> 12%
where the time goes in v5:
time: 167 us; the launch traced here: 166 us
  starting transfers between devices  79 us (47%)
  waiting for transfers between devices  40.4 us (24%)
  Pallas kernels  31.8 us (19%)
  local copies, waits for them, and re-layouts  8.07 us (5%)
  matrix products  4.77 us (3%)
  other arithmetic  1.72 us (1%)
    ppermute x27, starting transfers between devices, hop(): return lax.ppermute(x, 'col', [(source, target)])  62 us
    ppermute x27, waiting for transfers between devices, hop(): return lax.ppermute(x, 'col', [(source, target)])  25.3 us
    ppermute x19, starting transfers between devices, exchange(): return lax.ppermute(x, 'scen', [(i, i ^ mask) for i in range(count)])  17 us
    pallas_call x1, Pallas kernels, factor(): pl.pallas_call(factor_kernel, out_shape=(shape(rows, size), shape(each, w...  15.8 us
    ppermute x19, waiting for transfers between devices, exchange(): return lax.ppermute(x, 'scen', [(i, i ^ mask) for i in range(count)])  15 us
    pallas_call x1, Pallas kernels, product(): pl.pallas_call(functools.partial(product_kernel, edges, tall), out_shape=...  10 us
    unnamed x26, local copies, waits for them, and re-layouts  8.07 us
    dot_general x2, matrix products, high(): lax.dot_general(left, right, (dims, ((), ())), precision=lax.Precision.HI...  4.77 us
  transfers between devices with their start and end apart: 46, of which 18 were waited for; matrix products, arithmetic and copies ran while one was open for 4% of the time, Pallas kernels for 12%

profile of v5, /device:TPU:0, one launch (start us, length us, event | category | flops | bytes accessed | tf_op | source)
XLA Modules:
  0.0 166.3 jit_solution(7384346032961407988)
XLA Ops:
  0.6 10.0 %shard_map.46 = (f32[128,512]{1,0:T(8,128)}, f32[128,512]{1,0:T(8,128)}, f32[128,512]{1,0:T(8,128)}, f32[128,512]{1,0:T(8,128)}, f32[128,512]{1,0:T(8,128)}, /*i...) custom-call(s32[3]{0:T(128)} %pad_add_fusion.place_ref, ...), custom_call_target="tpu_custom_call" | custom-call | flops 4831838208 | bytes 8388608 | tf_op jit(solution)/shard_map/pallas_call | solution.py:175
  17.2 1.7 %collective-permute-done.17.refs_7_ = f32[128,512]{1,0:T(8,128)S(1)} collective-permute-done((f32[128,512]{1,0:T(8,128)}, f32[128,512]{1,0:T(8,128)S(1)}, u32[]{:S(2)}, u32[]{:S(2)}) %collective-permute-start.17) | collective-permute-done | bytes 262176 | tf_op jit(solution)/shard_map/ppermute | solution.py:403
  18.9 4.3 %collective-permute-start.22 = (f32[128,512]{1,0:T(8,128)}, f32[128,512]{1,0:T(8,128)S(1)}, u32[]{:S(2)}, u32[]{:S(2)}) collective-permute-start(f32[128,512]{1,0:T(8,128)} %get-tuple-element.37.refs_5_), channel_id=1, source_target_pairs={{0,1},{4,5},{8,9},{12,13},{16,17},{20,21},{24,25},{28,29}} | collective-permute-start | bytes 786440 | tf_op jit(solution)/shard_map/ppermute | solution.py:403
  23.2 1.3 collective-permute-done.18.refs_8_
  24.6 4.3 %collective-permute-start.23 = (f32[128,512]{1,0:T(8,128)}, f32[128,512]{1,0:T(8,128)S(1)}, u32[]{:S(2)}, u32[]{:S(2)}) collective-permute-start(f32[128,512]{1,0:T(8,128)} %get-tuple-element.38.refs_6_), channel_id=1, source_target_pairs={{0,1},{4,5},{8,9},{12,13},{16,17},{20,21},{24,25},{28,29}} | collective-permute-start | bytes 786440 | tf_op jit(solution)/shard_map/ppermute | solution.py:403
  30.2 4.3 %collective-permute-start.38 = (f32[128,512]{1,0:T(8,128)}, f32[128,512]{1,0:T(8,128)S(1)}, u32[]{:S(2)}, u32[]{:S(2)}) collective-permute-start(f32[128,512]{1,0:T(8,128)} %get-tuple-element.39.refs_0_), channel_id=1, source_target_pairs={{0,1},{4,5},{8,9},{12,13},{16,17},{20,21},{24,25},{28,29}} | collective-permute-start | bytes 786440 | tf_op jit(solution)/shard_map/ppermute | solution.py:403
  36.5 4.9 %collective-permute-done.21.refs_11_ = f32[128,512]{1,0:T(8,128)S(1)} collective-permute-done((f32[128,512]{1,0:T(8,128)}, f32[128,512]{1,0:T(8,128)S(1)}, u32[]{:S(2)}, u32[]{:S(2)}) %collective-permute-start.21) | collective-permute-done | bytes 262176 | tf_op jit(solution)/shard_map/ppermute | solution.py:403
  42.1 4.9 %collective-permute-done.22.refs_12_ = f32[128,512]{1,0:T(8,128)S(1)} collective-permute-done((f32[128,512]{1,0:T(8,128)}, f32[128,512]{1,0:T(8,128)S(1)}, u32[]{:S(2)}, u32[]{:S(2)}) %collective-permute-start.22) | collective-permute-done | bytes 262176 | tf_op jit(solution)/shard_map/ppermute | solution.py:403
  47.7 4.9 %collective-permute-done.23.refs_13_ = f32[128,512]{1,0:T(8,128)S(1)} collective-permute-done((f32[128,512]{1,0:T(8,128)}, f32[128,512]{1,0:T(8,128)S(1)}, u32[]{:S(2)}, u32[]{:S(2)}) %collective-permute-start.23) | collective-permute-done | bytes 262176 | tf_op jit(solution)/shard_map/ppermute | solution.py:403
  53.3 4.8 %collective-permute-done.38.refs_1_ = f32[128,512]{1,0:T(8,128)S(1)} collective-permute-done((f32[128,512]{1,0:T(8,128)}, f32[128,512]{1,0:T(8,128)S(1)}, u32[]{:S(2)}, u32[]{:S(2)}) %collective-permute-start.38) | collective-permute-done | bytes 262176 | tf_op jit(solution)/shard_map/ppermute | solution.py:403
  74.0 1.4 copy-done.10
  75.4 3.7 %fusion.first_ref = f32[512,1024]{1,0:T(8,128)S(1)} fusion(f32[896,512]{1,0:T(8,128)S(1)} %shard_map.48, f32[1,1024,1024]{2,1,0:T(8,128)S(1)} %copy-done.10), kind=kOutput, calls=%fused_computation | convolution fusion | flops 2818572288 | bytes 7602176 | tf_op jit(solution)/shard_map/dot_general | solution.py:16
  82.5 2.4 %collective-permute-start.3 = (f32[64,640]{1,0:T(8,128)S(1)}, f32[64,640]{1,0:T(8,128)S(1)}, u32[]{:S(2)}, u32[]{:S(2)}) collective-permute-start(f32[64,640]{1,0:T(8,128)S(1)} %get-tuple-element.51), channel_id=1, source_target_pairs={{0,16},{4,20},{8,24},{12,28},{16,0},{20,4},{24,8},{28,12},{1,17},{... | collective-permute-start | bytes 491528 | tf_op jit(solution)/shard_map/ppermute | solution.py:407
  84.9 1.5 collective-permute-start.1
  86.4 2.9 %collective-permute-done.3 = f32[64,640]{1,0:T(8,128)S(1)} collective-permute-done((f32[64,640]{1,0:T(8,128)S(1)}, f32[64,640]{1,0:T(8,128)S(1)}, u32[]{:S(2)}, u32[]{:S(2)}) %collective-permute-start.3) | collective-permute-done | bytes 163872 | tf_op jit(solution)/shard_map/ppermute | solution.py:407
  89.3 1.8 %collective-permute-start.4 = (f32[64,640]{1,0:T(8,128)S(1)}, f32[64,640]{1,0:T(8,128)S(1)}, u32[]{:S(2)}, u32[]{:S(2)}) collective-permute-start(f32[64,640]{1,0:T(8,128)S(1)} %add.35), channel_id=1, source_target_pairs={{0,8},{4,12},{8,0},{12,4},{16,24},{20,28},{24,16},{28,20},{1,9},{5... | collective-permute-start | bytes 491528 | tf_op jit(solution)/shard_map/ppermute | solution.py:407
  91.1 1.6 collective-permute-start.2
  92.7 2.3 %collective-permute-done.4 = f32[64,640]{1,0:T(8,128)S(1)} collective-permute-done((f32[64,640]{1,0:T(8,128)S(1)}, f32[64,640]{1,0:T(8,128)S(1)}, u32[]{:S(2)}, u32[]{:S(2)}) %collective-permute-start.4) | collective-permute-done | bytes 163872 | tf_op jit(solution)/shard_map/ppermute | solution.py:407
  95.1 1.5 collective-permute-done.2
  96.6 1.4 collective-permute-done.5.other_a
  98.0 15.8 %shard_map.47 = (f32[128,512]{1,0:T(8,128)S(1)}, f32[32,640]{1,0:T(8,128)S(1)}) custom-call(s32[3]{0:T(128)S(1)} %copy-done.8, f32[64,640]{1,0:T(8,128)S(1)} %add.33.own_a, f32[64,640]{1,0:T(8,128)S(1)} %add.36.own_b, f32[64,640]{1,0:T(8,128)S(1)} %collective-permute-done.5.other_a, f32[64,640]{1,0:T(8,128)S(1)} %collective-permute-done.6.other_b, ...), custom_call_target="tpu_custom_call" | custom-call | flops 2684354560 | bytes 3145728 | tf_op jit(solution)/shard_map/pallas_call | solution.py:340
  113.8 28.0 %collective-permute-start.9 = (f32[32,640]{1,0:T(8,128)S(1)}, f32[32,640]{1,0:T(8,128)}, u32[]{:S(2)}, u32[]{:S(2)}) collective-permute-start(f32[32,640]{1,0:T(8,128)S(1)} %get-tuple-element.31), channel_id=1, source_target_pairs={{0,3},{4,7},{8,11},{12,15},{16,19},{20,23},{24,27},{28,31}} | collective-permute-start | bytes 245768 | tf_op jit(solution)/shard_map/ppermute | solution.py:403
  141.8 1.9 %collective-permute-start.8 = (f32[32,640]{1,0:T(8,128)S(1)}, f32[32,640]{1,0:T(8,128)}, u32[]{:S(2)}, u32[]{:S(2)}) collective-permute-start(f32[32,640]{1,0:T(8,128)S(1)} %get-tuple-element.31), channel_id=1, source_target_pairs={{0,2},{4,6},{8,10},{12,14},{16,18},{20,22},{24,26},{28,30}} | collective-permute-start | bytes 245768 | tf_op jit(solution)/shard_map/ppermute | solution.py:403
  143.7 1.9 %collective-permute-start.7 = (f32[32,640]{1,0:T(8,128)S(1)}, f32[32,640]{1,0:T(8,128)}, u32[]{:S(2)}, u32[]{:S(2)}) collective-permute-start(f32[32,640]{1,0:T(8,128)S(1)} %get-tuple-element.31), channel_id=1, source_target_pairs={{0,1},{4,5},{8,9},{12,13},{16,17},{20,21},{24,25},{28,29}} | collective-permute-start | bytes 245768 | tf_op jit(solution)/shard_map/ppermute | solution.py:403
  149.4 1.5 collective-permute-start.15
  150.9 1.5 collective-permute-start.13
  153.0 2.5 %collective-permute-done.42.got_ref = f32[2,256,128]{2,1,0:T(8,128)S(1)} collective-permute-done((f32[2,256,128]{2,1,0:T(8,128)S(1)}, f32[2,256,128]{2,1,0:T(8,128)S(1)}, u32[]{:S(2)}, u32[]{:S(2)}) %collective-permute-start.42) | collective-permute-done | bytes 262176 | tf_op jit(solution)/shard_map/ppermute | solution.py:407
  156.1 1.4 collective-permute-done.44.got_ref
  157.6 1.3 collective-permute-start.43
  159.5 1.4 collective-permute-start.45
  162.8 1.8 %collective-permute-done.45.refs_11_ = f32[1,256,128]{2,1,0:T(8,128)S(1)} collective-permute-done((f32[1,256,128]{2,1,0:T(8,128)S(1)}, f32[1,256,128]{2,1,0:T(8,128)S(1)}, u32[]{:S(2)}, u32[]{:S(2)}) %collective-permute-start.45) | collective-permute-done | bytes 131104 | tf_op jit(solution)/shard_map/ppermute | solution.py:407
  164.5 1.8 %shard_map.54 = f32[128,512]{1,0:T(8,128)} custom-call(s32[3]{0:T(128)S(1)} %copy-done.8, f32[32,640]{1,0:T(8,128)S(1)} %add_add_fusion.refs_0_, f32[32,640]{1,0:T(8,128)S(1)} %collective-permute-done.10.refs_1_, f32[32,640]{1,0:T(8,128)S(1)} %collective-permute-done.11.refs_2_, f32[32,640]{1,0:T(8,128)S(1)} %collective-permute-done.12.refs_3_, ...), custom_call_target="tpu_custom_call" | custom-call | flops 201326592 | bytes 2097152 | tf_op jit(solution)/shard_map/pallas_call | solution.py:391
  (104 shorter events, 39.0 us)
Async XLA Ops:
  10.6 8.3 %collective-permute-start.17 = (f32[128,512]{1,0:T(8,128)}, f32[128,512]{1,0:T(8,128)S(1)}, u32[]{:S(2)}, u32[]{:S(2)}) collective-permute-start(f32[128,512]{1,0:T(8,128)} %get-tuple-element.32.refs_0_), channel_id=1, source_target_pairs={{0,1},{4,5},{8,9},{12,13},{16,17},{20,21},{24,25},{28,29}} | collective-permute-start | bytes 786440 | tf_op jit(solution)/shard_map/ppermute | solution.py:403
  12.0 12.6 %collective-permute-start.18 = (f32[128,512]{1,0:T(8,128)}, f32[128,512]{1,0:T(8,128)S(1)}, u32[]{:S(2)}, u32[]{:S(2)}) collective-permute-start(f32[128,512]{1,0:T(8,128)} %get-tuple-element.33.refs_1_), channel_id=1, source_target_pairs={{0,1},{4,5},{8,9},{12,13},{16,17},{20,21},{24,25},{28,29}} | collective-permute-start | bytes 786440 | tf_op jit(solution)/shard_map/ppermute | solution.py:403
  13.3 16.9 %collective-permute-start.19 = (f32[128,512]{1,0:T(8,128)}, f32[128,512]{1,0:T(8,128)S(1)}, u32[]{:S(2)}, u32[]{:S(2)}) collective-permute-start(f32[128,512]{1,0:T(8,128)} %get-tuple-element.34.refs_2_), channel_id=1, source_target_pairs={{0,1},{4,5},{8,9},{12,13},{16,17},{20,21},{24,25},{28,29}} | collective-permute-start | bytes 786440 | tf_op jit(solution)/shard_map/ppermute | solution.py:403
  14.6 21.2 %collective-permute-start.20 = (f32[128,512]{1,0:T(8,128)}, f32[128,512]{1,0:T(8,128)S(1)}, u32[]{:S(2)}, u32[]{:S(2)}) collective-permute-start(f32[128,512]{1,0:T(8,128)} %get-tuple-element.35.refs_3_), channel_id=1, source_target_pairs={{0,1},{4,5},{8,9},{12,13},{16,17},{20,21},{24,25},{28,29}} | collective-permute-start | bytes 786440 | tf_op jit(solution)/shard_map/ppermute | solution.py:403
  15.9 25.5 %collective-permute-start.21 = (f32[128,512]{1,0:T(8,128)}, f32[128,512]{1,0:T(8,128)S(1)}, u32[]{:S(2)}, u32[]{:S(2)}) collective-permute-start(f32[128,512]{1,0:T(8,128)} %get-tuple-element.36.refs_4_), channel_id=1, source_target_pairs={{0,1},{4,5},{8,9},{12,13},{16,17},{20,21},{24,25},{28,29}} | collective-permute-start | bytes 786440 | tf_op jit(solution)/shard_map/ppermute | solution.py:403
  18.9 28.1 %collective-permute-start.22 = (f32[128,512]{1,0:T(8,128)}, f32[128,512]{1,0:T(8,128)S(1)}, u32[]{:S(2)}, u32[]{:S(2)}) collective-permute-start(f32[128,512]{1,0:T(8,128)} %get-tuple-element.37.refs_5_), channel_id=1, source_target_pairs={{0,1},{4,5},{8,9},{12,13},{16,17},{20,21},{24,25},{28,29}} | collective-permute-start | bytes 786440 | tf_op jit(solution)/shard_map/ppermute | solution.py:403
  24.6 28.1 %collective-permute-start.23 = (f32[128,512]{1,0:T(8,128)}, f32[128,512]{1,0:T(8,128)S(1)}, u32[]{:S(2)}, u32[]{:S(2)}) collective-permute-start(f32[128,512]{1,0:T(8,128)} %get-tuple-element.38.refs_6_), channel_id=1, source_target_pairs={{0,1},{4,5},{8,9},{12,13},{16,17},{20,21},{24,25},{28,29}} | collective-permute-start | bytes 786440 | tf_op jit(solution)/shard_map/ppermute | solution.py:403
  30.2 27.9 %collective-permute-start.38 = (f32[128,512]{1,0:T(8,128)}, f32[128,512]{1,0:T(8,128)S(1)}, u32[]{:S(2)}, u32[]{:S(2)}) collective-permute-start(f32[128,512]{1,0:T(8,128)} %get-tuple-element.39.refs_0_), channel_id=1, source_target_pairs={{0,1},{4,5},{8,9},{12,13},{16,17},{20,21},{24,25},{28,29}} | collective-permute-start | bytes 786440 | tf_op jit(solution)/shard_map/ppermute | solution.py:403
  35.8 23.0 %collective-permute-start.24 = (f32[128,512]{1,0:T(8,128)S(1)}, f32[128,512]{1,0:T(8,128)S(1)}, u32[]{:S(2)}, u32[]{:S(2)}) collective-permute-start(f32[128,512]{1,0:T(8,128)S(1)} %collective-permute-done.17.refs_7_), channel_id=1, source_target_pairs={{1,2},{5,6},{9,10},{13,14},{17,18},{21,22},{25,26},{29,30}} | collective-permute-start | bytes 786440 | tf_op jit(solution)/shard_map/ppermute | solution.py:403
  41.4 18.0 %collective-permute-start.25 = (f32[128,512]{1,0:T(8,128)S(1)}, f32[128,512]{1,0:T(8,128)S(1)}, u32[]{:S(2)}, u32[]{:S(2)}) collective-permute-start(f32[128,512]{1,0:T(8,128)S(1)} %collective-permute-done.18.refs_8_), channel_id=1, source_target_pairs={{1,2},{5,6},{9,10},{13,14},{17,18},{21,22},{25,26},{29,30}} | collective-permute-start | bytes 786440 | tf_op jit(solution)/shard_map/ppermute | solution.py:403
  47.0 13.1 %collective-permute-start.26 = (f32[128,512]{1,0:T(8,128)S(1)}, f32[128,512]{1,0:T(8,128)S(1)}, u32[]{:S(2)}, u32[]{:S(2)}) collective-permute-start(f32[128,512]{1,0:T(8,128)S(1)} %collective-permute-done.19.refs_9_), channel_id=1, source_target_pairs={{1,2},{5,6},{9,10},{13,14},{17,18},{21,22},{25,26},{29,30}} | collective-permute-start | bytes 786440 | tf_op jit(solution)/shard_map/ppermute | solution.py:403
  52.6 8.2 %collective-permute-start.27 = (f32[128,512]{1,0:T(8,128)S(1)}, f32[128,512]{1,0:T(8,128)S(1)}, u32[]{:S(2)}, u32[]{:S(2)}) collective-permute-start(f32[128,512]{1,0:T(8,128)S(1)} %collective-permute-done.20.refs_10_), channel_id=1, source_target_pairs={{1,2},{5,6},{9,10},{13,14},{17,18},{21,22},{25,26},{29,30}} | collective-permute-start | bytes 786440 | tf_op jit(solution)/shard_map/ppermute | solution.py:403
  58.8 3.5 %collective-permute-start.29 = (f32[128,512]{1,0:T(8,128)S(1)}, f32[128,512]{1,0:T(8,128)S(1)}, u32[]{:S(2)}, u32[]{:S(2)}) collective-permute-start(f32[128,512]{1,0:T(8,128)S(1)} %collective-permute-done.22.refs_12_), channel_id=1, source_target_pairs={{1,2},{5,6},{9,10},{13,14},{17,18},{21,22},{25,26},{29,30}} | collective-permute-start | bytes 786440 | tf_op jit(solution)/shard_map/ppermute | solution.py:403
  59.4 3.5 %collective-permute-start.30 = (f32[128,512]{1,0:T(8,128)S(1)}, f32[128,512]{1,0:T(8,128)S(1)}, u32[]{:S(2)}, u32[]{:S(2)}) collective-permute-start(f32[128,512]{1,0:T(8,128)S(1)} %collective-permute-done.23.refs_13_), channel_id=1, source_target_pairs={{1,2},{5,6},{9,10},{13,14},{17,18},{21,22},{25,26},{29,30}} | collective-permute-start | bytes 786440 | tf_op jit(solution)/shard_map/ppermute | solution.py:403
  65.7 16.8 %collective-permute-start = (f32[128,640]{1,0:T(8,128)}, f32[128,640]{1,0:T(8,128)S(1)}, u32[]{:S(2)}, u32[]{:S(2)}) collective-permute-start(f32[128,640]{1,0:T(8,128)} %get-tuple-element.29), channel_id=1, source_target_pairs={{0,4},{4,0},{8,12},{12,8},{16,20},{20,16},{24,28},{28,24},{1,5},{5... | collective-permute-start | bytes 983048 | tf_op jit(solution)/shard_map/ppermute | solution.py:407
  65.8 13.3 %collective-permute-start.40 = (f32[128,512]{1,0:T(8,128)S(1)}, f32[128,512]{1,0:T(8,128)S(1)}, u32[]{:S(2)}, u32[]{:S(2)}) collective-permute-start(f32[128,512]{1,0:T(8,128)S(1)} %collective-permute-done.39.refs_2_), channel_id=1, source_target_pairs={{2,3},{6,7},{10,11},{14,15},{18,19},{22,23},{26,27},{30,31}} | collective-permute-start | bytes 786440 | tf_op jit(solution)/shard_map/ppermute | solution.py:403
  81.9 63.7 %collective-permute-start.41 = (f32[4,512,128]{2,1,0:T(8,128)S(1)}, f32[4,512,128]{2,1,0:T(8,128)S(1)}, u32[]{:S(2)}, u32[]{:S(2)}) collective-permute-start(f32[4,512,128]{2,1,0:T(8,128)S(1)} %get-tuple-element.41), channel_id=1, source_target_pairs={{0,4},{4,0},{8,12},{12,8},{16,20},{20,16},{24,28},{28,24},{1,5},{5... | collective-permute-start | bytes 3145736 | tf_op jit(solution)/shard_map/ppermute | solution.py:407
  82.5 6.8 %collective-permute-start.3 = (f32[64,640]{1,0:T(8,128)S(1)}, f32[64,640]{1,0:T(8,128)S(1)}, u32[]{:S(2)}, u32[]{:S(2)}) collective-permute-start(f32[64,640]{1,0:T(8,128)S(1)} %get-tuple-element.51), channel_id=1, source_target_pairs={{0,16},{4,20},{8,24},{12,28},{16,0},{20,4},{24,8},{28,12},{1,17},{... | collective-permute-start | bytes 491528 | tf_op jit(solution)/shard_map/ppermute | solution.py:407
  84.9 6.2 %collective-permute-start.1 = (f32[64,640]{1,0:T(8,128)S(1)}, f32[64,640]{1,0:T(8,128)S(1)}, u32[]{:S(2)}, u32[]{:S(2)}) collective-permute-start(f32[64,640]{1,0:T(8,128)S(1)} %get-tuple-element.52), channel_id=1, source_target_pairs={{0,8},{4,12},{8,0},{12,4},{16,24},{20,28},{24,16},{28,20},{1,9},{5... | collective-permute-start | bytes 491528 | tf_op jit(solution)/shard_map/ppermute | solution.py:407
  89.3 5.6 %collective-permute-start.4 = (f32[64,640]{1,0:T(8,128)S(1)}, f32[64,640]{1,0:T(8,128)S(1)}, u32[]{:S(2)}, u32[]{:S(2)}) collective-permute-start(f32[64,640]{1,0:T(8,128)S(1)} %add.35), channel_id=1, source_target_pairs={{0,8},{4,12},{8,0},{12,4},{16,24},{20,28},{24,16},{28,20},{1,9},{5... | collective-permute-start | bytes 491528 | tf_op jit(solution)/shard_map/ppermute | solution.py:407
  91.1 5.4 %collective-permute-start.2 = (f32[64,640]{1,0:T(8,128)S(1)}, f32[64,640]{1,0:T(8,128)S(1)}, u32[]{:S(2)}, u32[]{:S(2)}) collective-permute-start(f32[64,640]{1,0:T(8,128)S(1)} %add.32), channel_id=1, source_target_pairs={{0,16},{4,20},{8,24},{12,28},{16,0},{20,4},{24,8},{28,12},{1,17},{... | collective-permute-start | bytes 491528 | tf_op jit(solution)/shard_map/ppermute | solution.py:407
  113.8 34.7 %collective-permute-start.9 = (f32[32,640]{1,0:T(8,128)S(1)}, f32[32,640]{1,0:T(8,128)}, u32[]{:S(2)}, u32[]{:S(2)}) collective-permute-start(f32[32,640]{1,0:T(8,128)S(1)} %get-tuple-element.31), channel_id=1, source_target_pairs={{0,3},{4,7},{8,11},{12,15},{16,19},{20,23},{24,27},{28,31}} | collective-permute-start | bytes 245768 | tf_op jit(solution)/shard_map/ppermute | solution.py:403
  141.8 6.6 %collective-permute-start.8 = (f32[32,640]{1,0:T(8,128)S(1)}, f32[32,640]{1,0:T(8,128)}, u32[]{:S(2)}, u32[]{:S(2)}) collective-permute-start(f32[32,640]{1,0:T(8,128)S(1)} %get-tuple-element.31), channel_id=1, source_target_pairs={{0,2},{4,6},{8,10},{12,14},{16,18},{20,22},{24,26},{28,30}} | collective-permute-start | bytes 245768 | tf_op jit(solution)/shard_map/ppermute | solution.py:403
  143.7 4.7 %collective-permute-start.7 = (f32[32,640]{1,0:T(8,128)S(1)}, f32[32,640]{1,0:T(8,128)}, u32[]{:S(2)}, u32[]{:S(2)}) collective-permute-start(f32[32,640]{1,0:T(8,128)S(1)} %get-tuple-element.31), channel_id=1, source_target_pairs={{0,1},{4,5},{8,9},{12,13},{16,17},{20,21},{24,25},{28,29}} | collective-permute-start | bytes 245768 | tf_op jit(solution)/shard_map/ppermute | solution.py:403
  146.3 9.2 %collective-permute-start.42 = (f32[2,256,128]{2,1,0:T(8,128)S(1)}, f32[2,256,128]{2,1,0:T(8,128)S(1)}, u32[]{:S(2)}, u32[]{:S(2)}) collective-permute-start(f32[2,256,128]{2,1,0:T(8,128)S(1)} %get-tuple-element.43), channel_id=1, source_target_pairs={{0,8},{4,12},{8,0},{12,4},{16,24},{20,28},{24,16},{28,20},{1,9},{5... | collective-permute-start | bytes 786440 | tf_op jit(solution)/shard_map/ppermute | solution.py:407
  147.5 10.1 %collective-permute-start.44 = (f32[2,256,128]{2,1,0:T(8,128)S(1)}, f32[2,256,128]{2,1,0:T(8,128)S(1)}, u32[]{:S(2)}, u32[]{:S(2)}) collective-permute-start(f32[2,256,128]{2,1,0:T(8,128)S(1)} %get-tuple-element.47), channel_id=1, source_target_pairs={{0,16},{4,20},{8,24},{12,28},{16,0},{20,4},{24,8},{28,12},{1,17},{... | collective-permute-start | bytes 786440 | tf_op jit(solution)/shard_map/ppermute | solution.py:407
  149.4 10.1 %collective-permute-start.15 = (f32[32,640]{1,0:T(8,128)S(1)}, f32[32,640]{1,0:T(8,128)S(1)}, u32[]{:S(2)}, u32[]{:S(2)}) collective-permute-start(f32[32,640]{1,0:T(8,128)S(1)} %add_add_fusion.refs_0_), channel_id=1, source_target_pairs={{0,24},{4,28},{8,16},{12,20},{16,8},{20,12},{24,0},{28,4},{1,25},{... | collective-permute-start | bytes 245768 | tf_op jit(solution)/shard_map/ppermute | solution.py:407
  150.9 10.0 %collective-permute-start.13 = (f32[32,640]{1,0:T(8,128)S(1)}, f32[32,640]{1,0:T(8,128)S(1)}, u32[]{:S(2)}, u32[]{:S(2)}) collective-permute-start(f32[32,640]{1,0:T(8,128)S(1)} %add_add_fusion.refs_0_), channel_id=1, source_target_pairs={{0,16},{4,20},{8,24},{12,28},{16,0},{20,4},{24,8},{28,12},{1,17},{... | collective-permute-start | bytes 245768 | tf_op jit(solution)/shard_map/ppermute | solution.py:407
  152.4 8.6 %collective-permute-start.11 = (f32[32,640]{1,0:T(8,128)S(1)}, f32[32,640]{1,0:T(8,128)S(1)}, u32[]{:S(2)}, u32[]{:S(2)}) collective-permute-start(f32[32,640]{1,0:T(8,128)S(1)} %add_add_fusion.refs_0_), channel_id=1, source_target_pairs={{0,8},{4,12},{8,0},{12,4},{16,24},{20,28},{24,16},{28,20},{1,9},{5... | collective-permute-start | bytes 245768 | tf_op jit(solution)/shard_map/ppermute | solution.py:407
  155.5 5.9 %collective-permute-start.10 = (f32[32,640]{1,0:T(8,128)S(1)}, f32[32,640]{1,0:T(8,128)S(1)}, u32[]{:S(2)}, u32[]{:S(2)}) collective-permute-start(f32[32,640]{1,0:T(8,128)S(1)} %add_add_fusion.refs_0_), channel_id=1, source_target_pairs={{0,4},{4,0},{8,12},{12,8},{16,20},{20,16},{24,28},{28,24},{1,5},{5... | collective-permute-start | bytes 245768 | tf_op jit(solution)/shard_map/ppermute | solution.py:407
  157.6 5.2 %collective-permute-start.43 = (f32[1,256,128]{2,1,0:T(8,128)S(1)}, f32[1,256,128]{2,1,0:T(8,128)S(1)}, u32[]{:S(2)}, u32[]{:S(2)}) collective-permute-start(f32[1,256,128]{2,1,0:T(8,128)S(1)} %get-tuple-element.45), channel_id=1, source_target_pairs={{0,16},{4,20},{8,24},{12,28},{16,0},{20,4},{24,8},{28,12},{1,17},{... | collective-permute-start | bytes 393224 | tf_op jit(solution)/shard_map/ppermute | solution.py:407
  159.5 5.0 %collective-permute-start.45 = (f32[1,256,128]{2,1,0:T(8,128)S(1)}, f32[1,256,128]{2,1,0:T(8,128)S(1)}, u32[]{:S(2)}, u32[]{:S(2)}) collective-permute-start(f32[1,256,128]{2,1,0:T(8,128)S(1)} %get-tuple-element.49), channel_id=1, source_target_pairs={{0,8},{4,12},{8,0},{12,4},{16,24},{20,28},{24,16},{28,20},{1,9},{5... | collective-permute-start | bytes 393224 | tf_op jit(solution)/shard_map/ppermute | solution.py:407
  (27 other events, 135.0 us)

commit v6 on v5

--- a/solution.py
+++ b/solution.py
@@ -126,7 +126,7 @@
 def product_kernel(edges, tall, place_ref, mask_ref, inverse_hbm, coupling_hbm, *refs):
     count = len(edges) - 1
     pieces = refs[:count]
-    keep_a, keep_b, send, panel, rows, ph, plo, qh, ql, rect, sems = refs[count:]
+    keep, send, panel, rows, ph, plo, qh, ql, rect, sems = refs[count:]
 
     @pl.when(place_ref[0] == 0)
     def _():
@@ -163,8 +163,7 @@
         core = place_ref[1] & 1
         mine = pl.multiple_of(core * half, half)
         theirs = pl.multiple_of((1 - core) * half, half)
-        keep_a[...] = rect[pl.ds(mine, half // 2), :]
-        keep_b[...] = rect[pl.ds(mine + half // 2, half // 2), :]
+        keep[...] = rect[pl.ds(mine, half), :]
         send[...] = rect[pl.ds(theirs, half), :]
 
 
@@ -175,9 +174,9 @@
     return pl.pallas_call(
         functools.partial(product_kernel, edges, tall),
         out_shape=tuple(shape(b - a, width) for a, b in zip(edges, edges[1:]))
-        + (shape(high_rows // 4, wide), shape(high_rows // 4, wide), shape(high_rows // 2, wide)),
+        + (shape(high_rows // 2, wide), shape(high_rows // 2, wide)),
         in_specs=[SMEM, SMEM, HBM, HBM],
-        out_specs=tuple(vmem(count + 3)),
+        out_specs=tuple(vmem(count + 2)),
         scratch_shapes=[pltpu.VMEM((depth, width), jnp.float32), pltpu.VMEM((depth // tall, tall, depth), jnp.float32)]
         + [pltpu.VMEM((depth, width), jnp.bfloat16)] * 4
         + [pltpu.VMEM((high_rows, wide), jnp.float32), pltpu.SemaphoreType.DMA((1 + depth // tall,))],
@@ -240,30 +239,29 @@
     )(place, first, second)
 
 
-def turn_kernel(cuts, place_ref, own_ref, got_ref, *outs):
-    for (low, high_row, position, bit), keep_ref, send_ref in zip(cuts, outs[::2], outs[1::2]):
-        mine = (place_ref[1] >> bit) & 1
-        rows = slice(low, high_row)
-        for ref, value in ((keep_ref, mine), (send_ref, 1 - mine)):
-            for j in range(ref.shape[0]):
-                at = ((j >> position) << (position + 1)) + (j & ((1 << position) - 1)) + (value << position)
-                ref[j] = own_ref[at, rows, :] + got_ref[at, rows, :]
-
-
-def turn(place, own, got, cuts):
-    blocks, _, wide = own.shape
-    outs = tuple(shape(blocks // 2, high_row - low, wide) for low, high_row, _, _ in cuts for _ in range(2))
+def turn_kernel(near, far, place_ref, own_ref, got_ref, keep_ref, send_ref):
+    core = place_ref[1] & 1
+    bit, position = (jnp.where(core == 0, near[i], far[i]) for i in range(2))
+    mine = (place_ref[1] >> bit) & 1
+    for ref, value in ((keep_ref, mine), (send_ref, 1 - mine)):
+        for j in range(ref.shape[0]):
+            at = ((j >> position) << (position + 1)) + (j & ((1 << position) - 1)) + (value << position)
+            ref[j] = own_ref[at] + got_ref[at]
+
+
+def turn(place, own, got, near, far):
+    half = shape(own.shape[0] // 2, *own.shape[1:])
     return pl.pallas_call(
-        functools.partial(turn_kernel, cuts),
-        out_shape=outs,
+        functools.partial(turn_kernel, near, far),
+        out_shape=(half, half),
         in_specs=[SMEM] + vmem(2),
-        out_specs=tuple(vmem(len(outs))),
+        out_specs=tuple(vmem(2)),
         compiler_params=pltpu.CompilerParams(vmem_limit_bytes=12 << 20),
         cost_estimate=pl.CostEstimate(flops=own.size, bytes_accessed=12 * own.size, transcendentals=0),
     )(place, own, got)
 
 
-def factor_kernel(place_ref, own_a, own_b, other_a, other_b, diag_ref, own_ref, piece_ref, l_ref, w_ref, rect_ref, base_ref, scale_ref):
+def factor_kernel(place_ref, strip, other, diag_ref, own_ref, piece_ref, l_ref, w_ref, rect_ref, base_ref, scale_ref):
     size = w_ref.shape[0]
     nb = size // BLOCK
     plane, me = place_ref[0], place_ref[1]
@@ -271,14 +269,11 @@
     @pl.when(plane == 0)
     def _():
         half = rect_ref.shape[0] // 2
-        quarter = half // 2
         core = me & 1
         mine = pl.multiple_of(core * half, half)
         theirs = pl.multiple_of((1 - core) * half, half)
-        rect_ref[pl.ds(mine, quarter), :] = own_a[...]
-        rect_ref[pl.ds(mine + quarter, quarter), :] = own_b[...]
-        rect_ref[pl.ds(theirs, quarter), :] = other_a[...]
-        rect_ref[pl.ds(theirs + quarter, quarter), :] = other_b[...]
+        rect_ref[pl.ds(mine, half), :] = strip[...]
+        rect_ref[pl.ds(theirs, half), :] = other[...]
         row = lax.broadcasted_iota(jnp.int32, (BLOCK, BLOCK), 0)
         col = lax.broadcasted_iota(jnp.int32, (BLOCK, BLOCK), 1)
         for i, block, low in strips(nb):
@@ -340,7 +335,7 @@
     return pl.pallas_call(
         factor_kernel,
         out_shape=(shape(rows, size), shape(each, wide)),
-        in_specs=[SMEM] + vmem(5),
+        in_specs=[SMEM] + vmem(3),
         out_specs=tuple(vmem(2)),
         scratch_shapes=[
             pltpu.VMEM((size, size), jnp.float32),
@@ -355,19 +350,13 @@
 
 
 def last_kernel(count, place_ref, *refs):
-    pieces, (keep_a, got_a, keep_b, got_b, own_ref, out_ref, rect_ref, rows_ref) = refs[:count], refs[count:]
+    pieces, (sums, got, own_ref, out_ref, rect_ref, rows_ref) = refs[:count], refs[count:]
     me, first = place_ref[1], place_ref[2]
-    rows, width = out_ref.shape
+    _, width = out_ref.shape
     nb = width // BLOCK
     each = pieces[0].shape[0]
-    if len(keep_a.shape) == 3:
-        half = keep_a.shape[1]
-        rows_ref[:, :half] = (keep_a[0] + got_a[0]).T
-        rows_ref[:, half:] = (keep_b[0] + got_b[0]).T
-    else:
-        half = rows // 2
-        rows_ref[:half, :] = keep_a[...] + got_a[...]
-        rows_ref[half:, :] = keep_b[...] + got_b[...]
+    total = sums[...] + got[...]
+    rows_ref[...] = total[0].T if len(sums.shape) == 3 else total
     for m in range(count):
         rect_ref[pl.ds(pl.multiple_of((me ^ m) * each, each), each), :] = pieces[m][...]
     for i, block, low in strips(nb):
@@ -391,7 +380,7 @@
     return pl.pallas_call(
         functools.partial(last_kernel, len(pieces)),
         out_shape=shape(rows, width),
-        in_specs=[SMEM] + vmem(len(pieces) + 5),
+        in_specs=[SMEM] + vmem(len(pieces) + 3),
         out_specs=vmem(1)[0],
         scratch_shapes=[pltpu.VMEM((tall, wide), jnp.float32), pltpu.VMEM((rows, width), jnp.float32)],
         compiler_params=pltpu.CompilerParams(vmem_limit_bytes=12 << 20),
@@ -410,57 +399,51 @@
 def orders(count):
     bits = count.bit_length() - 1
     split = 1 + bits // 2
-    return bits, list(range(1, split)), list(range(split, bits))
-
-
-def halve(x, names, bit, count):
-    axis = names.index(bit)
-    mine = (lax.axis_index("scen") >> bit) & 1
-    keep = lax.dynamic_index_in_dim(x, mine, axis, keepdims=False)
-    send = lax.dynamic_index_in_dim(x, 1 - mine, axis, keepdims=False)
-    return keep, exchange(send, 1 << bit, count), [n for n in names if n != bit]
+    first, second = list(range(1, split)), list(range(split, bits))
+    return bits, first + second, second + first
+
+
+def crossed(x, near, far, count):
+    return lax.ppermute(x, "scen", [(i, i ^ (1 << (far if i & 1 else near))) for i in range(count)])
 
 
 def scatter_sum(x):
     count = lax.axis_size("scen")
-    bits, first, second = orders(count)
-    rows = x.shape[0] // count
-    x = x.reshape((2,) * bits + (rows,) + x.shape[1:])
-    keep, got, names = halve(x, list(range(bits - 1, -1, -1)), 0, count)
-    x = keep + got
-    lead = (slice(None),) * len(names)
-    parts = [x[lead + (slice(0, rows // 2),)], x[lead + (slice(rows // 2, rows),)]]
-    lists, pairs = [names, names], [None, None]
-    for a, b in zip(first + second, second + first):
+    bits, near, far = orders(count)
+    me = lax.axis_index("scen")
+    core = me & 1
+    x = x.reshape((count // 2, 2, x.shape[0] // count) + x.shape[1:])
+    keep = lax.dynamic_index_in_dim(x, core, 1, keepdims=False)
+    got = exchange(lax.dynamic_index_in_dim(x, 1 - core, 1, keepdims=False), 1, count)
+    left = [list(range(1, bits)), list(range(1, bits))]
+    for a, b in zip(near, far):
+        x = keep + got
+        tall = x.shape[0] // 2
+        picks = []
         for i, bit in ((0, a), (1, b)):
-            if pairs[i] is not None:
-                parts[i] = pairs[i][0] + pairs[i][1]
-            keep, got, lists[i] = halve(parts[i], lists[i], bit, count)
-            pairs[i] = (keep, got)
-    return pairs[0] + pairs[1]
+            position = left[i].index(bit)
+            left[i].remove(bit)
+            mine = (me >> bit) & 1
+            j = jnp.arange(tall)
+            base = ((j >> position) << (position + 1)) + (j & ((1 << position) - 1))
+            picks.append((base + (mine << position), base + ((1 - mine) << position)))
+        keep, send = (jnp.take(x, jnp.where(core == 0, picks[0][i], picks[1][i]), axis=0) for i in range(2))
+        got = crossed(send, a, b, count)
+    return keep[0], got[0]
 
 
 def scatter_sum_columns(place, first, second):
     count = lax.axis_size("scen")
     bits, near, far = orders(count)
-    half = first.shape[0] // 2
     keep, send = part(place, first, second, count)
     got = exchange(send, 1, count)
     left = [list(range(1, bits)), list(range(1, bits))]
-    pairs = None
-    for a, b in zip(near + far, far + near):
-        if pairs is None:
-            cuts = tuple((i * half, (i + 1) * half, left[i].index(bit), bit) for i, bit in ((0, a), (1, b)))
-            outs = turn(place, keep, got, cuts)
-        else:
-            outs = ()
-            for i, bit in ((0, a), (1, b)):
-                outs += turn(place, *pairs[i], ((0, half, left[i].index(bit), bit),))
-        pairs = []
-        for i, bit in ((0, a), (1, b)):
-            left[i].remove(bit)
-            pairs.append((outs[2 * i], exchange(outs[2 * i + 1], 1 << bit, count)))
-    return pairs[0] + pairs[1]
+    for a, b in zip(near, far):
+        keep, send = turn(place, keep, got, (a, left[0].index(a)), (b, left[1].index(b)))
+        left[0].remove(a)
+        left[1].remove(b)
+        got = crossed(send, a, b, count)
+    return keep, got
 
 
 PIECES = 8
@@ -481,26 +464,24 @@
     place = jnp.stack([plane, me, plane * local.shape[1] + me * rows])
     edge = bounds(local.shape[0])
 
-    *own, keep_a, keep_b, send = product(place, tile_mask, inverses[0], local, width, edge)
+    *own, strip, send = product(place, tile_mask, inverses[0], local, width, edge)
 
     groups = [own]
     for h in range(planes - 1):
         groups.append([hop(groups[h][k], h, h + 1) for k in range(PIECES)])
 
-    got = exchange(send, 1, scen)
-    a, b = keep_a + got[: got.shape[0] // 2], keep_b + got[got.shape[0] // 2 :]
+    strip = strip + exchange(send, 1, scen)
     _, near, far = orders(scen)
-    for p, q in zip(near + far, far + near):
-        got_a = exchange(a, 1 << p, scen)
-        got_b = exchange(b, 1 << q, scen)
-        a, b = a + got_a, b + got_b
-    parts = (a, b, exchange(a, 1, scen), exchange(b, 1, scen))
+    for p, q in zip(near, far):
+        strip = strip + crossed(strip, p, q, scen)
+    other = exchange(strip, 1, scen)
     each = width // BLOCK // 2 * BLOCK // scen
-    lower, piece = factor(place, parts, hess_diag[None, :], each, rows)
+    lower, piece = factor(place, (strip, other), hess_diag[None, :], each, rows)
 
     mine = jnp.where(plane == 0, piece, 0.0)
     for h in range(1, planes):
-        mine = mine + hop(piece, 0, h)
+        piece = hop(piece, h - 1, h)
+        mine = mine + piece
     pieces = [mine if m == 0 else exchange(mine, m, scen) for m in range(0, scen, 2)]
     pieces = [p for m in range(0, scen, 2) for p in (pieces[m // 2], exchange(pieces[m // 2], 1, scen))]
 

time: 167 us -> 158 us (0.946)
  the two profiles are of different devices: /device:TPU:0 before, /device:TPU:19 now
where the time goes in v6:
time: 158 us
  waiting for transfers between devices  86.3 us (55%)
  starting transfers between devices  48.5 us (31%)
  Pallas kernels  8.61 us (5%)
  local copies, waits for them, and re-layouts  8.07 us (5%)
  matrix products  4.77 us (3%)
    ppermute x27, waiting for transfers between devices, hop(): return lax.ppermute(x, 'col', [(source, target)])  73.7 us
    ppermute x27, starting transfers between devices, hop(): return lax.ppermute(x, 'col', [(source, target)])  29.3 us
    ppermute x10, starting transfers between devices, exchange(): return lax.ppermute(x, 'scen', [(i, i ^ mask) for i in range(count)])  16.3 us
    ppermute x4, waiting for transfers between devices, crossed(): lax.ppermute(x, 'scen', [(i, i ^ 1 << (far if i & 1 else near)) for i in...  11.1 us
    unnamed x24, local copies, waits for them, and re-layouts  8.07 us
    dot_general x2, matrix products, high(): lax.dot_general(left, right, (dims, ((), ())), precision=lax.Precision.HI...  4.77 us
  transfers between devices with their start and end apart: 41, of which 17 were waited for; matrix products, arithmetic and copies ran while one was open for 3% of the time, Pallas kernels for 3%

profile of v6, /device:TPU:19, one launch (start us, length us, event | category | flops | bytes accessed | tf_op | source)
XLA Modules:
  0.0 157.5 jit_solution(8620911636319565853)
XLA Ops:
  0.7 2.3 %shard_map.46 = (f32[128,512]{1,0:T(8,128)}, f32[128,512]{1,0:T(8,128)}, f32[128,512]{1,0:T(8,128)}, f32[128,512]{1,0:T(8,128)}, f32[128,512]{1,0:T(8,128)}, /*i...) custom-call(s32[3]{0:T(128)} %pad_add_fusion.place_ref, ...), custom_call_target="tpu_custom_call" | custom-call | flops 4831838208 | bytes 8388608 | tf_op jit(solution)/shard_map/pallas_call | solution.py:174
  15.1 26.2 %collective-permute-done.21.refs_14_ = f32[128,512]{1,0:T(8,128)S(1)} collective-permute-done((f32[128,512]{1,0:T(8,128)S(1)}, f32[128,512]{1,0:T(8,128)S(1)}, u32[]{:S(2)}, u32[]{:S(2)}) %collective-permute-start.21) | collective-permute-done | bytes 262176 | tf_op jit(solution)/shard_map/ppermute | solution.py:392
  42.6 4.3 %collective-permute-done.22.refs_15_ = f32[128,512]{1,0:T(8,128)S(1)} collective-permute-done((f32[128,512]{1,0:T(8,128)S(1)}, f32[128,512]{1,0:T(8,128)S(1)}, u32[]{:S(2)}, u32[]{:S(2)}) %collective-permute-start.22) | collective-permute-done | bytes 262176 | tf_op jit(solution)/shard_map/ppermute | solution.py:392
  48.2 4.3 %collective-permute-done.23.refs_16_ = f32[128,512]{1,0:T(8,128)S(1)} collective-permute-done((f32[128,512]{1,0:T(8,128)S(1)}, f32[128,512]{1,0:T(8,128)S(1)}, u32[]{:S(2)}, u32[]{:S(2)}) %collective-permute-start.23) | collective-permute-done | bytes 262176 | tf_op jit(solution)/shard_map/ppermute | solution.py:392
  53.8 4.3 %collective-permute-done.24.refs_17_ = f32[128,512]{1,0:T(8,128)S(1)} collective-permute-done((f32[128,512]{1,0:T(8,128)S(1)}, f32[128,512]{1,0:T(8,128)S(1)}, u32[]{:S(2)}, u32[]{:S(2)}) %collective-permute-start.24) | collective-permute-done | bytes 262176 | tf_op jit(solution)/shard_map/ppermute | solution.py:392
  58.1 1.3 collective-permute-start.28
  59.4 5.2 %collective-permute-done.25.refs_18_ = f32[128,512]{1,0:T(8,128)S(1)} collective-permute-done((f32[128,512]{1,0:T(8,128)S(1)}, f32[128,512]{1,0:T(8,128)S(1)}, u32[]{:S(2)}, u32[]{:S(2)}) %collective-permute-start.25) | collective-permute-done | bytes 262176 | tf_op jit(solution)/shard_map/ppermute | solution.py:392
  65.9 4.3 %collective-permute-done.26.refs_19_ = f32[128,512]{1,0:T(8,128)S(1)} collective-permute-done((f32[128,512]{1,0:T(8,128)S(1)}, f32[128,512]{1,0:T(8,128)S(1)}, u32[]{:S(2)}, u32[]{:S(2)}) %collective-permute-start.26) | collective-permute-done | bytes 262176 | tf_op jit(solution)/shard_map/ppermute | solution.py:392
  70.2 1.3 collective-permute-start.30
  71.5 4.3 %collective-permute-done.27.refs_20_ = f32[128,512]{1,0:T(8,128)S(1)} collective-permute-done((f32[128,512]{1,0:T(8,128)S(1)}, f32[128,512]{1,0:T(8,128)S(1)}, u32[]{:S(2)}, u32[]{:S(2)}) %collective-permute-start.27) | collective-permute-done | bytes 262176 | tf_op jit(solution)/shard_map/ppermute | solution.py:392
  77.1 4.3 %collective-permute-done.36.refs_2_ = f32[128,512]{1,0:T(8,128)S(1)} collective-permute-done((f32[128,512]{1,0:T(8,128)S(1)}, f32[128,512]{1,0:T(8,128)S(1)}, u32[]{:S(2)}, u32[]{:S(2)}) %collective-permute-start.36) | collective-permute-done | bytes 262176 | tf_op jit(solution)/shard_map/ppermute | solution.py:392
  81.4 1.3 collective-permute-start.32
  82.8 1.3 collective-permute-start.33
  84.1 1.3 collective-permute-start.34
  85.4 1.9 %collective-permute-start = (f32[128,640]{1,0:T(8,128)}, f32[128,640]{1,0:T(8,128)S(1)}, u32[]{:S(2)}, u32[]{:S(2)}) collective-permute-start(f32[128,640]{1,0:T(8,128)} %get-tuple-element.24), channel_id=1, source_target_pairs={{0,4},{4,0},{8,12},{12,8},{16,20},{20,16},{24,28},{28,24},{1,5},{5... | collective-permute-start | bytes 983048 | tf_op jit(solution)/shard_map/ppermute | solution.py:396
  87.3 1.3 collective-permute-start.37
  88.6 5.1 %collective-permute-done.33.refs_26_ = f32[128,512]{1,0:T(8,128)S(1)} collective-permute-done((f32[128,512]{1,0:T(8,128)S(1)}, f32[128,512]{1,0:T(8,128)S(1)}, u32[]{:S(2)}, u32[]{:S(2)}) %collective-permute-start.33) | collective-permute-done | bytes 262176 | tf_op jit(solution)/shard_map/ppermute | solution.py:392
  93.7 5.6 %collective-permute-done.34.refs_27_ = f32[128,512]{1,0:T(8,128)S(1)} collective-permute-done((f32[128,512]{1,0:T(8,128)S(1)}, f32[128,512]{1,0:T(8,128)S(1)}, u32[]{:S(2)}, u32[]{:S(2)}) %collective-permute-start.34) | collective-permute-done | bytes 262176 | tf_op jit(solution)/shard_map/ppermute | solution.py:392
  106.7 1.4 copy-done.10
  108.2 3.7 %fusion.first_ref = f32[512,1024]{1,0:T(8,128)S(1)} fusion(f32[896,512]{1,0:T(8,128)S(1)} %shard_map.48, f32[1,1024,1024]{2,1,0:T(8,128)S(1)} %copy-done.10), kind=kOutput, calls=%fused_computation | convolution fusion | flops 2818572288 | bytes 7602176 | tf_op jit(solution)/shard_map/dot_general | solution.py:16
  114.7 3.2 %collective-permute-start.38 = (f32[4,512,128]{2,1,0:T(8,128)S(1)}, f32[4,512,128]{2,1,0:T(8,128)S(1)}, u32[]{:S(2)}, u32[]{:S(2)}) collective-permute-start(f32[4,512,128]{2,1,0:T(8,128)S(1)} %get-tuple-element.35), channel_id=1, source_target_pairs={{0,4},{4,0},{8,12},{12,8},{16,20},{20,16},{24,28},{28,24},{1,5},{5... | collective-permute-start | bytes 3145736 | tf_op jit(solution)/shard_map/ppermute | solution.py:396
  118.0 1.3 collective-permute-start.1
  119.3 5.0 %collective-permute-done.1 = f32[128,640]{1,0:T(8,128)S(1)} collective-permute-done((f32[128,640]{1,0:T(8,128)S(1)}, f32[128,640]{1,0:T(8,128)S(1)}, u32[]{:S(2)}, u32[]{:S(2)}) %collective-permute-start.1) | collective-permute-done | bytes 327712 | tf_op jit(solution)/shard_map/ppermute | solution.py:407
  124.4 6.1 %collective-permute-done.2 = f32[128,640]{1,0:T(8,128)S(1)} collective-permute-done((f32[128,640]{1,0:T(8,128)S(1)}, f32[128,640]{1,0:T(8,128)S(1)}, u32[]{:S(2)}, u32[]{:S(2)}) %collective-permute-start.2) | collective-permute-done | bytes 327712 | tf_op jit(solution)/shard_map/ppermute | solution.py:407
  130.6 1.8 %collective-permute-start.3 = (f32[128,640]{1,0:T(8,128)S(1)}, f32[128,640]{1,0:T(8,128)S(1)}, u32[]{:S(2)}, u32[]{:S(2)}) collective-permute-start(f32[128,640]{1,0:T(8,128)S(1)} %add.24.strip), channel_id=1, source_target_pairs={{0,4},{4,0},{8,12},{12,8},{16,20},{20,16},{24,28},{28,24},{1,5},{5... | collective-permute-start | bytes 983048 | tf_op jit(solution)/shard_map/ppermute | solution.py:396
  133.1 1.3 collective-permute-start.39
  137.1 4.9 %collective-permute-done.5 = f32[32,640]{1,0:T(8,128)S(1)} collective-permute-done((f32[32,640]{1,0:T(8,128)S(1)}, f32[32,640]{1,0:T(8,128)S(1)}, u32[]{:S(2)}, u32[]{:S(2)}) %collective-permute-start.5) | collective-permute-done | bytes 81952 | tf_op jit(solution)/shard_map/ppermute | solution.py:392
  145.2 1.7 %collective-permute-start.10 = (f32[32,640]{1,0:T(8,128)S(1)}, f32[32,640]{1,0:T(8,128)S(1)}, u32[]{:S(2)}, u32[]{:S(2)}) collective-permute-start(f32[32,640]{1,0:T(8,128)S(1)} %add_add_fusion.refs_0_), channel_id=1, source_target_pairs={{0,16},{4,20},{8,24},{12,28},{16,0},{20,4},{24,8},{28,12},{1,17},{... | collective-permute-start | bytes 245768 | tf_op jit(solution)/shard_map/ppermute | solution.py:396
  147.6 2.0 %collective-permute-start.7 = (f32[32,640]{1,0:T(8,128)S(1)}, f32[32,640]{1,0:T(8,128)S(1)}, u32[]{:S(2)}, u32[]{:S(2)}) collective-permute-start(f32[32,640]{1,0:T(8,128)S(1)} %add_add_fusion.refs_0_), channel_id=1, source_target_pairs={{0,4},{4,0},{8,12},{12,8},{16,20},{20,16},{24,28},{28,24},{1,5},{5... | collective-permute-start | bytes 245768 | tf_op jit(solution)/shard_map/ppermute | solution.py:396
  149.8 2.3 %collective-permute-start.13 = (f32[32,640]{1,0:T(8,128)S(1)}, f32[32,640]{1,0:T(8,128)S(1)}, u32[]{:S(2)}, u32[]{:S(2)}) collective-permute-start(f32[32,640]{1,0:T(8,128)S(1)} %collective-permute-done.12.refs_6_), channel_id=1, source_target_pairs={{0,4},{4,0},{8,12},{12,8},{16,20},{20,16},{24,28},{28,24},{1,5},{5... | collective-permute-start | bytes 245768 | tf_op jit(solution)/shard_map/ppermute | solution.py:396
  152.1 2.3 %collective-permute-start.11 = (f32[32,640]{1,0:T(8,128)S(1)}, f32[32,640]{1,0:T(8,128)S(1)}, u32[]{:S(2)}, u32[]{:S(2)}) collective-permute-start(f32[32,640]{1,0:T(8,128)S(1)} %collective-permute-done.10.refs_4_), channel_id=1, source_target_pairs={{0,4},{4,0},{8,12},{12,8},{16,20},{20,16},{24,28},{28,24},{1,5},{5... | collective-permute-start | bytes 245768 | tf_op jit(solution)/shard_map/ppermute | solution.py:396
  155.8 1.8 %shard_map.53 = f32[128,512]{1,0:T(8,128)} custom-call(s32[3]{0:T(128)S(1)} %copy-done.8, f32[32,640]{1,0:T(8,128)S(1)} %add_add_fusion.refs_0_, f32[32,640]{1,0:T(8,128)S(1)} %collective-permute-done.7.refs_1_, f32[32,640]{1,0:T(8,128)S(1)} %collective-permute-done.8.refs_2_, f32[32,640]{1,0:T(8,128)S(1)} %collective-permute-done.9.refs_3_, ...), custom_call_target="tpu_custom_call" | custom-call | flops 201326592 | bytes 2097152 | tf_op jit(solution)/shard_map/pallas_call | solution.py:380
  (89 shorter events, 38.1 us)
Async XLA Ops:
  5.7 4.1 %collective-permute-start.18 = (f32[128,512]{1,0:T(8,128)}, f32[128,512]{1,0:T(8,128)S(1)}, u32[]{:S(2)}, u32[]{:S(2)}) collective-permute-start(f32[128,512]{1,0:T(8,128)} %get-tuple-element.30.refs_4_), channel_id=1, source_target_pairs={{0,1},{4,5},{8,9},{12,13},{16,17},{20,21},{24,25},{28,29}} | collective-permute-start | bytes 786440 | tf_op jit(solution)/shard_map/ppermute | solution.py:392
  6.4 4.7 %collective-permute-start.19 = (f32[128,512]{1,0:T(8,128)}, f32[128,512]{1,0:T(8,128)S(1)}, u32[]{:S(2)}, u32[]{:S(2)}) collective-permute-start(f32[128,512]{1,0:T(8,128)} %get-tuple-element.31.refs_5_), channel_id=1, source_target_pairs={{0,1},{4,5},{8,9},{12,13},{16,17},{20,21},{24,25},{28,29}} | collective-permute-start | bytes 786440 | tf_op jit(solution)/shard_map/ppermute | solution.py:392
  7.1 5.3 %collective-permute-start.20 = (f32[128,512]{1,0:T(8,128)}, f32[128,512]{1,0:T(8,128)S(1)}, u32[]{:S(2)}, u32[]{:S(2)}) collective-permute-start(f32[128,512]{1,0:T(8,128)} %get-tuple-element.32.refs_6_), channel_id=1, source_target_pairs={{0,1},{4,5},{8,9},{12,13},{16,17},{20,21},{24,25},{28,29}} | collective-permute-start | bytes 786440 | tf_op jit(solution)/shard_map/ppermute | solution.py:392
  7.8 5.9 %collective-permute-start.35 = (f32[128,512]{1,0:T(8,128)}, f32[128,512]{1,0:T(8,128)S(1)}, u32[]{:S(2)}, u32[]{:S(2)}) collective-permute-start(f32[128,512]{1,0:T(8,128)} %get-tuple-element.33.refs_0_), channel_id=1, source_target_pairs={{0,1},{4,5},{8,9},{12,13},{16,17},{20,21},{24,25},{28,29}} | collective-permute-start | bytes 786440 | tf_op jit(solution)/shard_map/ppermute | solution.py:392
  8.5 32.8 %collective-permute-start.21 = (f32[128,512]{1,0:T(8,128)S(1)}, f32[128,512]{1,0:T(8,128)S(1)}, u32[]{:S(2)}, u32[]{:S(2)}) collective-permute-start(f32[128,512]{1,0:T(8,128)S(1)} %collective-permute-done.14.refs_7_), channel_id=1, source_target_pairs={{1,2},{5,6},{9,10},{13,14},{17,18},{21,22},{25,26},{29,30}} | collective-permute-start | bytes 786440 | tf_op jit(solution)/shard_map/ppermute | solution.py:392
  9.8 37.1 %collective-permute-start.22 = (f32[128,512]{1,0:T(8,128)S(1)}, f32[128,512]{1,0:T(8,128)S(1)}, u32[]{:S(2)}, u32[]{:S(2)}) collective-permute-start(f32[128,512]{1,0:T(8,128)S(1)} %collective-permute-done.15.refs_8_), channel_id=1, source_target_pairs={{1,2},{5,6},{9,10},{13,14},{17,18},{21,22},{25,26},{29,30}} | collective-permute-start | bytes 786440 | tf_op jit(solution)/shard_map/ppermute | solution.py:392
  11.1 41.4 %collective-permute-start.23 = (f32[128,512]{1,0:T(8,128)S(1)}, f32[128,512]{1,0:T(8,128)S(1)}, u32[]{:S(2)}, u32[]{:S(2)}) collective-permute-start(f32[128,512]{1,0:T(8,128)S(1)} %collective-permute-done.16.refs_9_), channel_id=1, source_target_pairs={{1,2},{5,6},{9,10},{13,14},{17,18},{21,22},{25,26},{29,30}} | collective-permute-start | bytes 786440 | tf_op jit(solution)/shard_map/ppermute | solution.py:392
  12.4 45.7 %collective-permute-start.24 = (f32[128,512]{1,0:T(8,128)S(1)}, f32[128,512]{1,0:T(8,128)S(1)}, u32[]{:S(2)}, u32[]{:S(2)}) collective-permute-start(f32[128,512]{1,0:T(8,128)S(1)} %collective-permute-done.17.refs_10_), channel_id=1, source_target_pairs={{1,2},{5,6},{9,10},{13,14},{17,18},{21,22},{25,26},{29,30}} | collective-permute-start | bytes 786440 | tf_op jit(solution)/shard_map/ppermute | solution.py:392
  13.8 50.8 %collective-permute-start.25 = (f32[128,512]{1,0:T(8,128)S(1)}, f32[128,512]{1,0:T(8,128)S(1)}, u32[]{:S(2)}, u32[]{:S(2)}) collective-permute-start(f32[128,512]{1,0:T(8,128)S(1)} %collective-permute-done.18.refs_11_), channel_id=1, source_target_pairs={{1,2},{5,6},{9,10},{13,14},{17,18},{21,22},{25,26},{29,30}} | collective-permute-start | bytes 786440 | tf_op jit(solution)/shard_map/ppermute | solution.py:392
  41.3 28.9 %collective-permute-start.26 = (f32[128,512]{1,0:T(8,128)S(1)}, f32[128,512]{1,0:T(8,128)S(1)}, u32[]{:S(2)}, u32[]{:S(2)}) collective-permute-start(f32[128,512]{1,0:T(8,128)S(1)} %collective-permute-done.19.refs_12_), channel_id=1, source_target_pairs={{1,2},{5,6},{9,10},{13,14},{17,18},{21,22},{25,26},{29,30}} | collective-permute-start | bytes 786440 | tf_op jit(solution)/shard_map/ppermute | solution.py:392
  46.9 28.9 %collective-permute-start.27 = (f32[128,512]{1,0:T(8,128)S(1)}, f32[128,512]{1,0:T(8,128)S(1)}, u32[]{:S(2)}, u32[]{:S(2)}) collective-permute-start(f32[128,512]{1,0:T(8,128)S(1)} %collective-permute-done.20.refs_13_), channel_id=1, source_target_pairs={{1,2},{5,6},{9,10},{13,14},{17,18},{21,22},{25,26},{29,30}} | collective-permute-start | bytes 786440 | tf_op jit(solution)/shard_map/ppermute | solution.py:392
  52.5 28.9 %collective-permute-start.36 = (f32[128,512]{1,0:T(8,128)S(1)}, f32[128,512]{1,0:T(8,128)S(1)}, u32[]{:S(2)}, u32[]{:S(2)}) collective-permute-start(f32[128,512]{1,0:T(8,128)S(1)} %collective-permute-done.35.refs_1_), channel_id=1, source_target_pairs={{1,2},{5,6},{9,10},{13,14},{17,18},{21,22},{25,26},{29,30}} | collective-permute-start | bytes 786440 | tf_op jit(solution)/shard_map/ppermute | solution.py:392
  58.1 24.6 %collective-permute-start.28 = (f32[128,512]{1,0:T(8,128)S(1)}, f32[128,512]{1,0:T(8,128)S(1)}, u32[]{:S(2)}, u32[]{:S(2)}) collective-permute-start(f32[128,512]{1,0:T(8,128)S(1)} %collective-permute-done.21.refs_14_), channel_id=1, source_target_pairs={{2,3},{6,7},{10,11},{14,15},{18,19},{22,23},{26,27},{30,31}} | collective-permute-start | bytes 786440 | tf_op jit(solution)/shard_map/ppermute | solution.py:392
  64.6 19.5 %collective-permute-start.29 = (f32[128,512]{1,0:T(8,128)S(1)}, f32[128,512]{1,0:T(8,128)S(1)}, u32[]{:S(2)}, u32[]{:S(2)}) collective-permute-start(f32[128,512]{1,0:T(8,128)S(1)} %collective-permute-done.22.refs_15_), channel_id=1, source_target_pairs={{2,3},{6,7},{10,11},{14,15},{18,19},{22,23},{26,27},{30,31}} | collective-permute-start | bytes 786440 | tf_op jit(solution)/shard_map/ppermute | solution.py:392
  70.2 15.2 %collective-permute-start.30 = (f32[128,512]{1,0:T(8,128)S(1)}, f32[128,512]{1,0:T(8,128)S(1)}, u32[]{:S(2)}, u32[]{:S(2)}) collective-permute-start(f32[128,512]{1,0:T(8,128)S(1)} %collective-permute-done.23.refs_16_), channel_id=1, source_target_pairs={{2,3},{6,7},{10,11},{14,15},{18,19},{22,23},{26,27},{30,31}} | collective-permute-start | bytes 786440 | tf_op jit(solution)/shard_map/ppermute | solution.py:392
  75.8 11.5 %collective-permute-start.31 = (f32[128,512]{1,0:T(8,128)S(1)}, f32[128,512]{1,0:T(8,128)S(1)}, u32[]{:S(2)}, u32[]{:S(2)}) collective-permute-start(f32[128,512]{1,0:T(8,128)S(1)} %collective-permute-done.24.refs_17_), channel_id=1, source_target_pairs={{2,3},{6,7},{10,11},{14,15},{18,19},{22,23},{26,27},{30,31}} | collective-permute-start | bytes 786440 | tf_op jit(solution)/shard_map/ppermute | solution.py:392
  81.4 7.2 %collective-permute-start.32 = (f32[128,512]{1,0:T(8,128)S(1)}, f32[128,512]{1,0:T(8,128)S(1)}, u32[]{:S(2)}, u32[]{:S(2)}) collective-permute-start(f32[128,512]{1,0:T(8,128)S(1)} %collective-permute-done.25.refs_18_), channel_id=1, source_target_pairs={{2,3},{6,7},{10,11},{14,15},{18,19},{22,23},{26,27},{30,31}} | collective-permute-start | bytes 786440 | tf_op jit(solution)/shard_map/ppermute | solution.py:392
  82.8 10.9 %collective-permute-start.33 = (f32[128,512]{1,0:T(8,128)S(1)}, f32[128,512]{1,0:T(8,128)S(1)}, u32[]{:S(2)}, u32[]{:S(2)}) collective-permute-start(f32[128,512]{1,0:T(8,128)S(1)} %collective-permute-done.26.refs_19_), channel_id=1, source_target_pairs={{2,3},{6,7},{10,11},{14,15},{18,19},{22,23},{26,27},{30,31}} | collective-permute-start | bytes 786440 | tf_op jit(solution)/shard_map/ppermute | solution.py:392
  84.1 15.2 %collective-permute-start.34 = (f32[128,512]{1,0:T(8,128)S(1)}, f32[128,512]{1,0:T(8,128)S(1)}, u32[]{:S(2)}, u32[]{:S(2)}) collective-permute-start(f32[128,512]{1,0:T(8,128)S(1)} %collective-permute-done.27.refs_20_), channel_id=1, source_target_pairs={{2,3},{6,7},{10,11},{14,15},{18,19},{22,23},{26,27},{30,31}} | collective-permute-start | bytes 786440 | tf_op jit(solution)/shard_map/ppermute | solution.py:392
  85.4 32.5 %collective-permute-start = (f32[128,640]{1,0:T(8,128)}, f32[128,640]{1,0:T(8,128)S(1)}, u32[]{:S(2)}, u32[]{:S(2)}) collective-permute-start(f32[128,640]{1,0:T(8,128)} %get-tuple-element.24), channel_id=1, source_target_pairs={{0,4},{4,0},{8,12},{12,8},{16,20},{20,16},{24,28},{28,24},{1,5},{5... | collective-permute-start | bytes 983048 | tf_op jit(solution)/shard_map/ppermute | solution.py:396
  87.3 24.6 %collective-permute-start.37 = (f32[128,512]{1,0:T(8,128)S(1)}, f32[128,512]{1,0:T(8,128)S(1)}, u32[]{:S(2)}, u32[]{:S(2)}) collective-permute-start(f32[128,512]{1,0:T(8,128)S(1)} %collective-permute-done.36.refs_2_), channel_id=1, source_target_pairs={{2,3},{6,7},{10,11},{14,15},{18,19},{22,23},{26,27},{30,31}} | collective-permute-start | bytes 786440 | tf_op jit(solution)/shard_map/ppermute | solution.py:392
  114.7 17.7 %collective-permute-start.38 = (f32[4,512,128]{2,1,0:T(8,128)S(1)}, f32[4,512,128]{2,1,0:T(8,128)S(1)}, u32[]{:S(2)}, u32[]{:S(2)}) collective-permute-start(f32[4,512,128]{2,1,0:T(8,128)S(1)} %get-tuple-element.35), channel_id=1, source_target_pairs={{0,4},{4,0},{8,12},{12,8},{16,20},{20,16},{24,28},{28,24},{1,5},{5... | collective-permute-start | bytes 3145736 | tf_op jit(solution)/shard_map/ppermute | solution.py:396
  118.0 6.3 %collective-permute-start.1 = (f32[128,640]{1,0:T(8,128)S(1)}, f32[128,640]{1,0:T(8,128)S(1)}, u32[]{:S(2)}, u32[]{:S(2)}) collective-permute-start(f32[128,640]{1,0:T(8,128)S(1)} %add.22), channel_id=1, source_target_pairs={{0,8},{4,20},{8,0},{12,28},{16,24},{20,4},{24,16},{28,12},{1,9},{5... | collective-permute-start | bytes 983048 | tf_op jit(solution)/shard_map/ppermute | solution.py:407
  124.3 6.3 %collective-permute-start.2 = (f32[128,640]{1,0:T(8,128)S(1)}, f32[128,640]{1,0:T(8,128)S(1)}, u32[]{:S(2)}, u32[]{:S(2)}) collective-permute-start(f32[128,640]{1,0:T(8,128)S(1)} %add.23), channel_id=1, source_target_pairs={{0,16},{4,12},{8,24},{12,4},{16,0},{20,28},{24,8},{28,20},{1,17},{... | collective-permute-start | bytes 983048 | tf_op jit(solution)/shard_map/ppermute | solution.py:407
  133.1 10.3 %collective-permute-start.39 = (f32[2,512,128]{2,1,0:T(8,128)S(1)}, f32[2,512,128]{2,1,0:T(8,128)S(1)}, u32[]{:S(2)}, u32[]{:S(2)}) collective-permute-start(f32[2,512,128]{2,1,0:T(8,128)S(1)} %get-tuple-element.37), channel_id=1, source_target_pairs={{0,8},{4,20},{8,0},{12,28},{16,24},{20,4},{24,16},{28,12},{1,9},{5... | collective-permute-start | bytes 1572872 | tf_op jit(solution)/shard_map/ppermute | solution.py:407
  135.8 6.2 %collective-permute-start.5 = (f32[32,640]{1,0:T(8,128)S(1)}, f32[32,640]{1,0:T(8,128)S(1)}, u32[]{:S(2)}, u32[]{:S(2)}) collective-permute-start(f32[32,640]{1,0:T(8,128)S(1)} %collective-permute-done.4), channel_id=1, source_target_pairs={{1,2},{5,6},{9,10},{13,14},{17,18},{21,22},{25,26},{29,30}} | collective-permute-start | bytes 245768 | tf_op jit(solution)/shard_map/ppermute | solution.py:392
  144.0 11.7 %collective-permute-start.40 = (f32[1,512,128]{2,1,0:T(8,128)S(1)}, f32[1,512,128]{2,1,0:T(8,128)S(1)}, u32[]{:S(2)}, u32[]{:S(2)}) collective-permute-start(f32[1,512,128]{2,1,0:T(8,128)S(1)} %get-tuple-element.39), channel_id=1, source_target_pairs={{0,16},{4,12},{8,24},{12,4},{16,0},{20,28},{24,8},{28,20},{1,17},{... | collective-permute-start | bytes 786440 | tf_op jit(solution)/shard_map/ppermute | solution.py:407
  144.9 4.9 %collective-permute-start.12 = (f32[32,640]{1,0:T(8,128)S(1)}, f32[32,640]{1,0:T(8,128)S(1)}, u32[]{:S(2)}, u32[]{:S(2)}) collective-permute-start(f32[32,640]{1,0:T(8,128)S(1)} %add_add_fusion.refs_0_), channel_id=1, source_target_pairs={{0,24},{4,28},{8,16},{12,20},{16,8},{20,12},{24,0},{28,4},{1,25},{... | collective-permute-start | bytes 245768 | tf_op jit(solution)/shard_map/ppermute | solution.py:396
  145.2 7.0 %collective-permute-start.10 = (f32[32,640]{1,0:T(8,128)S(1)}, f32[32,640]{1,0:T(8,128)S(1)}, u32[]{:S(2)}, u32[]{:S(2)}) collective-permute-start(f32[32,640]{1,0:T(8,128)S(1)} %add_add_fusion.refs_0_), channel_id=1, source_target_pairs={{0,16},{4,20},{8,24},{12,28},{16,0},{20,4},{24,8},{28,12},{1,17},{... | collective-permute-start | bytes 245768 | tf_op jit(solution)/shard_map/ppermute | solution.py:396
  146.8 7.7 %collective-permute-start.8 = (f32[32,640]{1,0:T(8,128)S(1)}, f32[32,640]{1,0:T(8,128)S(1)}, u32[]{:S(2)}, u32[]{:S(2)}) collective-permute-start(f32[32,640]{1,0:T(8,128)S(1)} %add_add_fusion.refs_0_), channel_id=1, source_target_pairs={{0,8},{4,12},{8,0},{12,4},{16,24},{20,28},{24,16},{28,20},{1,9},{5... | collective-permute-start | bytes 245768 | tf_op jit(solution)/shard_map/ppermute | solution.py:396
  147.6 6.9 %collective-permute-start.7 = (f32[32,640]{1,0:T(8,128)S(1)}, f32[32,640]{1,0:T(8,128)S(1)}, u32[]{:S(2)}, u32[]{:S(2)}) collective-permute-start(f32[32,640]{1,0:T(8,128)S(1)} %add_add_fusion.refs_0_), channel_id=1, source_target_pairs={{0,4},{4,0},{8,12},{12,8},{16,20},{20,16},{24,28},{28,24},{1,5},{5... | collective-permute-start | bytes 245768 | tf_op jit(solution)/shard_map/ppermute | solution.py:396
  149.8 4.7 %collective-permute-start.13 = (f32[32,640]{1,0:T(8,128)S(1)}, f32[32,640]{1,0:T(8,128)S(1)}, u32[]{:S(2)}, u32[]{:S(2)}) collective-permute-start(f32[32,640]{1,0:T(8,128)S(1)} %collective-permute-done.12.refs_6_), channel_id=1, source_target_pairs={{0,4},{4,0},{8,12},{12,8},{16,20},{20,16},{24,28},{28,24},{1,5},{5... | collective-permute-start | bytes 245768 | tf_op jit(solution)/shard_map/ppermute | solution.py:396
  (21 other events, 163.0 us)
